TPU v7x, 32 devices: a whole 2x2x4 slice. The times are simulated.
32 devices in a mesh: groups: 2 (over y), ctx: 4 (over z), head: 2 (over x), rep: 2 (over core).
Axes of the slice: x: 2, y: 2, z: 4, core: 2. Of those that a mesh axis runs over, the one named last changes fastest.
Arguments:
- q_self: bfloat16 [1024, 8192], P(('groups', 'ctx'), ('head', 'rep')), parts along dimension 0, may hold values from -64 to 64
- q_cross: bfloat16 [1024, 8192], P(('groups', 'ctx'), ('head', 'rep')), parts along dimension 0, may hold values from -64 to 64
- kv_self: bfloat16 [2, 1024, 1024], P(None, ('groups', 'ctx'), 'head'), parts along dimension 1, may hold values from -4 to 4
- image_kv: bfloat16 [2, 16, 1601, 1024], P(None, ('groups', 'ctx'), None, 'head'), parts along dimension 1, may hold values from -4 to 4
- cross_gate: float32 [64], P(('head', 'rep')), may hold values from -2 to 2
- doc_lengths: int32 [8], P('groups'), parts along dimension 0, may hold values from 1 to 256, 512 in all
- pair_tiles: int32 [32, 4], P(('groups', 'ctx')), parts along dimension 0, may hold values from 0 to 7, as said below
- tile_slot: int32 [16], P('groups'), parts along dimension 0, may hold values from 0 to 7, as said below
Outputs:
- mixed: bfloat16 [1024, 8192], P(('groups', 'ctx'), ('head', 'rep')), parts along dimension 0
There are 2 independent parts, one for each index of `groups`. A program takes and returns all parts, laid end to end along the dimension named above; an argument that names none is the same for every part. Nothing has to cross between parts.
Inputs may be any that keep to these rules, and one draw needn't show every extreme that they name: `pair_tiles`: each block lists 4 tiles; a tile may be listed more than once. Over the 4 blocks of one ctx index, the pairs name tiles stored at one ctx index (slots ctx * 2 onward) at most 4 times, and at most 1 of those blocks name some tile stored there; both bounds are met in every draw, and some ctx index is named 4 times by the blocks of every ctx index. A permutation: tile i is stored at slot tile_slot[i] of image_kv.
All inputs are finite; a program needn't handle non-finite values.
Results may differ from a plain program's by a relative error of at most 0.0034.
Values may be sent and summed in bfloat16 or wider, within the bound.
No kernel may reach another device: no remote copies, remote signals or barrier semaphores. Data moves between devices by JAX's collectives and lax.ppermute only.
A program may use at most 128 MiB of HBM per device.

v0:
```python
import math

import jax
import jax.numpy as jnp
from jax import lax
from jax.sharding import PartitionSpec as P

HEAD_DIM = 128
Q_HEADS = 64
KV_HEADS = 8
BLOCK = 32
PAIRS = 4


NEG_FILL = -1e30


def doc_index(doc_ends, positions):
    return jnp.sum((positions[:, None] >= doc_ends[None, :]).astype(jnp.int32), axis=1)


def send_back(outputs, log_sums):
    returned = lax.all_to_all(outputs, "ctx", split_axis=0, concat_axis=0, tiled=True)
    returned_sums = lax.all_to_all(log_sums, "ctx", split_axis=0, concat_axis=0, tiled=True)
    return (returned, returned_sums)


def attend_tiles(queries, query_pick, tile_pick, live_pick, tiles_kv, layout):
    kv_used, per_kv, head_dim = layout
    item_count = query_pick.shape[0]
    batch_size = math.gcd(item_count, 4)
    block_rows = queries.shape[1]
    q_width = queries.shape[2]
    local_heads = kv_used * per_kv
    score_scale = head_dim ** (-0.5)
    tile_len = tiles_kv.shape[2]

    def compute(operands):
        q_pick, t_pick = operands
        chosen_q = jnp.take(queries, q_pick, axis=0).reshape(
            batch_size, block_rows, kv_used, per_kv, head_dim
        )
        chosen_kv = jnp.take(tiles_kv, t_pick, axis=1)
        tile_keys = chosen_kv[0].reshape(batch_size, tile_len, kv_used, head_dim)
        tile_values = chosen_kv[1].reshape(batch_size, tile_len, kv_used, head_dim)
        scores = (
            jnp.einsum("btkgd,blkd->bkgtl", chosen_q, tile_keys, preferred_element_type=jnp.float32)
            * score_scale
        )
        row_best = jnp.max(scores, axis=4)
        weights = jnp.exp(scores - row_best[..., None])
        row_total = jnp.sum(weights, axis=4)
        blended = jnp.einsum(
            "bkgtl,blkd->btkgd",
            weights.astype(jnp.bfloat16),
            tile_values,
            preferred_element_type=jnp.float32,
        )
        blended = blended / jnp.transpose(row_total, (0, 3, 1, 2))[..., None]
        outputs = blended.reshape(batch_size, block_rows, q_width).astype(jnp.bfloat16)
        log_sums = (row_best + jnp.log(row_total)).reshape(batch_size, local_heads, block_rows)
        return (outputs, log_sums)

    def skipped(operands):
        return (
            jnp.zeros((batch_size, block_rows, q_width), jnp.bfloat16),
            jnp.zeros((batch_size, local_heads, block_rows), jnp.float32),
        )

    def one_batch(operands):
        q_pick, t_pick, live_now = operands
        return lax.cond(jnp.any(live_now), compute, skipped, (q_pick, t_pick))

    shaped = (
        query_pick.reshape(-1, batch_size),
        tile_pick.reshape(-1, batch_size),
        live_pick.reshape(-1, batch_size),
    )
    outputs, log_sums = lax.map(one_batch, shaped)
    return (
        outputs.reshape(item_count, block_rows, q_width),
        log_sums.reshape(item_count, local_heads, block_rows),
    )


def local(q_self, q_cross, kv_self, image_kv, cross_gate, doc_lengths, pair_tiles, tile_slot):
    tok_rows, q_width = q_self.shape
    head_dim = HEAD_DIM
    local_heads = q_width // head_dim
    grouping = Q_HEADS // KV_HEADS
    per_kv = min(local_heads, grouping)
    kv_used = local_heads // per_kv
    kv_first = lax.axis_index("rep") * local_heads // grouping
    kv_cols = kv_used * head_dim
    score_scale = head_dim ** (-0.5)
    layout = (kv_used, per_kv, head_dim)
    own_kv = lax.dynamic_slice_in_dim(kv_self, kv_first * head_dim, kv_cols, 2)
    tiles_kv = lax.dynamic_slice_in_dim(image_kv, kv_first * head_dim, kv_cols, 3)
    doc_ends = jnp.cumsum(doc_lengths)
    row_start = lax.axis_index("ctx") * tok_rows
    query_pos = row_start + jnp.arange(tok_rows, dtype=jnp.int32)
    query_doc = doc_index(doc_ends, query_pos)
    self_q = q_self.reshape(tok_rows, kv_used, per_kv, head_dim)
    shape_three = (tok_rows, kv_used, per_kv)
    starting = (
        jnp.full(shape_three, NEG_FILL, jnp.float32),
        jnp.zeros(shape_three, jnp.float32),
        jnp.zeros(shape_three + (head_dim,), jnp.float32),
    )
    shard_kv = lax.all_gather(own_kv, "ctx", axis=1, tiled=True)
    key_rows = shard_kv.shape[1]
    step_rows = math.gcd(key_rows, 512)

    def absorb_rows(turn_index, running_state):
        row_best, row_total, weighted = running_state
        offset = turn_index * step_rows
        part_kv = lax.dynamic_slice_in_dim(shard_kv, offset, step_rows, 1)
        tile_keys = part_kv[0].reshape(step_rows, kv_used, head_dim)
        tile_values = part_kv[1].reshape(step_rows, kv_used, head_dim)
        key_pos = offset + jnp.arange(step_rows, dtype=jnp.int32)
        key_doc = doc_index(doc_ends, key_pos)
        allowed = (key_pos[None, :] <= query_pos[:, None]) & (
            key_doc[None, :] == query_doc[:, None]
        )
        allowed = allowed[:, None, None, :]
        scores = (
            jnp.einsum("tkgd,nkd->tkgn", self_q, tile_keys, preferred_element_type=jnp.float32)
            * score_scale
        )
        scores = jnp.where(allowed, scores, NEG_FILL)
        new_best = jnp.maximum(row_best, jnp.max(scores, axis=3))
        weights = jnp.where(allowed, jnp.exp(scores - new_best[..., None]), 0.0)
        fading = jnp.exp(row_best - new_best)
        row_total = row_total * fading + jnp.sum(weights, axis=3)
        weighted = weighted * fading[..., None] + jnp.einsum(
            "tkgn,nkd->tkgd",
            weights.astype(jnp.bfloat16),
            tile_values,
            preferred_element_type=jnp.float32,
        )
        return (new_best, row_total, weighted)

    row_best, row_total, weighted = lax.fori_loop(0, key_rows // step_rows, absorb_rows, starting)
    self_out = (weighted / row_total[..., None]).reshape(tok_rows, q_width)
    block_count = tok_rows // BLOCK
    request_count = block_count * PAIRS
    ctx_count = lax.axis_size("ctx")
    tiles_dev = image_kv.shape[1]
    all_tiles = tile_slot.shape[0]
    capacity = max(2, -(-request_count // ctx_count))
    flat_tiles = pair_tiles.reshape(request_count)
    tile_match = flat_tiles[:, None] == jnp.arange(all_tiles, dtype=jnp.int32)[None, :]
    stored_at = jnp.sum(jnp.where(tile_match, tile_slot[None, :], 0), axis=1)
    owner_ctx = stored_at // tiles_dev
    local_tile = stored_at % tiles_dev
    q_blocks = q_cross.reshape(block_count, BLOCK, q_width)
    block_ids = jnp.arange(block_count, dtype=jnp.int32)
    owner_grid = owner_ctx.reshape(block_count, PAIRS)
    ctx_ids = jnp.arange(ctx_count, dtype=jnp.int32)
    block_reads = jnp.any(owner_grid[:, :, None] == ctx_ids[None, None, :], axis=1)
    reads_count = block_reads.astype(jnp.int32)
    block_rank = jnp.cumsum(reads_count, axis=0) - reads_count
    block_cap = max(1, capacity // PAIRS)
    slot_count = ctx_count * block_cap
    slot_of_pair = owner_grid * block_cap + jnp.take_along_axis(block_rank, owner_grid, axis=1)
    unit_slot = ctx_ids[None, :] * block_cap + block_rank
    unit_match = block_reads[:, :, None] & (
        unit_slot[:, :, None] == jnp.arange(slot_count, dtype=jnp.int32)[None, None, :]
    )
    slot_block = jnp.sum(jnp.where(unit_match, block_ids[:, None, None], 0), axis=(0, 1))
    slot_live = jnp.any(unit_match, axis=(0, 1)).astype(jnp.int32)
    outgoing = jnp.take(q_blocks, slot_block, axis=0).reshape(ctx_count, block_cap, BLOCK, q_width)
    wanted = slot_live.reshape(ctx_count, block_cap)
    arrived = lax.all_to_all(outgoing, "ctx", split_axis=0, concat_axis=0, tiled=True)
    asked = lax.all_to_all(wanted, "ctx", split_axis=0, concat_axis=0, tiled=True)
    sources, slots_here = asked.shape
    item_count = sources * slots_here
    flat_q = arrived.reshape(item_count, BLOCK, q_width)
    pair_count = item_count * tiles_dev
    pair_ids = jnp.arange(pair_count, dtype=jnp.int32)
    live_pairs = jnp.repeat(asked.reshape(item_count), tiles_dev) > 0
    outputs, log_sums = attend_tiles(
        flat_q, pair_ids // tiles_dev, pair_ids % tiles_dev, live_pairs, tiles_kv, layout
    )
    partials, log_sums = send_back(
        outputs.reshape(sources, slots_here, tiles_dev, BLOCK, q_width),
        log_sums.reshape(sources, slots_here, tiles_dev, local_heads, BLOCK),
    )
    result_index = slot_of_pair.reshape(request_count) * tiles_dev + local_tile
    flat_partials = partials.reshape(slot_count * tiles_dev, BLOCK, q_width)
    flat_sums = log_sums.reshape(slot_count * tiles_dev, local_heads, BLOCK)
    pair_out = (
        jnp.take(flat_partials, result_index, axis=0)
        .astype(jnp.float32)
        .reshape(block_count, PAIRS, BLOCK, local_heads, head_dim)
    )
    pair_sums = jnp.take(flat_sums, result_index, axis=0).reshape(
        block_count, PAIRS, local_heads, BLOCK
    )
    top_sum = jnp.max(pair_sums, axis=1, keepdims=True)
    factors = jnp.exp(pair_sums - top_sum)
    denominator = jnp.sum(factors, axis=1)
    shares = jnp.transpose(factors, (0, 1, 3, 2))[..., None]
    cross_sum = jnp.sum(shares * pair_out, axis=1)
    cross_out = (cross_sum / jnp.transpose(denominator, (0, 2, 1))[..., None]).reshape(
        tok_rows, q_width
    )
    head_gate = jnp.repeat(jnp.tanh(cross_gate), head_dim)
    return (self_out + head_gate[None, :] * cross_out).astype(jnp.bfloat16)


def solution(mesh):
    in_specs = (
        P(("groups", "ctx"), ("head", "rep")),
        P(("groups", "ctx"), ("head", "rep")),
        P(None, ("groups", "ctx"), "head"),
        P(None, ("groups", "ctx"), None, "head"),
        P(("head", "rep")),
        P("groups"),
        P(("groups", "ctx"), None),
        P("groups"),
    )
    out_specs = P(("groups", "ctx"), ("head", "rep"))
    return jax.shard_map(local, mesh=mesh, in_specs=in_specs, out_specs=out_specs, check_vma=False)
```

profile of v0, /device:TPU:0, one launch (start us, length us, event | category | flops | bytes accessed | tf_op | source)
XLA Modules:
  0.0 198.7 jit_solution(3391583909885249993)
XLA Ops:
  3.1 6.3 %all-to-all-start = ((s32[4,1,1]{2,1,0:T(1,128)}), s32[4,1,1]{2,1,0:T(1,128)S(1)}, u32[]{:S(2)}, u32[]{:S(2)}) async-start(s32[4,1,1]{2,1,0:T(1,128)} %copy.69), calls=%async_computation | async-start | bytes 4096 | tf_op jit(solution)/shard_map/all_to_all | solution.py:175
  9.6 6.2 %constant_dynamic-slice_fusion.1 = bf16[2,2,1601,256]{3,1,2,0:T(2,128)(2,1)} fusion(bf16[2,2,1601,512]{3,1,2,0:T(2,128)(2,1)} %param.17, s32[]{:T(128)S(6)} %select_n.197), kind=kLoop, calls=%fused_computation.127 | loop fusion | bytes 6557700 | tf_op jit(solution)/shard_map/dynamic_slice | solution.py:98
  16.0 15.5 %all_gather.3 = bf16[2,512,256]{1,2,0:T(8,128)(2,1)S(1)} all-gather(bf16[2,128,256]{1,2,0:T(8,128)(2,1)S(1)} %copy.89), channel_id=1, replica_groups=mesh['groups'=2,'ctx'=4,'head'=2,'rep'=2] {'ctx'}, dimensions={1}, use_global_device_ids=true | all-gather | bytes 655360 | tf_op jit(solution)/shard_map/all_gather | solution.py:110
  34.4 2.8 %fusion.22 = (f32[128,2,8]{0,2,1:T(8,128)S(1)}, f32[2,512,128,8]{2,1,3,0:T(8,128)}) fusion(pred[128,512]{0,1:T(8,128)(4,1)S(1)} %fusion.41, bf16[512,2,128,1]{0,2,3,1:T(8,128)(2,1)S(1)} %bitcast.174, bf16[128,2,8,128]{3,2,1,0:T(8,128)(2,1)S(1)} %bitcast.172), kind=kOutput, calls=%fused_computation.49 | convolution fusion | flops 271579136 | bytes 5054464 | tf_op jit(solution)/shard_map/while/body/eval_jaxpr/tkgd,nkd->tkgn/dot_general | solution.py:127
  37.2 3.7 %all-to-all-start.1 = ((bf16[4,1,32,2048]{3,2,1,0:T(8,128)(2,1)}), bf16[4,1,32,2048]{3,2,1,0:T(8,128)(2,1)S(1)}, u32[]{:S(2)}, u32[]{:S(2)}) async-start(bf16[4,1,32,2048]{3,2,1,0:T(8,128)(2,1)} %select_bitcast_fusion.1), calls=%async_computation.1 | async-start | bytes 1048576 | tf_op jit(solution)/shard_map/all_to_all | solution.py:174
  41.5 4.2 %copy.90 = bf16[2,2,1601,256]{3,2,1,0:T(8,128)(2,1)} copy(bf16[2,2,1601,256]{3,1,2,0:T(2,128)(2,1)} %constant_dynamic-slice_fusion.1) | data formatting | bytes 6557696
  47.8 5.4 %all-to-all-done.1 = bf16[4,1,32,2048]{3,2,1,0:T(8,128)(2,1)S(1)} async-done(((bf16[4,1,32,2048]{3,2,1,0:T(8,128)(2,1)}), bf16[4,1,32,2048]{3,2,1,0:T(8,128)(2,1)S(1)}, u32[]{:S(2)}, u32[]{:S(2)}) %all-to-all-start.1) | async-done | bytes 524320 | tf_op jit(solution)/shard_map/all_to_all | solution.py:174
  53.3 102.7 %while.3 = (s32[]{:T(128)}, bf16[2,4,32,2048]{3,2,1,0:T(8,128)(2,1)}, f32[2,4,16,32]{3,2,1,0:T(8,128)S(1)}, pred[2,4]{1,0:T(4,128)(4,1)S(1)}, bf16[2,2,1601,256]...) while((s32[]{:T(128)}, ...), condition=%wide.region_16.18_spmd.clone, body=%wide.region_10.17_spmd.clone.sunk | while | flops 1709066496 | bytes 105846136 | solution.py:79
  54.6 49.2 %conditional.3 = (bf16[1,4,32,2048]{3,2,1,0:T(8,128)(2,1)S(1)}, f32[1,4,16,32]{3,2,1,0:T(8,128)S(1)}) conditional(s32[]{:T(128)} %convert_element_type.96, () %tuple.63, (s32[2,4]{1,0:T(2,128)S(1)}, s32[]{:T(128)}, bf16[2,2,1601,256]{3,2,1,0:T(8,128)(2,1)}, s32[2,4]{1,0:T(2,128)S(1)}, bf16[4,32,2048]{2,1,0:T(8,128)(2,1)S(1)}, ...), branch_computations={%region_12.13_spmd, %region_13.16_spmd.clone} | conditional | flops 1709066368 | bytes 104731136 | solution.py:72
  55.5 5.7 %gather_fusion = bf16[4,2,1601,256]{3,2,1,0:T(8,128)(2,1)} fusion(bf16[2,2,1601,256]{3,2,1,0:T(8,128)(2,1)} %get-tuple-element.170, s32[1024]{0:T(1024)S(1)} %pad_clamp_fusion.1), kind=kCustom, calls=%fused_computation.1.clone | custom fusion | bytes 13115408 | tf_op jit(solution)/shard_map/while/body/eval_jaxpr/cond/branch_1_fun/jit(_take)/gather | solution.py:43
  61.2 3.6 %select_bitcast_fusion = bf16[2,4,1601,256]{3,2,0,1:T(8,128)(2,1)S(1)} fusion(bf16[4,2,1601,256]{3,2,1,0:T(8,128)(2,1)} %gather_fusion, pred[4]{0:T(512)(128)(4,1)S(1)} %get-tuple-element.216), kind=kLoop, calls=%fused_computation.16 | loop fusion | flops 3278848 | bytes 13115396 | tf_op jit(solution)/shard_map/while/body/eval_jaxpr/cond/branch_1_fun/jit(_take)/select_n | solution.py:43
  64.8 3.2 %fusion.61 = (bf16[1,4,1601,256]{3,2,0,1:T(8,128)(2,1)}, bf16[1,4,1601,256]{3,2,0,1:T(8,128)(2,1)}) fusion(bf16[2,4,1601,256]{3,2,0,1:T(8,128)(2,1)S(1)} %select_bitcast_fusion), kind=kLoop, calls=%fused_computation.134 | loop fusion | bytes 13115392 | tf_op jit(solution)/shard_map/while/body/eval_jaxpr/cond/branch_1_fun/slice | solution.py:44
  68.0 5.5 %copy.86 = bf16[1,4,1601,256]{2,3,1,0:T(8,128)(2,1)} copy(bf16[1,4,1601,256]{3,2,0,1:T(8,128)(2,1)} %get-tuple-element.210) | data formatting | bytes 6557696 | tf_op jit(solution)/shard_map/while/body/eval_jaxpr/cond/branch_1_fun/slice | solution.py:44
  73.5 8.8 %bitcast_reduce_fusion = (f32[4,2,8,32]{3,2,1,0:T(8,128)S(1)}, f32[4,2,1601,32,8]{2,3,4,1,0:T(8,128)}) fusion(bf16[4,1601,2,128,1]{1,3,4,2,0:T(8,128)(2,1)} %bitcast.162, bf16[4,32,2,8,128]{4,3,2,1,0:T(8,128)(2,1)S(1)} %bitcast.164), kind=kOutput, calls=%fused_computation.9 | convolution fusion | flops 845940736 | bytes 16926720 | tf_op jit(solution)/shard_map/while/body/eval_jaxpr/cond/branch_1_fun/btkgd,blkd->bkgtl/dot_general | solution.py:47
  82.2 7.3 %fusion.5 = f32[4,2,8,32]{3,2,1,0:T(8,128)S(1)} fusion(f32[4,2,1601,32,8]{2,3,4,1,0:T(8,128)} %get-tuple-element.215, f32[4,2,8,32]{3,2,1,0:T(8,128)S(1)} %get-tuple-element.214), kind=kLoop, calls=%fused_computation.11 | loop fusion | flops 9834496 | bytes 13131776 | tf_op jit(solution)/shard_map/while/body/eval_jaxpr/cond/branch_1_fun/reduce_sum | solution.py:52
  89.6 5.5 %copy.85 = bf16[1,4,1601,256]{2,3,1,0:T(8,128)(2,1)} copy(bf16[1,4,1601,256]{3,2,0,1:T(8,128)(2,1)} %get-tuple-element.211) | data formatting | bytes 6557696 | tf_op jit(solution)/shard_map/while/body/eval_jaxpr/cond/branch_1_fun/slice | solution.py:45
  95.0 8.3 %divide_convert_fusion = bf16[4,32,2,8,128]{4,1,3,2,0:T(8,128)(2,1)S(1)} fusion(bf16[4,1601,2,128,1]{1,3,4,2,0:T(8,128)(2,1)} %bitcast.163, f32[4,2,1601,32,8]{2,3,4,1,0:T(8,128)} %get-tuple-element.215, f32[4,2,8,32]{3,2,1,0:T(8,128)S(1)} %get-tuple-element.214, f32[4,32,2,8]{1,3,2,0:T(8,128)S(1)} %bitcast.171), kind=kOutput, calls=%fused_computation.18 | convolution fusion | flops 849745920 | bytes 16934912 | tf_op jit(solution)/shard_map/while/body/eval_jaxpr/cond/branch_1_fun/bkgtl,blkd->btkgd/dot_general | solution.py:53
  106.0 49.2 %conditional.3 = (bf16[1,4,32,2048]{3,2,1,0:T(8,128)(2,1)S(1)}, f32[1,4,16,32]{3,2,1,0:T(8,128)S(1)}) conditional(s32[]{:T(128)} %convert_element_type.96, () %tuple.63, (s32[2,4]{1,0:T(2,128)S(1)}, s32[]{:T(128)}, bf16[2,2,1601,256]{3,2,1,0:T(8,128)(2,1)}, s32[2,4]{1,0:T(2,128)S(1)}, bf16[4,32,2048]{2,1,0:T(8,128)(2,1)S(1)}, ...), branch_computations={%region_12.13_spmd, %region_13.16_spmd.clone} | conditional | flops 1709066368 | bytes 104731136 | solution.py:72
  106.9 5.7 %gather_fusion = bf16[4,2,1601,256]{3,2,1,0:T(8,128)(2,1)} fusion(bf16[2,2,1601,256]{3,2,1,0:T(8,128)(2,1)} %get-tuple-element.170, s32[1024]{0:T(1024)S(1)} %pad_clamp_fusion.1), kind=kCustom, calls=%fused_computation.1.clone | custom fusion | bytes 13115408 | tf_op jit(solution)/shard_map/while/body/eval_jaxpr/cond/branch_1_fun/jit(_take)/gather | solution.py:43
  112.6 3.6 %select_bitcast_fusion = bf16[2,4,1601,256]{3,2,0,1:T(8,128)(2,1)S(1)} fusion(bf16[4,2,1601,256]{3,2,1,0:T(8,128)(2,1)} %gather_fusion, pred[4]{0:T(512)(128)(4,1)S(1)} %get-tuple-element.216), kind=kLoop, calls=%fused_computation.16 | loop fusion | flops 3278848 | bytes 13115396 | tf_op jit(solution)/shard_map/while/body/eval_jaxpr/cond/branch_1_fun/jit(_take)/select_n | solution.py:43
  116.1 3.2 %fusion.61 = (bf16[1,4,1601,256]{3,2,0,1:T(8,128)(2,1)}, bf16[1,4,1601,256]{3,2,0,1:T(8,128)(2,1)}) fusion(bf16[2,4,1601,256]{3,2,0,1:T(8,128)(2,1)S(1)} %select_bitcast_fusion), kind=kLoop, calls=%fused_computation.134 | loop fusion | bytes 13115392 | tf_op jit(solution)/shard_map/while/body/eval_jaxpr/cond/branch_1_fun/slice | solution.py:44
  119.3 5.5 %copy.86 = bf16[1,4,1601,256]{2,3,1,0:T(8,128)(2,1)} copy(bf16[1,4,1601,256]{3,2,0,1:T(8,128)(2,1)} %get-tuple-element.210) | data formatting | bytes 6557696 | tf_op jit(solution)/shard_map/while/body/eval_jaxpr/cond/branch_1_fun/slice | solution.py:44
  124.8 8.8 %bitcast_reduce_fusion = (f32[4,2,8,32]{3,2,1,0:T(8,128)S(1)}, f32[4,2,1601,32,8]{2,3,4,1,0:T(8,128)}) fusion(bf16[4,1601,2,128,1]{1,3,4,2,0:T(8,128)(2,1)} %bitcast.162, bf16[4,32,2,8,128]{4,3,2,1,0:T(8,128)(2,1)S(1)} %bitcast.164), kind=kOutput, calls=%fused_computation.9 | convolution fusion | flops 845940736 | bytes 16926720 | tf_op jit(solution)/shard_map/while/body/eval_jaxpr/cond/branch_1_fun/btkgd,blkd->bkgtl/dot_general | solution.py:47
  133.6 7.3 %fusion.5 = f32[4,2,8,32]{3,2,1,0:T(8,128)S(1)} fusion(f32[4,2,1601,32,8]{2,3,4,1,0:T(8,128)} %get-tuple-element.215, f32[4,2,8,32]{3,2,1,0:T(8,128)S(1)} %get-tuple-element.214), kind=kLoop, calls=%fused_computation.11 | loop fusion | flops 9834496 | bytes 13131776 | tf_op jit(solution)/shard_map/while/body/eval_jaxpr/cond/branch_1_fun/reduce_sum | solution.py:52
  140.9 5.5 %copy.85 = bf16[1,4,1601,256]{2,3,1,0:T(8,128)(2,1)} copy(bf16[1,4,1601,256]{3,2,0,1:T(8,128)(2,1)} %get-tuple-element.211) | data formatting | bytes 6557696 | tf_op jit(solution)/shard_map/while/body/eval_jaxpr/cond/branch_1_fun/slice | solution.py:45
  146.4 8.3 %divide_convert_fusion = bf16[4,32,2,8,128]{4,1,3,2,0:T(8,128)(2,1)S(1)} fusion(bf16[4,1601,2,128,1]{1,3,4,2,0:T(8,128)(2,1)} %bitcast.163, f32[4,2,1601,32,8]{2,3,4,1,0:T(8,128)} %get-tuple-element.215, f32[4,2,8,32]{3,2,1,0:T(8,128)S(1)} %get-tuple-element.214, f32[4,32,2,8]{1,3,2,0:T(8,128)S(1)} %bitcast.171), kind=kOutput, calls=%fused_computation.18 | convolution fusion | flops 849745920 | bytes 16934912 | tf_op jit(solution)/shard_map/while/body/eval_jaxpr/cond/branch_1_fun/bkgtl,blkd->btkgd/dot_general | solution.py:53
  156.7 3.5 %all-to-all-start.2 = ((f32[4,1,1024]{2,1,0:T(1,128)}), f32[4,1,1024]{2,1,0:T(1,128)S(1)}, u32[]{:S(2)}, u32[]{:S(2)}) async-start(f32[4,1,1024]{2,1,0:T(1,128)} %reshape.533), calls=%async_computation.2 | async-start | bytes 32768 | tf_op jit(solution)/shard_map/all_to_all | solution.py:24
  161.1 4.5 %all-to-all-done.2 = f32[4,1,1024]{2,1,0:T(1,128)S(1)} async-done(((f32[4,1,1024]{2,1,0:T(1,128)}), f32[4,1,1024]{2,1,0:T(1,128)S(1)}, u32[]{:S(2)}, u32[]{:S(2)}) %all-to-all-start.2) | async-done | bytes 16416 | tf_op jit(solution)/shard_map/all_to_all | solution.py:24
  165.5 3.5 %all-to-all-start.3 = ((bf16[4,1,2,32,2048]{4,3,2,1,0:T(8,128)(2,1)}), bf16[4,1,2,32,2048]{4,3,2,1,0:T(8,128)(2,1)S(1)}, u32[]{:S(2)}, u32[]{:S(2)}) async-start(bf16[4,1,2,32,2048]{4,3,2,1,0:T(8,128)(2,1)} %bitcast.35), calls=%async_computation.3 | async-start | bytes 2097152 | tf_op jit(solution)/shard_map/all_to_all | solution.py:23
  169.1 4.4 %fusion.36 = f32[128,2,8,128]{0,3,2,1:T(8,128)} fusion(bf16[512,2,128,1]{0,2,3,1:T(8,128)(2,1)S(1)} %bitcast.177, f32[2,512,128,8]{2,1,3,0:T(8,128)} %get-tuple-element.226, f32[128,2,8]{0,2,1:T(8,128)S(1)} %copy-done.10, pred[128,512]{0,1:T(8,128)(4,1)S(1)} %copy-done.5, f32[128,2,8]{0,2,1:T(8,128)S(1)} %copy-done.15, f32[128,2,8]{0,2,1:T(8,128)S(1)} %copy-done.14), kind=kOutput, calls=%fused_computation.59 | convolution fusion | flops 274202624 | bytes 5595136 | tf_op jit(solution)/shard_map/while/body/eval_jaxpr/tkgn,nkd->tkgd/dot_general | solution.py:135
  177.6 13.9 %all-to-all-done.3 = bf16[4,1,2,32,2048]{4,3,2,1,0:T(8,128)(2,1)S(1)} async-done(((bf16[4,1,2,32,2048]{4,3,2,1,0:T(8,128)(2,1)}), bf16[4,1,2,32,2048]{4,3,2,1,0:T(8,128)(2,1)S(1)}, u32[]{:S(2)}, u32[]{:S(2)}) %all-to-all-start.3) | async-done | bytes 1048608 | tf_op jit(solution)/shard_map/all_to_all | solution.py:23
  193.5 2.3 %copy.93 = bf16[64,8,16,128]{3,2,1,0:T(8,128)(2,1)S(1)} copy(bf16[64,8,16,128]{3,1,2,0:T(8,128)(2,1)} %bitcast.169) | data formatting | bytes 4194304
  (138 shorter events, 25.0 us)
Async XLA Ops:
  0.0 32.7 %copy-start = (bf16[128,2048]{1,0:T(8,128)(2,1)S(1)}, bf16[128,2048]{1,0:T(8,128)(2,1)}, u32[]{:S(2)}) copy-start(bf16[128,2048]{1,0:T(8,128)(2,1)} %param.15) | copy-start | bytes 1572868
  0.0 15.9 %copy-start.8 = (bf16[2,128,512]{2,1,0:T(8,128)(2,1)S(1)}, bf16[2,128,512]{2,1,0:T(8,128)(2,1)}, u32[]{:S(2)}) copy-start(bf16[2,128,512]{2,1,0:T(8,128)(2,1)} %param.16) | copy-start | bytes 786436
  1.6 39.3 %copy-start.16 = (s32[16]{0:T(128)}, s32[16]{0:T(128)S(1)}, u32[]{:S(2)}) copy-start(s32[16]{0:T(128)S(1)} %select_reduce_fusion.2) | copy-start | bytes 196
  1.7 14.2 %copy-start.11 = (s32[4,4]{1,0:T(4,128)}, s32[4,4]{1,0:T(4,128)S(1)}, u32[]{:S(2)}) copy-start(s32[4,4]{1,0:T(4,128)S(1)} %reduce_sum.86) | copy-start | bytes 196
  3.1 34.1 %all-to-all-start = ((s32[4,1,1]{2,1,0:T(1,128)}), s32[4,1,1]{2,1,0:T(1,128)S(1)}, u32[]{:S(2)}, u32[]{:S(2)}) async-start(s32[4,1,1]{2,1,0:T(1,128)} %copy.69), calls=%async_computation | async-start | bytes 4096 | tf_op jit(solution)/shard_map/all_to_all | solution.py:175
  9.6 22.6 %copy-start.18 = (s32[4]{0:T(128)S(1)}, s32[4]{0:T(128)}, u32[]{:S(2)}) copy-start(s32[4]{0:T(128)} %param.19) | copy-start | bytes 52
  9.6 23.0 %copy-start.6 = (bf16[128,2048]{1,0:T(8,128)(2,1)S(1)}, bf16[128,2048]{1,0:T(8,128)(2,1)}, u32[]{:S(2)}) copy-start(bf16[128,2048]{1,0:T(8,128)(2,1)} %param.14) | copy-start | bytes 1572868
  34.4 11.4 %copy-start.4 = (pred[128,512]{0,1:T(8,128)(4,1)}, pred[128,512]{0,1:T(8,128)(4,1)S(1)}, u32[]{:S(2)}) copy-start(pred[128,512]{0,1:T(8,128)(4,1)S(1)} %fusion.41) | copy-start | bytes 196612
  37.2 16.1 %all-to-all-start.1 = ((bf16[4,1,32,2048]{3,2,1,0:T(8,128)(2,1)}), bf16[4,1,32,2048]{3,2,1,0:T(8,128)(2,1)S(1)}, u32[]{:S(2)}, u32[]{:S(2)}) async-start(bf16[4,1,32,2048]{3,2,1,0:T(8,128)(2,1)} %select_bitcast_fusion.1), calls=%async_computation.1 | async-start | bytes 1048576 | tf_op jit(solution)/shard_map/all_to_all | solution.py:174
  40.8 5.9 %copy-start.9 = (f32[128,2,8]{0,2,1:T(8,128)}, f32[128,2,8]{0,2,1:T(8,128)S(1)}, u32[]{:S(2)}) copy-start(f32[128,2,8]{0,2,1:T(8,128)S(1)} %broadcast_maximum_fusion) | copy-start | bytes 24580
  41.5 4.2 %copy-start.3 = (f32[2,512,128,8]{2,1,3,0:T(8,128)S(1)}, f32[2,512,128,8]{2,1,3,0:T(8,128)}, u32[]{:S(2)}) copy-start(f32[2,512,128,8]{2,1,3,0:T(8,128)} %get-tuple-element.226) | copy-start | bytes 12582916
  53.2 106.9 %copy-start.13 = (s32[4,4,1]{1,0,2:T(4,128)S(1)}, s32[4,4,1]{1,0,2:T(4,128)}, u32[]{:S(2)}) copy-start(s32[4,4,1]{1,0,2:T(4,128)} %reduce_sum.87) | copy-start | bytes 196
  53.2 107.0 %copy-start.2 = (s32[4,4]{1,0:T(4,128)S(1)}, s32[4,4]{1,0:T(4,128)}, u32[]{:S(2)}) copy-start(s32[4,4]{1,0:T(4,128)} %get-tuple-element.209) | copy-start | bytes 196
  156.0 13.1 %copy-start.5 = (pred[128,512]{0,1:T(8,128)(4,1)S(1)}, pred[128,512]{0,1:T(8,128)(4,1)}, u32[]{:S(2)}) copy-start(pred[128,512]{0,1:T(8,128)(4,1)} %copy-done.4) | copy-start | bytes 196612
  156.0 13.1 %copy-start.7 = (bf16[1,512,256]{1,2,0:T(8,128)(2,1)S(1)}, bf16[1,512,256]{1,2,0:T(8,128)(2,1)}, u32[]{:S(2)}) copy-start(bf16[1,512,256]{1,2,0:T(8,128)(2,1)} %get-tuple-element.220) | copy-start | bytes 786436
  156.0 13.1 %copy-start.10 = (f32[128,2,8]{0,2,1:T(8,128)S(1)}, f32[128,2,8]{0,2,1:T(8,128)}, u32[]{:S(2)}) copy-start(f32[128,2,8]{0,2,1:T(8,128)} %copy-done.9) | copy-start | bytes 24580
  156.0 13.1 %copy-start.14 = (f32[128,2,8]{0,2,1:T(8,128)S(1)}, f32[128,2,8]{0,2,1:T(8,128)}, u32[]{:S(2)}) copy-start(f32[128,2,8]{0,2,1:T(8,128)} %get-tuple-element.223) | copy-start | bytes 24580
  156.0 13.1 %copy-start.15 = (f32[128,2,8]{0,2,1:T(8,128)S(1)}, f32[128,2,8]{0,2,1:T(8,128)}, u32[]{:S(2)}) copy-start(f32[128,2,8]{0,2,1:T(8,128)} %get-tuple-element.224) | copy-start | bytes 24580
  156.7 8.8 %all-to-all-start.2 = ((f32[4,1,1024]{2,1,0:T(1,128)}), f32[4,1,1024]{2,1,0:T(1,128)S(1)}, u32[]{:S(2)}, u32[]{:S(2)}) async-start(f32[4,1,1024]{2,1,0:T(1,128)} %reshape.533), calls=%async_computation.2 | async-start | bytes 32768 | tf_op jit(solution)/shard_map/all_to_all | solution.py:24
  165.5 25.9 %all-to-all-start.3 = ((bf16[4,1,2,32,2048]{4,3,2,1,0:T(8,128)(2,1)}), bf16[4,1,2,32,2048]{4,3,2,1,0:T(8,128)(2,1)S(1)}, u32[]{:S(2)}, u32[]{:S(2)}) async-start(bf16[4,1,2,32,2048]{4,3,2,1,0:T(8,128)(2,1)} %bitcast.35), calls=%async_computation.3 | async-start | bytes 2097152 | tf_op jit(solution)/shard_map/all_to_all | solution.py:23
  169.1 6.0 %copy-start.19 = (f32[16]{0:T(128)S(1)}, f32[16]{0:T(128)}, u32[]{:S(2)}) copy-start(f32[16]{0:T(128)} %param.18) | copy-start | bytes 196
  169.1 6.0 %copy-start.17 = (s32[16]{0:T(128)S(1)}, s32[16]{0:T(128)}, u32[]{:S(2)}) copy-start(s32[16]{0:T(128)} %copy-done.16) | copy-start | bytes 196
  169.1 6.0 %copy-start.12 = (s32[4,4]{1,0:T(4,128)S(1)}, s32[4,4]{1,0:T(4,128)}, u32[]{:S(2)}) copy-start(s32[4,4]{1,0:T(4,128)} %copy-done.11) | copy-start | bytes 196
  193.5 5.2 %copy-start.1 = (bf16[128,2048]{1,0:T(8,128)(2,1)S(1)}, bf16[128,2048]{1,0:T(8,128)(2,1)}, u32[]{:S(2)}) copy-start(bf16[128,2048]{1,0:T(8,128)(2,1)} %param.15) | copy-start | bytes 1572868
where the time goes:
time: 200 us; the launch traced here: 199 us
  local copies, waits for them, and re-layouts  66.9 us (33%)
  matrix products  41.3 us (21%)
  other arithmetic  32.1 us (16%)
  waiting for transfers between devices  23.8 us (12%)
  starting transfers between devices  17 us (8%)
  blocking collectives  15.5 us (8%)
    dot_general x2, matrix products, compute(): jnp.einsum('btkgd,blkd->bkgtl', chosen_q, tile_keys, preferred_element_ty...  17.5 us
    slice x4, local copies, waits for them, and re-layouts, compute(): tile_keys = chosen_kv[0].reshape(batch_size, tile_len, kv_used, head_dim)  17.4 us
    dot_general x2, matrix products, compute(): jnp.einsum('bkgtl,blkd->btkgd', weights.astype(jnp.bfloat16), tile_values...  16.5 us
    all_gather x1, blocking collectives, local(): shard_kv = lax.all_gather(own_kv, 'ctx', axis=1, tiled=True)  15.5 us
    reduce_sum x2, other arithmetic, compute(): row_total = jnp.sum(weights, axis=4)  14.6 us
    all_to_all x1, waiting for transfers between devices, send_back(): lax.all_to_all(outputs, 'ctx', split_axis=0, concat_axis=0, tiled=True)  13.9 us
    gather x2, local copies, waits for them, and re-layouts, compute(): chosen_kv = jnp.take(tiles_kv, t_pick, axis=1)  11.3 us
    slice x2, local copies, waits for them, and re-layouts, compute(): tile_values = chosen_kv[1].reshape(batch_size, tile_len, kv_used, head_dim)  11 us
  transfers between devices with their start and end apart: 4, of which 3 were waited for; matrix products, arithmetic and copies ran while one was open for 14% of the time, Pallas kernels for 0%

commit v1 on v0

v1 whole, which is shorter than its diff:
```python
import functools
import math

import jax
import jax.numpy as jnp
from jax import lax
from jax.experimental import pallas as pl
from jax.experimental.pallas import tpu as pltpu
from jax.sharding import PartitionSpec as P

HEAD_DIM = 128
Q_HEADS = 64
KV_HEADS = 8
BLOCK = 32
PAIRS = 4

NEG_FILL = -1e30
META_ROWS = 16
EXP2_SCALE = HEAD_DIM ** (-0.5) * math.log2(math.e)


def owner_slots(pairs_ref, slots_ref):
    blocks, pairs = pairs_ref.shape
    return [[slots_ref[pairs_ref[b, p]] for p in range(pairs)] for b in range(blocks)]


def block_for(stored, owner, tiles_dev):
    block = jnp.int32(0)
    counts = [jnp.int32(0)] * tiles_dev
    for b, row in enumerate(stored):
        for slot in row:
            tile = slot - owner * tiles_dev
            block = jnp.where((tile >= 0) & (tile < tiles_dev), jnp.int32(b), block)
            counts = [n + (tile == i).astype(jnp.int32) for i, n in enumerate(counts)]
    return block, counts


def pack_body(where_ref, pairs_ref, slots_ref, q_ref, *out_refs, tiles_dev):
    stored = owner_slots(pairs_ref, slots_ref)
    heads = q_ref.shape[1] // HEAD_DIM
    tile_rows = lax.broadcasted_iota(jnp.int32, (META_ROWS, HEAD_DIM), 0)
    for distance, out_ref in enumerate(out_refs):
        block, counts = block_for(stored, where_ref[0] ^ distance, tiles_dev)
        rows = pl.ds(pl.multiple_of(block * BLOCK, BLOCK), BLOCK)
        for h in range(heads):
            out_ref[h * BLOCK : (h + 1) * BLOCK, :] = q_ref[rows, h * HEAD_DIM : (h + 1) * HEAD_DIM]
        meta = jnp.zeros((META_ROWS, HEAD_DIM), jnp.float32)
        for i, n in enumerate(counts):
            meta = jnp.where(tile_rows == i, n.astype(jnp.float32), meta)
        out_ref[heads * BLOCK :, :] = meta.astype(jnp.bfloat16)


def pack_queries(where, pair_tiles, tile_slot, q_cross, ctx_count, tiles_dev):
    rows = q_cross.shape[1] // HEAD_DIM * BLOCK + META_ROWS
    smem = pl.BlockSpec(memory_space=pltpu.SMEM)
    vmem = pl.BlockSpec(memory_space=pltpu.VMEM)
    return pl.pallas_call(
        functools.partial(pack_body, tiles_dev=tiles_dev),
        out_shape=[jax.ShapeDtypeStruct((rows, HEAD_DIM), jnp.bfloat16)] * ctx_count,
        in_specs=[smem, smem, smem, vmem],
        out_specs=[vmem] * ctx_count,
        name="pack_queries",
    )(where, pair_tiles, tile_slot, q_cross)


def tile_body(where_ref, q_ref, meta_ref, k_ref, v_ref, out_ref, lse_ref, best_sc, total_sc, sum_sc):
    tile = pl.program_id(1)

    @pl.when(tile == 0)
    def _():
        best_sc[...] = jnp.full(best_sc.shape, NEG_FILL, jnp.float32)
        total_sc[...] = jnp.zeros(total_sc.shape, jnp.float32)
        sum_sc[...] = jnp.zeros(sum_sc.shape, jnp.float32)

    scores = lax.dot_general(
        q_ref[...], k_ref[0, 0], (((1,), (1,)), ((), ())), preferred_element_type=jnp.float32
    )
    row_best = jnp.max(scores, axis=1, keepdims=True)
    weights = jnp.exp2((scores - row_best) * EXP2_SCALE)
    row_total = jnp.sum(weights, axis=1, keepdims=True)
    blended = jnp.dot(weights.astype(jnp.bfloat16), v_ref[0, 0], preferred_element_type=jnp.float32)
    meta = meta_ref[...].astype(jnp.float32)
    tile_rows = lax.broadcasted_iota(jnp.int32, meta.shape, 0)
    count = jnp.sum(jnp.where(tile_rows == tile, meta, 0.0), axis=0, keepdims=True)
    row_best = jnp.where(count > 0, row_best, NEG_FILL)
    old_best = best_sc[...]
    new_best = jnp.maximum(old_best, row_best)
    fading = jnp.exp2((old_best - new_best) * EXP2_SCALE)
    share = count * jnp.exp2((row_best - new_best) * EXP2_SCALE)
    best_sc[...] = new_best
    total_sc[...] = total_sc[...] * fading + row_total * share
    sum_sc[...] = sum_sc[...] * fading + blended * share

    @pl.when(tile == pl.num_programs(1) - 1)
    def _():
        total = total_sc[...]
        live = total > 0
        total = jnp.where(live, total, 1.0)
        out_ref[...] = (sum_sc[...] / total).astype(jnp.bfloat16)
        if lse_ref is not None:
            lse = best_sc[...] * (HEAD_DIM ** (-0.5)) + jnp.log(total)
            lse_ref[...] = jnp.where(live, lse, NEG_FILL)


def attend_tiles(where, packed, image_kv, kv_used, with_lse):
    tiles_dev, tile_len = image_kv.shape[1:3]
    q_rows = packed.shape[0] - META_ROWS
    rows = q_rows // kv_used
    meta_at = q_rows // META_ROWS
    out_spec = pl.BlockSpec((rows, HEAD_DIM), lambda k, i, w: (k, 0))
    out_specs = [out_spec]
    out_shape = [jax.ShapeDtypeStruct((q_rows, HEAD_DIM), jnp.bfloat16)]
    body = tile_body
    if with_lse:
        out_specs.append(out_spec)
        out_shape.append(jax.ShapeDtypeStruct((q_rows, HEAD_DIM), jnp.float32))
    else:
        body = lambda *refs: tile_body(*refs[:6], None, *refs[6:])
    return pl.pallas_call(
        body,
        out_shape=out_shape,
        grid_spec=pltpu.PrefetchScalarGridSpec(
            num_scalar_prefetch=1,
            grid=(kv_used, tiles_dev),
            in_specs=[
                pl.BlockSpec((rows, HEAD_DIM), lambda k, i, w: (k, 0)),
                pl.BlockSpec((META_ROWS, HEAD_DIM), lambda k, i, w: (meta_at, 0)),
                pl.BlockSpec((1, 1, tile_len, HEAD_DIM), lambda k, i, w: (0, i, 0, w[1] + k)),
                pl.BlockSpec((1, 1, tile_len, HEAD_DIM), lambda k, i, w: (1, i, 0, w[1] + k)),
            ],
            out_specs=out_specs,
            scratch_shapes=[pltpu.VMEM((rows, HEAD_DIM), jnp.float32)] * 3,
        ),
        name="attend_tiles",
    )(where, packed, packed, image_kv, image_kv)


def self_body(where_ref, docs_ref, q_ref, *refs):
    kv_refs, out_ref = refs[:-1], refs[-1]
    tok_rows = q_ref.shape[0]
    keys = jnp.concatenate([ref[0] for ref in kv_refs], axis=0)
    values = jnp.concatenate([ref[1] for ref in kv_refs], axis=0)
    shape = (tok_rows, keys.shape[0])
    row_start = where_ref[0] * tok_rows
    query_pos = row_start + lax.broadcasted_iota(jnp.int32, shape, 0)
    key_pos = row_start + tok_rows - shape[1] + lax.broadcasted_iota(jnp.int32, shape, 1)
    doc_start = jnp.zeros(shape, jnp.int32)
    doc_end = jnp.int32(0)
    for j in range(docs_ref.shape[0]):
        doc_end = doc_end + docs_ref[j]
        doc_start = jnp.where(query_pos >= doc_end, doc_end, doc_start)
    allowed = (key_pos <= query_pos) & (key_pos >= doc_start)
    for g in range(q_ref.shape[1] // HEAD_DIM):
        cols = slice(g * HEAD_DIM, (g + 1) * HEAD_DIM)
        scores = lax.dot_general(
            q_ref[:, cols], keys, (((1,), (1,)), ((), ())), preferred_element_type=jnp.float32
        )
        scores = jnp.where(allowed, scores, NEG_FILL)
        row_best = jnp.max(scores, axis=1, keepdims=True)
        weights = jnp.exp2((scores - row_best) * EXP2_SCALE)
        weights = jnp.where(allowed, weights, 0.0)
        row_total = jnp.sum(weights, axis=1, keepdims=True)
        blended = jnp.dot(weights.astype(jnp.bfloat16), values, preferred_element_type=jnp.float32)
        out_ref[:, cols] = blended / row_total


def attend_self(where, doc_lengths, q_self, pieces, kv_self, kv_used, per_kv):
    tok_rows, q_width = q_self.shape
    piece_spec = pl.BlockSpec((2, tok_rows, HEAD_DIM), lambda k, w, d: (0, 0, k))
    own_spec = pl.BlockSpec((2, tok_rows, HEAD_DIM), lambda k, w, d: (0, 0, w[1] + k))
    q_spec = pl.BlockSpec((tok_rows, per_kv * HEAD_DIM), lambda k, w, d: (0, k))
    return pl.pallas_call(
        self_body_call,
        out_shape=jax.ShapeDtypeStruct((tok_rows, q_width), jnp.float32),
        grid_spec=pltpu.PrefetchScalarGridSpec(
            num_scalar_prefetch=2,
            grid=(kv_used,),
            in_specs=[q_spec] + [piece_spec] * len(pieces) + [own_spec],
            out_specs=q_spec,
        ),
        name="attend_self",
    )(where, doc_lengths, q_self, *pieces, kv_self)


def self_body_call(*refs):
    self_body(*refs)


def mix_body(where_ref, pairs_ref, slots_ref, gate_ref, self_ref, *refs, tiles_dev):
    partial_refs, out_ref = refs[:-1], refs[-1]
    stored = owner_slots(pairs_ref, slots_ref)
    for distance, partial_ref in enumerate(partial_refs):
        block, _ = block_for(stored, where_ref[0] ^ distance, tiles_dev)
        rows = pl.ds(pl.multiple_of(block * BLOCK, BLOCK), BLOCK)
        for h in range(self_ref.shape[1] // HEAD_DIM):
            cols = slice(h * HEAD_DIM, (h + 1) * HEAD_DIM)
            cross = partial_ref[h * BLOCK : (h + 1) * BLOCK, :].astype(jnp.float32)
            mixed = self_ref[rows, cols] + gate_ref[:, cols] * cross
            out_ref[rows, cols] = mixed.astype(jnp.bfloat16)


def mix(where, pair_tiles, tile_slot, gate_cols, self_out, partials, tiles_dev):
    smem = pl.BlockSpec(memory_space=pltpu.SMEM)
    vmem = pl.BlockSpec(memory_space=pltpu.VMEM)
    return pl.pallas_call(
        functools.partial(mix_body, tiles_dev=tiles_dev),
        out_shape=jax.ShapeDtypeStruct(self_out.shape, jnp.bfloat16),
        in_specs=[smem] * 3 + [vmem] * (2 + len(partials)),
        out_specs=vmem,
        name="mix",
    )(where, pair_tiles, tile_slot, gate_cols, self_out, *partials)


def mix_owners(where, pair_tiles, tile_slot, gate_cols, self_out, partials, sums, tiles_dev):
    block_count = pair_tiles.shape[0]
    tok_rows, q_width = self_out.shape
    heads = q_width // HEAD_DIM
    owners = jnp.take(tile_slot, pair_tiles.reshape(-1), axis=0).reshape(block_count, -1) // tiles_dev
    partners = where[0] ^ jnp.arange(len(partials), dtype=jnp.int32)
    live = jnp.any(owners[:, :, None] == partners[None, None, :], axis=1)[:, :, None, None]
    lse = jnp.stack(sums)[None]
    top = jnp.max(jnp.where(live, lse, NEG_FILL), axis=1, keepdims=True)
    factors = jnp.where(live, jnp.exp(lse - top), 0.0)
    pieces = jnp.stack(partials).astype(jnp.float32)[None]
    cross = jnp.sum(factors * pieces, axis=1) / jnp.sum(factors, axis=1)
    cross = jnp.transpose(cross.reshape(block_count, heads, BLOCK, HEAD_DIM), (0, 2, 1, 3))
    return (self_out + gate_cols * cross.reshape(tok_rows, q_width)).astype(jnp.bfloat16)


def local(q_self, q_cross, kv_self, image_kv, cross_gate, doc_lengths, pair_tiles, tile_slot):
    tok_rows, q_width = q_self.shape
    local_heads = q_width // HEAD_DIM
    grouping = Q_HEADS // KV_HEADS
    per_kv = min(local_heads, grouping)
    kv_used = local_heads // per_kv
    ctx_count = lax.axis_size("ctx")
    tiles_dev = image_kv.shape[1]
    request_count = pair_tiles.shape[0] * PAIRS
    capacity = max(2, -(-request_count // ctx_count))
    one_owner = ctx_count * capacity == request_count and capacity == PAIRS
    reach = min(ctx_count - 1, -(-(ctx_count * tok_rows // 2 - 1) // tok_rows))

    here = lax.axis_index("ctx").astype(jnp.int32)
    kv_first = (lax.axis_index("rep") * local_heads // grouping).astype(jnp.int32)
    where = jnp.stack([here, kv_first])

    def exchange(array, distance):
        return lax.ppermute(array, "ctx", [(i, i ^ distance) for i in range(ctx_count)])

    piece = lax.dynamic_slice_in_dim(kv_self, kv_first * HEAD_DIM, kv_used * HEAD_DIM, 2)
    pieces = []
    for step in range(reach):
        piece = lax.ppermute(piece, "ctx", [(i, i + 1) for i in range(step, ctx_count - 1)])
        pieces.insert(0, piece)

    packed = pack_queries(where, pair_tiles, tile_slot, q_cross, ctx_count, tiles_dev)
    order = list(range(ctx_count - 1, 0, -1))
    arrived = {d: exchange(packed[d], d) for d in order}
    arrived[0] = packed[0]
    partials, sums = {}, {}
    for d in [0] + order:
        results = attend_tiles(where, arrived[d], image_kv, kv_used, not one_owner)
        partials[d] = exchange(results[0], d) if d else results[0]
        if not one_owner:
            sums[d] = exchange(results[1], d) if d else results[1]
    self_out = attend_self(where, doc_lengths, q_self, pieces, kv_self, kv_used, per_kv)
    gate_cols = jnp.repeat(jnp.tanh(cross_gate), HEAD_DIM)[None, :]
    partials = [partials[d] for d in range(ctx_count)]
    if one_owner:
        return mix(where, pair_tiles, tile_slot, gate_cols, self_out, partials, tiles_dev)
    sums = [sums[d] for d in range(ctx_count)]
    return mix_owners(where, pair_tiles, tile_slot, gate_cols, self_out, partials, sums, tiles_dev)


def solution(mesh):
    in_specs = (
        P(("groups", "ctx"), ("head", "rep")),
        P(("groups", "ctx"), ("head", "rep")),
        P(None, ("groups", "ctx"), "head"),
        P(None, ("groups", "ctx"), None, "head"),
        P(("head", "rep")),
        P("groups"),
        P(("groups", "ctx"), None),
        P("groups"),
    )
    out_specs = P(("groups", "ctx"), ("head", "rep"))
    return jax.shard_map(local, mesh=mesh, in_specs=in_specs, out_specs=out_specs, check_vma=False)
```

time: 200 us -> 70.9 us (0.35)
  local copies, waits for them, and re-layouts: 66.9 us -> 11 us
  matrix products: 41.3 us -> 0 us
  Pallas kernels: 0 us -> 39.1 us
  other arithmetic: 32.1 us -> 0.56 us
  waiting for transfers between devices: 23.8 us -> 0.02 us
  blocking collectives: 15.5 us -> 0 us
  starting transfers between devices: 17 us -> 19.5 us
    dot_general x6 -> x0, matrix products: 41.3 us -> none  [the longest x2 17.5 us: compute(): jnp.einsum('btkgd,blkd->bkgtl', chosen_q, tile_keys, preferred_element_ty...]
    pallas_call x0 -> x7, Pallas kernels: none -> 39.1 us  [the longest x4 27.7 us: attend_tiles(): pl.pallas_call(body, out_shape=out_shape, grid_spec=pltpu.PrefetchScalarG...]
    slice x7 -> x0, local copies, waits for them, and re-layouts: 29.1 us -> none  [the longest x4 17.4 us: compute(): tile_keys = chosen_kv[0].reshape(batch_size, tile_len, kv_used, head_dim)]
    all_to_all x4 -> x0, waiting for transfers between devices: 23.8 us -> none  [the longest x1 13.9 us: send_back(): lax.all_to_all(outputs, 'ctx', split_axis=0, concat_axis=0, tiled=True)]
    ppermute x0 -> x8, starting transfers between devices: none -> 19.5 us  [the longest x6 16 us: exchange(): lax.ppermute(array, 'ctx', [(i, i ^ distance) for i in range(ctx_count)])]
    reduce_sum x9 -> x0, other arithmetic: 18.1 us -> none  [the longest x2 14.6 us: compute(): row_total = jnp.sum(weights, axis=4)]
    all_to_all x4 -> x0, starting transfers between devices: 17 us -> none  [the longest x1 6.35 us: local(): lax.all_to_all(wanted, 'ctx', split_axis=0, concat_axis=0, tiled=True)]
    gather x10 -> x0, local copies, waits for them, and re-layouts: 16.5 us -> none  [the longest x2 11.3 us: compute(): chosen_kv = jnp.take(tiles_kv, t_pick, axis=1)]
  transfers between devices with their start and end apart: 4 -> 8, of which waited for: 3 -> 0; matrix products, arithmetic and copies ran while one was open for 14% -> 11% of each run, Pallas kernels for 0% -> 49%
where the time goes in v1:
time: 70.9 us; the launch traced here: 70.3 us
  Pallas kernels  39.1 us (55%)
  starting transfers between devices  19.5 us (28%)
  local copies, waits for them, and re-layouts  11 us (16%)
    pallas_call x4, Pallas kernels, attend_tiles(): pl.pallas_call(body, out_shape=out_shape, grid_spec=pltpu.PrefetchScalarG...  27.7 us
    ppermute x6, starting transfers between devices, exchange(): lax.ppermute(array, 'ctx', [(i, i ^ distance) for i in range(ctx_count)])  16 us
    unnamed x19, local copies, waits for them, and re-layouts  9.39 us
    pallas_call x1, Pallas kernels, attend_self(): pl.pallas_call(self_body_call, out_shape=jax.ShapeDtypeStruct((tok_rows,...  7 us
    ppermute x2, starting transfers between devices, local(): lax.ppermute(piece, 'ctx', [(i, i + 1) for i in range(step, ctx_count - 1)])  3.47 us
    pallas_call x1, Pallas kernels, mix(): pl.pallas_call(functools.partial(mix_body, tiles_dev=tiles_dev), out_shap...  2.32 us
    pallas_call x1, Pallas kernels, pack_queries(): pl.pallas_call(functools.partial(pack_body, tiles_dev=tiles_dev), out_sha...  2.16 us
  transfers between devices with their start and end apart: 8, of which 0 were waited for; matrix products, arithmetic and copies ran while one was open for 11% of the time, Pallas kernels for 49%

profile of v1, /device:TPU:0, one launch (start us, length us, event | category | flops | bytes accessed | tf_op | source)
XLA Modules:
  0.0 70.3 jit_solution(10127235487941442128)
XLA Ops:
  0.0 0.6 pad_add_fusion.refs_0_.where_ref
  0.6 2.2 %pack_queries.1 = (bf16[528,128]{1,0:T(8,128)(2,1)}, bf16[528,128]{1,0:T(8,128)(2,1)}, bf16[528,128]{1,0:T(8,128)(2,1)}, bf16[528,128]{1,0:T(8,128)(2,1)}) custom-call(s32[2]{0:T(128)} %pad_add_fusion.refs_0_.where_ref, s32[4,4]{1,0:T(4,128)} %pairs_ref.3, s32[8]{0:T(128)} %slots_ref.3, bf16[128,2048]{1,0:T(8,128)(2,1)} %q_ref.1), custom_call_target="tpu_custom_call" | custom-call | tf_op jit(solution)/shard_map/pack_queries/pallas_call | solution.py:57
  2.7 3.1 %collective-permute-start.2 = (bf16[528,128]{1,0:T(8,128)(2,1)}, bf16[528,128]{1,0:T(8,128)(2,1)S(1)}, u32[]{:S(2)}, u32[]{:S(2)}) collective-permute-start(bf16[528,128]{1,0:T(8,128)(2,1)} %get-tuple-element.10), channel_id=1, source_target_pairs={{0,4},{4,0},{8,12},{12,8},{1,5},{5,1},{9,13},{13,9},{2,6},{6,2},{1... | collective-permute-start | bytes 405512 | tf_op jit(solution)/shard_map/ppermute | solution.py:248
  5.8 2.6 %collective-permute-start.4 = (bf16[528,128]{1,0:T(8,128)(2,1)}, bf16[528,128]{1,0:T(8,128)(2,1)S(1)}, u32[]{:S(2)}, u32[]{:S(2)}) collective-permute-start(bf16[528,128]{1,0:T(8,128)(2,1)} %get-tuple-element.11), channel_id=1, source_target_pairs={{0,8},{4,12},{8,0},{12,4},{1,9},{5,13},{9,1},{13,5},{2,10},{6,14},... | collective-permute-start | bytes 405512 | tf_op jit(solution)/shard_map/ppermute | solution.py:248
  8.4 0.0 collective-permute-start.6
  8.4 0.9 %constant_dynamic-slice_fusion = bf16[2,128,256]{2,1,0:T(8,128)(2,1)S(1)} fusion(bf16[2,128,512]{2,1,0:T(8,128)(2,1)} %refs_5_.1, s32[]{:T(128)S(6)} %select_n.9), kind=kLoop, calls=%fused_computation.1 | loop fusion | bytes 262148 | tf_op jit(solution)/shard_map/dynamic_slice | solution.py:250
  9.3 2.8 %collective-permute-start = (bf16[2,128,256]{2,1,0:T(8,128)(2,1)S(1)}, bf16[2,128,256]{2,1,0:T(8,128)(2,1)S(1)}, u32[]{:S(2)}, u32[]{:S(2)}) collective-permute-start(bf16[2,128,256]{2,1,0:T(8,128)(2,1)S(1)} %constant_dynamic-slice_fusion), channel_id=1, source_target_pairs={{0,4},{4,8},{8,12},{1,5},{5,9},{9,13},{2,6},{6,10},{10,14},{3,7},{... | collective-permute-start | bytes 393224 | tf_op jit(solution)/shard_map/ppermute | solution.py:253
  12.1 6.8 %copy.9.refs_3_.refs_4_ = bf16[2,2,1601,512]{3,2,1,0:T(8,128)(2,1)} copy(bf16[2,2,1601,512]{3,1,2,0:T(2,128)(2,1)} %param.11) | data formatting | bytes 13115392 | tf_op args[3]
  18.9 0.0 collective-permute-done.refs_4_
  18.9 0.7 collective-permute-start.1
  19.5 0.0 collective-permute-done.2.refs_1_.refs_2_
  19.5 0.6 copy-done.2
  20.2 6.9 %attend_tiles.5 = bf16[512,128]{1,0:T(8,128)(2,1)} custom-call(s32[2]{0:T(128)} %pad_add_fusion.refs_0_.where_ref, bf16[528,128]{1,0:T(8,128)(2,1)} %copy-done.2, bf16[528,128]{1,0:T(8,128)(2,1)} %copy-done.2, bf16[2,2,1601,512]{3,2,1,0:T(8,128)(2,1)} %copy.9.refs_3_.refs_4_, bf16[2,2,1601,512]{3,2,1,0:T(8,128)(2,1)} %copy.9.refs_3_.refs_4_), custom_call_target="tpu_custom_call" | custom-call | tf_op jit(solution)/shard_map/attend_tiles/pallas_call | solution.py:119
  27.1 8.0 %collective-permute-start.3 = (bf16[512,128]{1,0:T(8,128)(2,1)}, bf16[512,128]{1,0:T(8,128)(2,1)S(1)}, u32[]{:S(2)}, u32[]{:S(2)}) collective-permute-start(bf16[512,128]{1,0:T(8,128)(2,1)} %attend_tiles.5), channel_id=1, source_target_pairs={{0,4},{4,0},{8,12},{12,8},{1,5},{5,1},{9,13},{13,9},{2,6},{6,2},{1... | collective-permute-start | bytes 393224 | tf_op jit(solution)/shard_map/ppermute | solution.py:248
  35.1 0.0 collective-permute-done.4.refs_1_.refs_2_
  35.1 0.6 copy-done.1
  35.8 6.9 %attend_tiles.6 = bf16[512,128]{1,0:T(8,128)(2,1)} custom-call(s32[2]{0:T(128)} %pad_add_fusion.refs_0_.where_ref, bf16[528,128]{1,0:T(8,128)(2,1)} %copy-done.1, bf16[528,128]{1,0:T(8,128)(2,1)} %copy-done.1, bf16[2,2,1601,512]{3,2,1,0:T(8,128)(2,1)} %copy.9.refs_3_.refs_4_, bf16[2,2,1601,512]{3,2,1,0:T(8,128)(2,1)} %copy.9.refs_3_.refs_4_), custom_call_target="tpu_custom_call" | custom-call | tf_op jit(solution)/shard_map/attend_tiles/pallas_call | solution.py:119
  42.6 0.0 collective-permute-start.5
  42.6 0.0 collective-permute-done.6.refs_1_.refs_2_
  42.7 0.6 copy-done
  43.3 6.9 %attend_tiles.7 = bf16[512,128]{1,0:T(8,128)(2,1)} custom-call(s32[2]{0:T(128)} %pad_add_fusion.refs_0_.where_ref, bf16[528,128]{1,0:T(8,128)(2,1)} %copy-done, bf16[528,128]{1,0:T(8,128)(2,1)} %copy-done, bf16[2,2,1601,512]{3,2,1,0:T(8,128)(2,1)} %copy.9.refs_3_.refs_4_, bf16[2,2,1601,512]{3,2,1,0:T(8,128)(2,1)} %copy.9.refs_3_.refs_4_), custom_call_target="tpu_custom_call" | custom-call | tf_op jit(solution)/shard_map/attend_tiles/pallas_call | solution.py:119
  50.2 2.4 %collective-permute-start.7 = (bf16[512,128]{1,0:T(8,128)(2,1)}, bf16[512,128]{1,0:T(8,128)(2,1)S(1)}, u32[]{:S(2)}, u32[]{:S(2)}) collective-permute-start(bf16[512,128]{1,0:T(8,128)(2,1)} %attend_tiles.7), channel_id=1, source_target_pairs={{0,12},{4,8},{8,4},{12,0},{1,13},{5,9},{9,5},{13,1},{2,14},{6,10},... | collective-permute-start | bytes 393224 | tf_op jit(solution)/shard_map/ppermute | solution.py:248
  52.6 7.0 %attend_tiles.4.refs_0_ = bf16[512,128]{1,0:T(8,128)(2,1)} custom-call(s32[2]{0:T(128)} %pad_add_fusion.refs_0_.where_ref, bf16[528,128]{1,0:T(8,128)(2,1)} %get-tuple-element.9.refs_1_.refs_2_, bf16[528,128]{1,0:T(8,128)(2,1)} %get-tuple-element.9.refs_1_.refs_2_, bf16[2,2,1601,512]{3,2,1,0:T(8,128)(2,1)} %copy.9.refs_3_.refs_4_, ...), custom_call_target="tpu_custom_call" | custom-call | tf_op jit(solution)/shard_map/attend_tiles/pallas_call | solution.py:119
  59.6 0.0 collective-permute-done.1.refs_3_
  59.6 0.0 copy-start.7
  59.6 0.6 copy-done.7
  60.2 7.0 %attend_self.1.self_ref = f32[128,2048]{1,0:T(8,128)} custom-call(s32[2]{0:T(128)} %pad_add_fusion.refs_0_.where_ref, s32[4]{0:T(128)} %refs_1_.1, bf16[128,2048]{1,0:T(8,128)(2,1)} %refs_2_.1, bf16[2,128,256]{2,1,0:T(8,128)(2,1)} %copy-done.7, bf16[2,128,256]{2,1,0:T(8,128)(2,1)} %copy-done.6, bf16[2,128,512]{2,1,0:T(8,128)(2,1)} %refs_5_.1), custom_call_target="tpu_custom_call" | custom-call | tf_op jit(solution)/shard_map/attend_self/pallas_call | solution.py:172
  67.2 0.0 collective-permute-done.3.refs_1_
  67.3 0.0 collective-permute-done.5.refs_2_
  67.3 0.7 broadcast_in_dim.3
  68.0 0.0 copy-done.5
  68.0 2.3 %mix.1 = bf16[128,2048]{1,0:T(8,128)(2,1)} custom-call(s32[2]{0:T(128)} %pad_add_fusion.refs_0_.where_ref, s32[4,4]{1,0:T(4,128)} %pairs_ref.3, s32[8]{0:T(128)} %slots_ref.3, f32[1,2048]{1,0:T(1,128)} %bitcast.3, f32[128,2048]{1,0:T(8,128)} %attend_self.1.self_ref, bf16[512,128]{1,0:T(8,128)(2,1)} %attend_tiles.4.refs_0_, bf16[512,128]{1,0:T(8,128)(2,1)} %copy-done.3, ...), custom_call_target="tpu_custom_call" | custom-call | tf_op jit(solution)/shard_map/mix/pallas_call | solution.py:205
  (14 shorter events, 0.0 us)
Async XLA Ops:
  2.7 16.8 %collective-permute-start.2 = (bf16[528,128]{1,0:T(8,128)(2,1)}, bf16[528,128]{1,0:T(8,128)(2,1)S(1)}, u32[]{:S(2)}, u32[]{:S(2)}) collective-permute-start(bf16[528,128]{1,0:T(8,128)(2,1)} %get-tuple-element.10), channel_id=1, source_target_pairs={{0,4},{4,0},{8,12},{12,8},{1,5},{5,1},{9,13},{13,9},{2,6},{6,2},{1... | collective-permute-start | bytes 405512 | tf_op jit(solution)/shard_map/ppermute | solution.py:248
  5.8 29.3 %collective-permute-start.4 = (bf16[528,128]{1,0:T(8,128)(2,1)}, bf16[528,128]{1,0:T(8,128)(2,1)S(1)}, u32[]{:S(2)}, u32[]{:S(2)}) collective-permute-start(bf16[528,128]{1,0:T(8,128)(2,1)} %get-tuple-element.11), channel_id=1, source_target_pairs={{0,8},{4,12},{8,0},{12,4},{1,9},{5,13},{9,1},{13,5},{2,10},{6,14},... | collective-permute-start | bytes 405512 | tf_op jit(solution)/shard_map/ppermute | solution.py:248
  8.4 34.3 %collective-permute-start.6 = (bf16[528,128]{1,0:T(8,128)(2,1)}, bf16[528,128]{1,0:T(8,128)(2,1)S(1)}, u32[]{:S(2)}, u32[]{:S(2)}) collective-permute-start(bf16[528,128]{1,0:T(8,128)(2,1)} %get-tuple-element.12), channel_id=1, source_target_pairs={{0,12},{4,8},{8,4},{12,0},{1,13},{5,9},{9,5},{13,1},{2,14},{6,10},... | collective-permute-start | bytes 405512 | tf_op jit(solution)/shard_map/ppermute | solution.py:248
  9.3 9.6 %collective-permute-start = (bf16[2,128,256]{2,1,0:T(8,128)(2,1)S(1)}, bf16[2,128,256]{2,1,0:T(8,128)(2,1)S(1)}, u32[]{:S(2)}, u32[]{:S(2)}) collective-permute-start(bf16[2,128,256]{2,1,0:T(8,128)(2,1)S(1)} %constant_dynamic-slice_fusion), channel_id=1, source_target_pairs={{0,4},{4,8},{8,12},{1,5},{5,9},{9,13},{2,6},{6,10},{10,14},{3,7},{... | collective-permute-start | bytes 393224 | tf_op jit(solution)/shard_map/ppermute | solution.py:253
  18.9 31.3 %copy-start.6 = (bf16[2,128,256]{2,1,0:T(8,128)(2,1)}, bf16[2,128,256]{2,1,0:T(8,128)(2,1)S(1)}, u32[]{:S(2)}) copy-start(bf16[2,128,256]{2,1,0:T(8,128)(2,1)S(1)} %collective-permute-done.refs_4_) | copy-start | bytes 393220
  18.9 40.7 %collective-permute-start.1 = (bf16[2,128,256]{2,1,0:T(8,128)(2,1)S(1)}, bf16[2,128,256]{2,1,0:T(8,128)(2,1)S(1)}, u32[]{:S(2)}, u32[]{:S(2)}) collective-permute-start(bf16[2,128,256]{2,1,0:T(8,128)(2,1)S(1)} %collective-permute-done.refs_4_), channel_id=1, source_target_pairs={{4,8},{8,12},{5,9},{9,13},{6,10},{10,14},{7,11},{11,15},{20,24},{2... | collective-permute-start | bytes 393224 | tf_op jit(solution)/shard_map/ppermute | solution.py:253
  19.5 0.7 copy-start.2
  27.1 40.2 %collective-permute-start.3 = (bf16[512,128]{1,0:T(8,128)(2,1)}, bf16[512,128]{1,0:T(8,128)(2,1)S(1)}, u32[]{:S(2)}, u32[]{:S(2)}) collective-permute-start(bf16[512,128]{1,0:T(8,128)(2,1)} %attend_tiles.5), channel_id=1, source_target_pairs={{0,4},{4,0},{8,12},{12,8},{1,5},{5,1},{9,13},{13,9},{2,6},{6,2},{1... | collective-permute-start | bytes 393224 | tf_op jit(solution)/shard_map/ppermute | solution.py:248
  35.1 0.6 copy-start.1
  42.6 24.6 %collective-permute-start.5 = (bf16[512,128]{1,0:T(8,128)(2,1)}, bf16[512,128]{1,0:T(8,128)(2,1)S(1)}, u32[]{:S(2)}, u32[]{:S(2)}) collective-permute-start(bf16[512,128]{1,0:T(8,128)(2,1)} %attend_tiles.6), channel_id=1, source_target_pairs={{0,8},{4,12},{8,0},{12,4},{1,9},{5,13},{9,1},{13,5},{2,10},{6,14},... | collective-permute-start | bytes 393224 | tf_op jit(solution)/shard_map/ppermute | solution.py:248
  42.6 0.7 copy-start
  50.2 17.1 %collective-permute-start.7 = (bf16[512,128]{1,0:T(8,128)(2,1)}, bf16[512,128]{1,0:T(8,128)(2,1)S(1)}, u32[]{:S(2)}, u32[]{:S(2)}) collective-permute-start(bf16[512,128]{1,0:T(8,128)(2,1)} %attend_tiles.7), channel_id=1, source_target_pairs={{0,12},{4,8},{8,4},{12,0},{1,13},{5,9},{9,5},{13,1},{2,14},{6,10},... | collective-permute-start | bytes 393224 | tf_op jit(solution)/shard_map/ppermute | solution.py:248
  52.6 7.0 %copy-start.8 = (f32[16]{0:T(128)S(1)}, f32[16]{0:T(128)}, u32[]{:S(2)}) copy-start(f32[16]{0:T(128)} %param.12) | copy-start | bytes 196
  59.6 0.7 copy-start.7
  67.2 0.7 %copy-start.3 = (bf16[512,128]{1,0:T(8,128)(2,1)}, bf16[512,128]{1,0:T(8,128)(2,1)S(1)}, u32[]{:S(2)}) copy-start(bf16[512,128]{1,0:T(8,128)(2,1)S(1)} %collective-permute-done.3.refs_1_) | copy-start | bytes 393220
  67.3 0.7 %copy-start.4 = (bf16[512,128]{1,0:T(8,128)(2,1)}, bf16[512,128]{1,0:T(8,128)(2,1)S(1)}, u32[]{:S(2)}) copy-start(bf16[512,128]{1,0:T(8,128)(2,1)S(1)} %collective-permute-done.5.refs_2_) | copy-start | bytes 393220
  67.3 0.7 %copy-start.5 = (bf16[512,128]{1,0:T(8,128)(2,1)}, bf16[512,128]{1,0:T(8,128)(2,1)S(1)}, u32[]{:S(2)}) copy-start(bf16[512,128]{1,0:T(8,128)(2,1)S(1)} %collective-permute-done.7.refs_3_) | copy-start | bytes 393220

commit v2 on v1

v2 whole, which is shorter than its diff:
```python
import functools
import math

import jax
import jax.numpy as jnp
from jax import lax
from jax.experimental import pallas as pl
from jax.experimental.pallas import tpu as pltpu
from jax.sharding import PartitionSpec as P

HEAD_DIM = 128
Q_HEADS = 64
KV_HEADS = 8
BLOCK = 32
PAIRS = 4

NEG_FILL = -1e30
META_ROWS = 16
KEY_CHUNK = 256
LOG2E = math.log2(math.e)
EXP2_SCALE = HEAD_DIM ** (-0.5) * LOG2E

SMEM = pl.BlockSpec(memory_space=pltpu.SMEM)
VMEM = pl.BlockSpec(memory_space=pltpu.VMEM)
ANY = pl.BlockSpec(memory_space=pl.ANY)
PARAMS = pltpu.CompilerParams(vmem_limit_bytes=24 << 20)


def in_vmem(array):
    return pltpu.with_memory_space_constraint(array, pltpu.VMEM)


def owner_slots(pairs_ref, slots_ref):
    blocks, pairs = pairs_ref.shape
    return [[slots_ref[pairs_ref[b, p]] for p in range(pairs)] for b in range(blocks)]


def block_for(stored, owner, tiles_dev):
    block = jnp.int32(0)
    counts = [jnp.int32(0)] * tiles_dev
    for b, row in enumerate(stored):
        for slot in row:
            tile = slot - owner * tiles_dev
            block = jnp.where((tile >= 0) & (tile < tiles_dev), jnp.int32(b), block)
            counts = [n + (tile == i).astype(jnp.int32) for i, n in enumerate(counts)]
    return block, counts


def owner_at(where_ref, distance, ctx_count):
    return lax.rem(where_ref[0] + distance, ctx_count)


def pack_body(where_ref, pairs_ref, slots_ref, q_ref, kv_hbm, *refs, tiles_dev, kv_used):
    out_refs, sem = refs[:-1], refs[-1]
    ctx_count = len(out_refs)
    heads = q_ref.shape[1] // HEAD_DIM
    tok_rows = kv_hbm.shape[1]
    kv_at = heads * BLOCK + META_ROWS
    copies = []
    for w in range(2):
        for k in range(kv_used):
            cols = pl.ds(pl.multiple_of((where_ref[1] + k) * HEAD_DIM, HEAD_DIM), HEAD_DIM)
            part = w * kv_used + k
            rows = pl.ds(kv_at + part * tok_rows, tok_rows)
            copies.append(
                pltpu.make_async_copy(kv_hbm.at[w, :, cols], out_refs[1].at[rows, :], sem.at[part])
            )
    for copy in copies:
        copy.start()
    stored = owner_slots(pairs_ref, slots_ref)
    lanes = lax.broadcasted_iota(jnp.int32, (META_ROWS, HEAD_DIM), 1)
    for distance, out_ref in enumerate(out_refs):
        block, counts = block_for(stored, owner_at(where_ref, distance, ctx_count), tiles_dev)
        rows = pl.ds(pl.multiple_of(block * BLOCK, BLOCK), BLOCK)
        for h in range(heads):
            out_ref[h * BLOCK : (h + 1) * BLOCK, :] = q_ref[rows, h * HEAD_DIM : (h + 1) * HEAD_DIM]
        meta = jnp.zeros((META_ROWS, HEAD_DIM), jnp.float32)
        for i, n in enumerate(counts):
            meta = jnp.where(lanes % tiles_dev == i, n.astype(jnp.float32), meta)
        out_ref[heads * BLOCK : kv_at, :] = meta.astype(jnp.bfloat16)
    for copy in copies:
        copy.wait()


def pack_queries(where, pair_tiles, tile_slot, q_cross, kv_self, ctx_count, tiles_dev, kv_used):
    rows = q_cross.shape[1] // HEAD_DIM * BLOCK + META_ROWS
    kv_rows = 2 * kv_used * kv_self.shape[1]
    return pl.pallas_call(
        functools.partial(pack_body, tiles_dev=tiles_dev, kv_used=kv_used),
        out_shape=[
            pltpu.VMEM((rows + (kv_rows if d == 1 else 0), HEAD_DIM), jnp.bfloat16)
            for d in range(ctx_count)
        ],
        in_specs=[SMEM, SMEM, SMEM, VMEM, ANY],
        out_specs=[VMEM] * ctx_count,
        scratch_shapes=[pltpu.SemaphoreType.DMA((2 * kv_used,))],
        compiler_params=PARAMS,
        name="pack_queries",
    )(where, pair_tiles, tile_slot, q_cross, kv_self)


def attend_head(q, meta, keys, values, key_count, scores_sc):
    rows = q.shape[0]
    padded = keys.shape[0]
    lanes = HEAD_DIM
    count = meta[0:1, :].astype(jnp.float32)
    bias = jnp.where(count > 0, jnp.log(jnp.maximum(count, 1.0)) * LOG2E, NEG_FILL)
    best = None
    for at in range(0, padded, KEY_CHUNK):
        size = min(KEY_CHUNK, padded - at)
        scores = lax.dot_general(
            q, keys[at : at + size, :], (((1,), (1,)), ((), ())), preferred_element_type=jnp.float32
        )
        for col in range(0, size, lanes):
            width = min(lanes, size - col)
            piece = scores[:, col : col + width]
            valid = key_count - at - col
            if width > valid:
                piece = jnp.where(lax.broadcasted_iota(jnp.int32, piece.shape, 1) < valid, piece, NEG_FILL)
            scores_sc[:, at + col : at + col + width] = piece
            if width == lanes:
                best = piece if best is None else jnp.maximum(best, piece)
            else:
                tail = piece
    best = jnp.max(best * EXP2_SCALE + bias, axis=1, keepdims=True)
    tail_width = padded % lanes
    if tail_width:
        tail = jnp.max(tail * EXP2_SCALE + bias[:, :tail_width], axis=1, keepdims=True)
        best = jnp.maximum(best, tail)
    shift = jnp.where(best > 0.5 * NEG_FILL, bias - best, NEG_FILL)
    totals = jnp.zeros((rows, lanes), jnp.float32)
    total = jnp.zeros((rows, 1), jnp.float32)
    blended = jnp.zeros((rows, HEAD_DIM), jnp.float32)
    for at in range(0, padded, KEY_CHUNK):
        size = min(KEY_CHUNK, padded - at)
        pieces = []
        for col in range(0, size, lanes):
            width = min(lanes, size - col)
            piece = scores_sc[:, at + col : at + col + width]
            weights = jnp.exp2(piece * EXP2_SCALE + shift[:, :width])
            if width == lanes:
                totals = totals + weights
            else:
                total = total + jnp.sum(weights, axis=1, keepdims=True)
            pieces.append(weights.astype(jnp.bfloat16))
        weights = jnp.concatenate(pieces, axis=1) if len(pieces) > 1 else pieces[0]
        blended = blended + jnp.dot(
            weights, values[at : at + size, :], preferred_element_type=jnp.float32
        )
    total = total + jnp.sum(totals, axis=1, keepdims=True)
    live = total > 0
    total = jnp.where(live, total, 1.0)
    out = (blended / total).astype(jnp.bfloat16)
    lse = jnp.where(live, best * (1.0 / LOG2E) + jnp.log(total), NEG_FILL)
    return out, jnp.broadcast_to(lse, (rows, lanes))


def attend_block(q_ref, keys_ref, values_ref, out_ref, lse_ref, scores_sc, key_count, wait):
    kv_used, padded_len, tiles_dev, _ = keys_ref.shape
    padded = padded_len * tiles_dev
    q_rows = scores_sc.shape[0] * kv_used
    rows = scores_sc.shape[0]
    meta = q_ref[q_rows : q_rows + META_ROWS, :]
    for k in range(kv_used):
        wait(k)
        own = slice(k * rows, (k + 1) * rows)
        keys = keys_ref.at[k].reshape(padded, HEAD_DIM)
        values = values_ref.at[k].reshape(padded, HEAD_DIM)
        out, lse = attend_head(q_ref[own, :], meta, keys, values, key_count, scores_sc)
        out_ref[own, :] = out
        if lse_ref is not None:
            lse_ref[own, :] = lse


def own_body(where_ref, q_ref, image_hbm, *refs, with_lse):
    out_ref = refs[0]
    lse_ref = refs[1] if with_lse else None
    keys_ref, values_ref, scores_sc, sem = refs[-4:]
    tile_len, tiles_dev = image_hbm.shape[1:3]
    kv_used, padded_len = keys_ref.shape[:2]

    def copies(k):
        cols = pl.ds(pl.multiple_of((where_ref[1] + k) * HEAD_DIM, HEAD_DIM), HEAD_DIM)
        held = pl.ds(0, tile_len)
        return [
            pltpu.make_async_copy(image_hbm.at[w, :, :, cols], ref.at[k, held], sem.at[w, k])
            for w, ref in enumerate((keys_ref, values_ref))
        ]

    for k in range(kv_used):
        for copy in copies(k):
            copy.start()
    pad = jnp.zeros((padded_len - tile_len, tiles_dev, HEAD_DIM), jnp.bfloat16)
    for k in range(kv_used):
        keys_ref[k, tile_len:] = pad
        values_ref[k, tile_len:] = pad

    def wait(k):
        for copy in copies(k):
            copy.wait()

    attend_block(
        q_ref, keys_ref, values_ref, out_ref, lse_ref, scores_sc, tile_len * tiles_dev, wait
    )


def attend_own(where, packed, image_kv, kv_used, q_rows, with_lse):
    _, tile_len, tiles_dev, _ = image_kv.shape
    held = pltpu.VMEM((kv_used, -(-tile_len // 8) * 8, tiles_dev, HEAD_DIM), jnp.bfloat16)
    out_shape = [pltpu.VMEM((q_rows, HEAD_DIM), jnp.bfloat16)]
    if with_lse:
        out_shape.append(pltpu.VMEM((q_rows, HEAD_DIM), jnp.float32))
    out_shape += [held, held]
    padded = held.shape[1] * tiles_dev
    results = pl.pallas_call(
        functools.partial(own_body, with_lse=with_lse),
        out_shape=out_shape,
        in_specs=[SMEM, VMEM, ANY],
        out_specs=[VMEM] * len(out_shape),
        scratch_shapes=[
            pltpu.VMEM((q_rows // kv_used, padded), jnp.float32),
            pltpu.SemaphoreType.DMA((2, kv_used)),
        ],
        compiler_params=PARAMS,
        name="attend_own",
    )(where, in_vmem(packed), image_kv)
    return results[:-2], [in_vmem(part) for part in results[-2:]]


def arrived_body(q_ref, keys_ref, values_ref, *refs, with_lse, riders, key_count, q_rows):
    rider_refs, refs = refs[: len(riders)], refs[len(riders) :]
    out_ref, scores_sc = refs[0], refs[-1]
    lse_ref = refs[1] if with_lse else None
    for ref, at in zip(rider_refs, riders):
        out_ref[q_rows:, :] = ref[at:, :]
    attend_block(
        q_ref, keys_ref, values_ref, out_ref, lse_ref, scores_sc, key_count, lambda k: None
    )


def attend_arrived(packed, held, key_count, q_rows, with_lse, rider=None):
    kv_used, padded_len, tiles_dev, _ = held[0].shape
    at = q_rows + META_ROWS
    riders = [] if rider is None else [rider]
    extra = 0 if rider is None else rider.shape[0] - at
    out_shape = [pltpu.VMEM((q_rows + extra, HEAD_DIM), jnp.bfloat16)]
    if with_lse:
        out_shape.append(pltpu.VMEM((q_rows, HEAD_DIM), jnp.float32))
    return pl.pallas_call(
        functools.partial(
            arrived_body,
            with_lse=with_lse,
            riders=[at] * len(riders),
            key_count=key_count,
            q_rows=q_rows,
        ),
        out_shape=out_shape,
        in_specs=[VMEM] * (3 + len(riders)),
        out_specs=[VMEM] * len(out_shape),
        scratch_shapes=[pltpu.VMEM((q_rows // kv_used, padded_len * tiles_dev), jnp.float32)],
        compiler_params=PARAMS,
        name="attend_arrived",
    )(in_vmem(packed), *held, *riders)


def self_body(where_ref, docs_ref, q_ref, *refs, starts, kv_used):
    kv_refs, out_ref, bias_sc = refs[:-2], refs[-2], refs[-1]
    tok_rows, q_width = q_ref.shape
    per_kv = q_width // HEAD_DIM // kv_used
    shape = bias_sc.shape
    row_start = where_ref[0] * tok_rows
    query_pos = row_start + lax.broadcasted_iota(jnp.int32, (tok_rows, 1), 0)
    key_pos = row_start + tok_rows - shape[1] + lax.broadcasted_iota(jnp.int32, shape, 1)
    doc_start = jnp.zeros((tok_rows, 1), jnp.int32)
    doc_end = jnp.int32(0)
    for j in range(docs_ref.shape[0]):
        doc_end = doc_end + docs_ref[j]
        doc_start = jnp.where(query_pos >= doc_end, doc_end, doc_start)
    bias_sc[...] = jnp.where((key_pos <= query_pos) & (key_pos >= doc_start), 0.0, NEG_FILL)
    for k in range(kv_used):
        keys, values = [
            jnp.concatenate(
                [
                    ref[at + (w * kv_used + k) * tok_rows : at + (w * kv_used + k + 1) * tok_rows, :]
                    for ref, at in zip(kv_refs, starts)
                ],
                axis=0,
            )
            for w in range(2)
        ]
        heads = range(k * per_kv, (k + 1) * per_kv)
        q = jnp.concatenate([q_ref[:, h * HEAD_DIM : (h + 1) * HEAD_DIM] for h in heads], axis=0)
        scores = lax.dot_general(
            q, keys, (((1,), (1,)), ((), ())), preferred_element_type=jnp.float32
        )
        scores = scores * EXP2_SCALE + jnp.concatenate([bias_sc[...]] * per_kv, axis=0)
        row_best = jnp.max(scores, axis=1, keepdims=True)
        weights = jnp.exp2(scores - row_best)
        row_total = jnp.sum(weights, axis=1, keepdims=True)
        blended = jnp.dot(weights.astype(jnp.bfloat16), values, preferred_element_type=jnp.float32)
        blended = blended / row_total
        for i, h in enumerate(heads):
            out_ref[:, h * HEAD_DIM : (h + 1) * HEAD_DIM] = blended[i * tok_rows : (i + 1) * tok_rows]


def attend_self(where, doc_lengths, q_self, pieces, kv_used):
    tok_rows, q_width = q_self.shape
    return pl.pallas_call(
        functools.partial(self_body, starts=[at for _, at in pieces], kv_used=kv_used),
        out_shape=pltpu.VMEM((tok_rows, q_width), jnp.float32),
        in_specs=[SMEM, SMEM] + [VMEM] * (1 + len(pieces)),
        out_specs=VMEM,
        scratch_shapes=[pltpu.VMEM((tok_rows, len(pieces) * tok_rows), jnp.float32)],
        compiler_params=PARAMS,
        name="attend_self",
    )(where, doc_lengths, in_vmem(q_self), *[in_vmem(array) for array, _ in pieces])


def mix_body(where_ref, pairs_ref, slots_ref, gate_ref, self_ref, *refs, tiles_dev):
    partial_refs, out_ref = refs[:-1], refs[-1]
    stored = owner_slots(pairs_ref, slots_ref)
    for distance, partial_ref in enumerate(partial_refs):
        owner = owner_at(where_ref, distance, len(partial_refs))
        block, _ = block_for(stored, owner, tiles_dev)
        rows = pl.ds(pl.multiple_of(block * BLOCK, BLOCK), BLOCK)
        for h in range(self_ref.shape[1] // HEAD_DIM):
            cols = slice(h * HEAD_DIM, (h + 1) * HEAD_DIM)
            cross = partial_ref[h * BLOCK : (h + 1) * BLOCK, :].astype(jnp.float32)
            mixed = self_ref[rows, cols] + gate_ref[:, cols] * cross
            out_ref[rows, cols] = mixed.astype(jnp.bfloat16)


def mix(where, pair_tiles, tile_slot, gate_cols, self_out, partials, tiles_dev):
    return pl.pallas_call(
        functools.partial(mix_body, tiles_dev=tiles_dev),
        out_shape=jax.ShapeDtypeStruct(self_out.shape, jnp.bfloat16),
        in_specs=[SMEM] * 3 + [VMEM] * (2 + len(partials)),
        out_specs=VMEM,
        compiler_params=PARAMS,
        name="mix",
    )(
        where,
        pair_tiles,
        tile_slot,
        gate_cols,
        in_vmem(self_out),
        *[in_vmem(partial) for partial in partials],
    )


def mix_owners(where, pair_tiles, tile_slot, gate_cols, self_out, partials, sums, tiles_dev):
    block_count = pair_tiles.shape[0]
    tok_rows, q_width = self_out.shape
    heads = q_width // HEAD_DIM
    ctx_count = len(partials)
    owners = jnp.take(tile_slot, pair_tiles.reshape(-1), axis=0).reshape(block_count, -1) // tiles_dev
    partners = (where[0] + jnp.arange(ctx_count, dtype=jnp.int32)) % ctx_count
    live = jnp.any(owners[:, :, None] == partners[None, None, :], axis=1)[:, :, None, None]
    lse = jnp.stack(sums)[None]
    top = jnp.max(jnp.where(live, lse, NEG_FILL), axis=1, keepdims=True)
    factors = jnp.where(live, jnp.exp(lse - top), 0.0)
    pieces = jnp.stack(partials).astype(jnp.float32)[None]
    cross = jnp.sum(factors * pieces, axis=1) / jnp.sum(factors, axis=1)
    cross = jnp.transpose(cross.reshape(block_count, heads, BLOCK, HEAD_DIM), (0, 2, 1, 3))
    return (self_out + gate_cols * cross.reshape(tok_rows, q_width)).astype(jnp.bfloat16)


def local(q_self, q_cross, kv_self, image_kv, cross_gate, doc_lengths, pair_tiles, tile_slot):
    tok_rows, q_width = q_self.shape
    local_heads = q_width // HEAD_DIM
    q_rows = local_heads * BLOCK
    grouping = Q_HEADS // KV_HEADS
    per_kv = min(local_heads, grouping)
    kv_used = local_heads // per_kv
    ctx_count = lax.axis_size("ctx")
    tiles_dev, tile_len = image_kv.shape[1:3]
    request_count = pair_tiles.shape[0] * PAIRS
    capacity = max(2, -(-request_count // ctx_count))
    one_owner = ctx_count * capacity == request_count and capacity == PAIRS
    with_lse = not one_owner
    reach = min(ctx_count - 1, -(-(ctx_count * tok_rows // 2 - 1) // tok_rows))

    here = lax.axis_index("ctx").astype(jnp.int32)
    kv_first = (lax.axis_index("rep") * local_heads // grouping).astype(jnp.int32)
    where = jnp.stack([here, kv_first])
    image_kv = jnp.transpose(image_kv, (0, 2, 1, 3))

    def send(array, distance):
        pairs = [(i, (i + distance) % ctx_count) for i in range(ctx_count)]
        return lax.ppermute(array, "ctx", pairs)

    packed = pack_queries(
        where, pair_tiles, tile_slot, q_cross, kv_self, ctx_count, tiles_dev, kv_used
    )
    last = ctx_count - 1
    order = [last] + list(range(last - 1, 0, -1))
    arrived = {d: send(packed[d], d) for d in [1] + order[:-1]}
    results = {}
    results[0], held = attend_own(where, packed[0], image_kv, kv_used, q_rows, with_lse)
    for d in order:
        rider = in_vmem(arrived[1]) if d == last else None
        answer = attend_arrived(
            arrived[d], held, tile_len * tiles_dev, q_rows, with_lse, rider
        )
        results[d] = [send(part, ctx_count - d) for part in answer]

    at = q_rows + META_ROWS
    pieces = [(packed[1], at), (arrived[1], at), (results[last][0], q_rows)][: reach + 1]
    for _ in range(len(pieces), reach + 1):
        array, first = pieces[-1]
        pieces.append((send(array[first:], 1), 0))
    self_out = attend_self(where, doc_lengths, q_self, pieces[::-1], kv_used)
    gate_cols = jnp.repeat(jnp.tanh(cross_gate), HEAD_DIM)[None, :]
    partials = [results[d][0] for d in range(ctx_count)]
    if one_owner:
        return mix(where, pair_tiles, tile_slot, gate_cols, self_out, partials, tiles_dev)
    partials = [partial[:q_rows] for partial in partials]
    sums = [results[d][1] for d in range(ctx_count)]
    return mix_owners(where, pair_tiles, tile_slot, gate_cols, self_out, partials, sums, tiles_dev)


def solution(mesh):
    in_specs = (
        P(("groups", "ctx"), ("head", "rep")),
        P(("groups", "ctx"), ("head", "rep")),
        P(None, ("groups", "ctx"), "head"),
        P(None, ("groups", "ctx"), None, "head"),
        P(("head", "rep")),
        P("groups"),
        P(("groups", "ctx"), None),
        P("groups"),
    )
    out_specs = P(("groups", "ctx"), ("head", "rep"))
    return jax.shard_map(local, mesh=mesh, in_specs=in_specs, out_specs=out_specs, check_vma=False)
```

time: 70.9 us -> 42.8 us (0.60)
  Pallas kernels: 39.1 us -> 22.7 us
  starting transfers between devices: 19.5 us -> 12.6 us
  local copies, waits for them, and re-layouts: 11 us -> 6.29 us
    pallas_call x6, Pallas kernels: 36.8 us -> 21.2 us  [the longest x3 11.5 us: attend_arrived(): pl.pallas_call(functools.partial(arrived_body, with_lse=with_lse, riders=...]
    ppermute x8 -> x6, starting transfers between devices: 19.5 us -> 12.6 us  [send(): return lax.ppermute(array, 'ctx', pairs)]
    unnamed x19 -> x20, local copies, waits for them, and re-layouts: 9.39 us -> 6.22 us
    dynamic_slice x1 -> x0, local copies, waits for them, and re-layouts: 0.91 us -> none  [local(): lax.dynamic_slice_in_dim(kv_self, kv_first * HEAD_DIM, kv_used * HEAD_DIM...]
    pallas_call x1, Pallas kernels: 2.32 us -> 1.54 us  [mix(): pl.pallas_call(functools.partial(mix_body, tiles_dev=tiles_dev), out_shap...]
  transfers between devices with their start and end apart: 8 -> 6, of which waited for: 0 -> 1; matrix products, arithmetic and copies ran while one was open for 11% -> 0% of each run, Pallas kernels for 49% -> 47%
where the time goes in v2:
time: 42.8 us; the launch traced here: 42.6 us
  Pallas kernels  22.7 us (53%)
  starting transfers between devices  12.6 us (29%)
  local copies, waits for them, and re-layouts  6.29 us (15%)
  waiting for transfers between devices  0.72 us (2%)
    ppermute x6, starting transfers between devices, send(): return lax.ppermute(array, 'ctx', pairs)  12.6 us
    pallas_call x3, Pallas kernels, attend_arrived(): pl.pallas_call(functools.partial(arrived_body, with_lse=with_lse, riders=...  11.5 us
    pallas_call x1, Pallas kernels, attend_own(): pl.pallas_call(functools.partial(own_body, with_lse=with_lse), out_shape=...  6.91 us
    unnamed x20, local copies, waits for them, and re-layouts  6.22 us
    pallas_call x1, Pallas kernels, attend_self(): pl.pallas_call(functools.partial(self_body, starts=[at for _, at in piece...  1.77 us
    pallas_call x1, Pallas kernels, mix(): pl.pallas_call(functools.partial(mix_body, tiles_dev=tiles_dev), out_shap...  1.54 us
    pallas_call x1, Pallas kernels, pack_queries(): pl.pallas_call(functools.partial(pack_body, tiles_dev=tiles_dev, kv_used=...  0.98 us
  transfers between devices with their start and end apart: 6, of which 1 were waited for; matrix products, arithmetic and copies ran while one was open for 0% of the time, Pallas kernels for 47%

profile of v2, /device:TPU:0, one launch (start us, length us, event | category | flops | bytes accessed | tf_op | source)
XLA Modules:
  0.0 42.6 jit_solution(7433730163459058822)
XLA Ops:
  0.0 0.1 pad_add_fusion.where_ref
  0.1 1.0 %copy-done.1 = bf16[128,2048]{1,0:T(8,128)(2,1)S(1)} copy-done((bf16[128,2048]{1,0:T(8,128)(2,1)S(1)}, bf16[128,2048]{1,0:T(8,128)(2,1)}, u32[]{:S(2)}) %copy-start.1) | copy-done | bytes 524312
  1.1 0.9 %copy-done.3 = bf16[2,128,512]{2,1,0:T(8,128)(2,1)S(1)} copy-done((bf16[2,128,512]{2,1,0:T(8,128)(2,1)S(1)}, bf16[2,128,512]{2,1,0:T(8,128)(2,1)}, u32[]{:S(2)}) %copy-start.3) | copy-done | bytes 262168
  2.1 0.7 %copy-done.4 = s32[4,4]{1,0:T(4,128)S(1)} copy-done((s32[4,4]{1,0:T(4,128)S(1)}, s32[4,4]{1,0:T(4,128)}, u32[]{:S(2)}) %copy-start.4) | copy-done | bytes 88
  2.8 0.7 %copy-done.6 = s32[8]{0:T(128)S(1)} copy-done((s32[8]{0:T(128)S(1)}, s32[8]{0:T(128)}, u32[]{:S(2)}) %copy-start.6) | copy-done | bytes 56
  3.4 1.0 %pack_queries.1 = (bf16[528,128]{1,0:T(8,128)(2,1)S(1)}, bf16[1040,128]{1,0:T(8,128)(2,1)S(1)}, bf16[528,128]{1,0:T(8,128)(2,1)S(1)}, bf16[528,128]{1,0:T(8,128)(2,1)S(1)}) custom-call(s32[2]{0:T(128)S(1)} %pad_add_fusion.where_ref, s32[4,4]{1,0:T(4,128)S(1)} %copy-done.4, s32[8]{0:T(128)S(1)} %copy-done.6, bf16[128,2048]{1,0:T(8,128)(2,1)S(1)} %copy-done.1, ...), custom_call_target="tpu_custom_call" | custom-call | tf_op jit(solution)/shard_map/pack_queries/pallas_call | solution.py:88
  4.4 3.1 %collective-permute-start.1 = (bf16[1040,128]{1,0:T(8,128)(2,1)S(1)}, bf16[1040,128]{1,0:T(8,128)(2,1)S(1)}, u32[]{:S(2)}, u32[]{:S(2)}) collective-permute-start(bf16[1040,128]{1,0:T(8,128)(2,1)S(1)} %get-tuple-element.16.refs_2_), channel_id=1, source_target_pairs={{0,4},{4,8},{8,12},{12,0},{1,5},{5,9},{9,13},{13,1},{2,6},{6,10},{... | collective-permute-start | bytes 798728 | tf_op jit(solution)/shard_map/ppermute | solution.py:390
  7.5 2.1 %collective-permute-start = (bf16[528,128]{1,0:T(8,128)(2,1)S(1)}, bf16[528,128]{1,0:T(8,128)(2,1)S(1)}, u32[]{:S(2)}, u32[]{:S(2)}) collective-permute-start(bf16[528,128]{1,0:T(8,128)(2,1)S(1)} %get-tuple-element.12), channel_id=1, source_target_pairs={{0,12},{4,0},{8,4},{12,8},{1,13},{5,1},{9,5},{13,9},{2,14},{6,2},{... | collective-permute-start | bytes 405512 | tf_op jit(solution)/shard_map/ppermute | solution.py:390
  9.6 0.9 %collective-permute-start.4 = (bf16[528,128]{1,0:T(8,128)(2,1)S(1)}, bf16[528,128]{1,0:T(8,128)(2,1)S(1)}, u32[]{:S(2)}, u32[]{:S(2)}) collective-permute-start(bf16[528,128]{1,0:T(8,128)(2,1)S(1)} %get-tuple-element.18), channel_id=1, source_target_pairs={{0,8},{4,12},{8,0},{12,4},{1,9},{5,13},{9,1},{13,5},{2,10},{6,14},... | collective-permute-start | bytes 405512 | tf_op jit(solution)/shard_map/ppermute | solution.py:390
  10.5 2.9 %copy-done = bf16[2,2,1601,512]{3,1,2,0:T(2,128)(2,1)S(1)} copy-done((bf16[2,2,1601,512]{3,1,2,0:T(2,128)(2,1)S(1)}, bf16[2,2,1601,512]{3,1,2,0:T(2,128)(2,1)}, u32[]{:S(2)}) %copy-start) | copy-done | bytes 6557720
  13.4 6.9 %attend_own.1 = (bf16[512,128]{1,0:T(8,128)(2,1)S(1)}, bf16[2,1608,2,128]{3,2,1,0:T(2,128)(2,1)S(1)}, bf16[2,1608,2,128]{3,2,1,0:T(2,128)(2,1)S(1)}) custom-call(s32[2]{0:T(128)S(1)} %pad_add_fusion.where_ref, bf16[528,128]{1,0:T(8,128)(2,1)S(1)} %get-tuple-element.13.q_ref, bf16[2,1601,2,512]{3,2,1,0:T(2,128)(2,1)S(1)} %bitcast.4), custom_call_target="tpu_custom_call" | custom-call | tf_op jit(solution)/shard_map/attend_own/pallas_call | solution.py:215
  20.3 0.0 collective-permute-done.q_ref
  20.3 0.0 collective-permute-done.1.refs_0_.refs_1_.q_ref
  20.3 3.8 %attend_arrived.3 = bf16[1024,128]{1,0:T(8,128)(2,1)S(1)} custom-call(bf16[528,128]{1,0:T(8,128)(2,1)S(1)} %collective-permute-done.q_ref, bf16[2,1608,2,128]{3,2,1,0:T(2,128)(2,1)S(1)} %get-tuple-element.14.keys_ref, bf16[2,1608,2,128]{3,2,1,0:T(2,128)(2,1)S(1)} %get-tuple-element.15.values_ref, ...), custom_call_target="tpu_custom_call" | custom-call | tf_op jit(solution)/shard_map/attend_arrived/pallas_call | solution.py:249
  24.2 1.8 %collective-permute-start.2 = (bf16[1024,128]{1,0:T(8,128)(2,1)S(1)}, bf16[1024,128]{1,0:T(8,128)(2,1)S(1)}, u32[]{:S(2)}, u32[]{:S(2)}) collective-permute-start(bf16[1024,128]{1,0:T(8,128)(2,1)S(1)} %attend_arrived.3), channel_id=1, source_target_pairs={{0,4},{4,8},{8,12},{12,0},{1,5},{5,9},{9,13},{13,1},{2,6},{6,10},{... | collective-permute-start | bytes 786440 | tf_op jit(solution)/shard_map/ppermute | solution.py:390
  26.0 0.0 collective-permute-done.4.q_ref
  26.0 3.8 %attend_arrived.5 = bf16[512,128]{1,0:T(8,128)(2,1)S(1)} custom-call(bf16[528,128]{1,0:T(8,128)(2,1)S(1)} %collective-permute-done.4.q_ref, bf16[2,1608,2,128]{3,2,1,0:T(2,128)(2,1)S(1)} %get-tuple-element.14.keys_ref, bf16[2,1608,2,128]{3,2,1,0:T(2,128)(2,1)S(1)} %get-tuple-element.15.values_ref), custom_call_target="tpu_custom_call" | custom-call | tf_op jit(solution)/shard_map/attend_arrived/pallas_call | solution.py:249
  29.8 0.0 copy-start.9
  29.9 0.0 copy-start.2
  29.9 0.0 copy-start.8
  29.9 1.8 %collective-permute-start.5 = (bf16[512,128]{1,0:T(8,128)(2,1)S(1)}, bf16[512,128]{1,0:T(8,128)(2,1)S(1)}, u32[]{:S(2)}, u32[]{:S(2)}) collective-permute-start(bf16[512,128]{1,0:T(8,128)(2,1)S(1)} %attend_arrived.5), channel_id=1, source_target_pairs={{0,8},{4,12},{8,0},{12,4},{1,9},{5,13},{9,1},{13,5},{2,10},{6,14},... | collective-permute-start | bytes 393224 | tf_op jit(solution)/shard_map/ppermute | solution.py:390
  31.6 3.8 %attend_arrived.4 = bf16[512,128]{1,0:T(8,128)(2,1)S(1)} custom-call(bf16[1040,128]{1,0:T(8,128)(2,1)S(1)} %collective-permute-done.1.refs_0_.refs_1_.q_ref, bf16[2,1608,2,128]{3,2,1,0:T(2,128)(2,1)S(1)} %get-tuple-element.14.keys_ref, bf16[2,1608,2,128]{3,2,1,0:T(2,128)(2,1)S(1)} %get-tuple-element.15.values_ref), custom_call_target="tpu_custom_call" | custom-call | tf_op jit(solution)/shard_map/attend_arrived/pallas_call | solution.py:249
  35.5 0.0 copy-start.5
  35.5 0.0 copy-start.7
  35.5 2.9 %collective-permute-start.3 = (bf16[512,128]{1,0:T(8,128)(2,1)S(1)}, bf16[512,128]{1,0:T(8,128)(2,1)S(1)}, u32[]{:S(2)}, u32[]{:S(2)}) collective-permute-start(bf16[512,128]{1,0:T(8,128)(2,1)S(1)} %attend_arrived.4), channel_id=1, source_target_pairs={{0,12},{4,0},{8,4},{12,8},{1,13},{5,1},{9,5},{13,9},{2,14},{6,2},{... | collective-permute-start | bytes 393224 | tf_op jit(solution)/shard_map/ppermute | solution.py:390
  38.4 0.0 copy-done.9
  38.4 0.0 collective-permute-done.2.refs_0_.refs_3_
  38.5 1.8 %attend_self.1.self_ref = f32[128,2048]{1,0:T(8,128)S(1)} custom-call(s32[2]{0:T(128)S(1)} %pad_add_fusion.where_ref, s32[4]{0:T(128)S(1)} %copy-done.8, bf16[128,2048]{1,0:T(8,128)(2,1)S(1)} %copy-done.2, bf16[1024,128]{1,0:T(8,128)(2,1)S(1)} %collective-permute-done.2.refs_0_.refs_3_, bf16[1040,128]{1,0:T(8,128)(2,1)S(1)} %collective-permute-done.1.refs_0_.refs_1_.q_ref, ...), custom_call_target="tpu_custom_call" | custom-call | tf_op jit(solution)/shard_map/attend_self/pallas_call | solution.py:308
  40.2 0.0 collective-permute-done.5.refs_2_
  40.2 0.7 %collective-permute-done.3.refs_1_ = bf16[512,128]{1,0:T(8,128)(2,1)S(1)} collective-permute-done((bf16[512,128]{1,0:T(8,128)(2,1)S(1)}, bf16[512,128]{1,0:T(8,128)(2,1)S(1)}, u32[]{:S(2)}, u32[]{:S(2)}) %collective-permute-start.3) | collective-permute-done | bytes 131104 | tf_op jit(solution)/shard_map/ppermute | solution.py:390
  40.9 0.1 broadcast_in_dim.3
  41.0 1.5 %mix.1 = bf16[128,2048]{1,0:T(8,128)(2,1)} custom-call(s32[2]{0:T(128)S(1)} %pad_add_fusion.where_ref, s32[4,4]{1,0:T(4,128)S(1)} %copy-done.5, s32[8]{0:T(128)S(1)} %copy-done.7, f32[1,2048]{1,0:T(1,128)S(1)} %bitcast.5, f32[128,2048]{1,0:T(8,128)S(1)} %attend_self.1.self_ref, bf16[512,128]{1,0:T(8,128)(2,1)S(1)} %get-tuple-element.17.refs_0_, ...), custom_call_target="tpu_custom_call" | custom-call | tf_op jit(solution)/shard_map/mix/pallas_call | solution.py:334
  (10 shorter events, 0.0 us)
Async XLA Ops:
  0.1 1.0 %copy-start.1 = (bf16[128,2048]{1,0:T(8,128)(2,1)S(1)}, bf16[128,2048]{1,0:T(8,128)(2,1)}, u32[]{:S(2)}) copy-start(bf16[128,2048]{1,0:T(8,128)(2,1)} %q_ref.2) | copy-start | bytes 1572868
  1.1 0.9 %copy-start.3 = (bf16[2,128,512]{2,1,0:T(8,128)(2,1)S(1)}, bf16[2,128,512]{2,1,0:T(8,128)(2,1)}, u32[]{:S(2)}) copy-start(bf16[2,128,512]{2,1,0:T(8,128)(2,1)} %kv_hbm.1) | copy-start | bytes 786436
  2.1 0.7 %copy-start.4 = (s32[4,4]{1,0:T(4,128)S(1)}, s32[4,4]{1,0:T(4,128)}, u32[]{:S(2)}) copy-start(s32[4,4]{1,0:T(4,128)} %pairs_ref.3) | copy-start | bytes 196
  2.8 0.7 %copy-start.6 = (s32[8]{0:T(128)S(1)}, s32[8]{0:T(128)}, u32[]{:S(2)}) copy-start(s32[8]{0:T(128)} %slots_ref.3) | copy-start | bytes 100
  4.4 15.9 %collective-permute-start.1 = (bf16[1040,128]{1,0:T(8,128)(2,1)S(1)}, bf16[1040,128]{1,0:T(8,128)(2,1)S(1)}, u32[]{:S(2)}, u32[]{:S(2)}) collective-permute-start(bf16[1040,128]{1,0:T(8,128)(2,1)S(1)} %get-tuple-element.16.refs_2_), channel_id=1, source_target_pairs={{0,4},{4,8},{8,12},{12,0},{1,5},{5,9},{9,13},{13,1},{2,6},{6,10},{... | collective-permute-start | bytes 798728 | tf_op jit(solution)/shard_map/ppermute | solution.py:390
  7.5 12.8 %collective-permute-start = (bf16[528,128]{1,0:T(8,128)(2,1)S(1)}, bf16[528,128]{1,0:T(8,128)(2,1)S(1)}, u32[]{:S(2)}, u32[]{:S(2)}) collective-permute-start(bf16[528,128]{1,0:T(8,128)(2,1)S(1)} %get-tuple-element.12), channel_id=1, source_target_pairs={{0,12},{4,0},{8,4},{12,8},{1,13},{5,1},{9,5},{13,9},{2,14},{6,2},{... | collective-permute-start | bytes 405512 | tf_op jit(solution)/shard_map/ppermute | solution.py:390
  9.6 16.4 %collective-permute-start.4 = (bf16[528,128]{1,0:T(8,128)(2,1)S(1)}, bf16[528,128]{1,0:T(8,128)(2,1)S(1)}, u32[]{:S(2)}, u32[]{:S(2)}) collective-permute-start(bf16[528,128]{1,0:T(8,128)(2,1)S(1)} %get-tuple-element.18), channel_id=1, source_target_pairs={{0,8},{4,12},{8,0},{12,4},{1,9},{5,13},{9,1},{13,5},{2,10},{6,14},... | collective-permute-start | bytes 405512 | tf_op jit(solution)/shard_map/ppermute | solution.py:390
  10.5 2.9 %copy-start = (bf16[2,2,1601,512]{3,1,2,0:T(2,128)(2,1)S(1)}, bf16[2,2,1601,512]{3,1,2,0:T(2,128)(2,1)}, u32[]{:S(2)}) copy-start(bf16[2,2,1601,512]{3,1,2,0:T(2,128)(2,1)} %param.11) | copy-start | bytes 19673092
  24.2 14.2 %collective-permute-start.2 = (bf16[1024,128]{1,0:T(8,128)(2,1)S(1)}, bf16[1024,128]{1,0:T(8,128)(2,1)S(1)}, u32[]{:S(2)}, u32[]{:S(2)}) collective-permute-start(bf16[1024,128]{1,0:T(8,128)(2,1)S(1)} %attend_arrived.3), channel_id=1, source_target_pairs={{0,4},{4,8},{8,12},{12,0},{1,5},{5,9},{9,13},{13,1},{2,6},{6,10},{... | collective-permute-start | bytes 786440 | tf_op jit(solution)/shard_map/ppermute | solution.py:390
  29.8 8.6 %copy-start.9 = (f32[16]{0:T(128)S(1)}, f32[16]{0:T(128)}, u32[]{:S(2)}) copy-start(f32[16]{0:T(128)} %param.12) | copy-start | bytes 196
  29.9 8.6 %copy-start.2 = (bf16[128,2048]{1,0:T(8,128)(2,1)S(1)}, bf16[128,2048]{1,0:T(8,128)(2,1)}, u32[]{:S(2)}) copy-start(bf16[128,2048]{1,0:T(8,128)(2,1)} %q_ref.3) | copy-start | bytes 1572868
  29.9 8.6 %copy-start.8 = (s32[4]{0:T(128)S(1)}, s32[4]{0:T(128)}, u32[]{:S(2)}) copy-start(s32[4]{0:T(128)} %docs_ref.1) | copy-start | bytes 52
  29.9 10.3 %collective-permute-start.5 = (bf16[512,128]{1,0:T(8,128)(2,1)S(1)}, bf16[512,128]{1,0:T(8,128)(2,1)S(1)}, u32[]{:S(2)}, u32[]{:S(2)}) collective-permute-start(bf16[512,128]{1,0:T(8,128)(2,1)S(1)} %attend_arrived.5), channel_id=1, source_target_pairs={{0,8},{4,12},{8,0},{12,4},{1,9},{5,13},{9,1},{13,5},{2,10},{6,14},... | collective-permute-start | bytes 393224 | tf_op jit(solution)/shard_map/ppermute | solution.py:390
  35.5 5.6 %copy-start.5 = (s32[4,4]{1,0:T(4,128)S(1)}, s32[4,4]{1,0:T(4,128)}, u32[]{:S(2)}) copy-start(s32[4,4]{1,0:T(4,128)} %pairs_ref.3) | copy-start | bytes 196
  35.5 5.5 %copy-start.7 = (s32[8]{0:T(128)S(1)}, s32[8]{0:T(128)}, u32[]{:S(2)}) copy-start(s32[8]{0:T(128)} %slots_ref.3) | copy-start | bytes 100
  35.5 5.5 %collective-permute-start.3 = (bf16[512,128]{1,0:T(8,128)(2,1)S(1)}, bf16[512,128]{1,0:T(8,128)(2,1)S(1)}, u32[]{:S(2)}, u32[]{:S(2)}) collective-permute-start(bf16[512,128]{1,0:T(8,128)(2,1)S(1)} %attend_arrived.4), channel_id=1, source_target_pairs={{0,12},{4,0},{8,4},{12,8},{1,13},{5,1},{9,5},{13,9},{2,14},{6,2},{... | collective-permute-start | bytes 393224 | tf_op jit(solution)/shard_map/ppermute | solution.py:390

commit v3 on v2

--- a/solution.py
+++ b/solution.py
@@ -8,6 +8,7 @@
 from jax.experimental.pallas import tpu as pltpu
 from jax.sharding import PartitionSpec as P
 
+
 HEAD_DIM = 128
 Q_HEADS = 64
 KV_HEADS = 8
@@ -15,19 +16,23 @@
 PAIRS = 4
 
 NEG_FILL = -1e30
-META_ROWS = 16
+META_ROWS = 8
 KEY_CHUNK = 256
 LOG2E = math.log2(math.e)
 EXP2_SCALE = HEAD_DIM ** (-0.5) * LOG2E
 
 SMEM = pl.BlockSpec(memory_space=pltpu.SMEM)
 VMEM = pl.BlockSpec(memory_space=pltpu.VMEM)
-ANY = pl.BlockSpec(memory_space=pl.ANY)
+HBM = pl.BlockSpec(memory_space=pltpu.HBM)
 PARAMS = pltpu.CompilerParams(vmem_limit_bytes=24 << 20)
 
 
 def in_vmem(array):
     return pltpu.with_memory_space_constraint(array, pltpu.VMEM)
+
+
+def in_hbm(array):
+    return pltpu.with_memory_space_constraint(array, pltpu.HBM)
 
 
 def owner_slots(pairs_ref, slots_ref):
@@ -55,7 +60,7 @@
     ctx_count = len(out_refs)
     heads = q_ref.shape[1] // HEAD_DIM
     tok_rows = kv_hbm.shape[1]
-    kv_at = heads * BLOCK + META_ROWS
+    kv_at = heads * BLOCK
     copies = []
     for w in range(2):
         for k in range(kv_used):
@@ -77,7 +82,7 @@
         meta = jnp.zeros((META_ROWS, HEAD_DIM), jnp.float32)
         for i, n in enumerate(counts):
             meta = jnp.where(lanes % tiles_dev == i, n.astype(jnp.float32), meta)
-        out_ref[heads * BLOCK : kv_at, :] = meta.astype(jnp.bfloat16)
+        out_ref[out_ref.shape[0] - META_ROWS :, :] = meta.astype(jnp.bfloat16)
     for copy in copies:
         copy.wait()
 
@@ -91,15 +96,15 @@
             pltpu.VMEM((rows + (kv_rows if d == 1 else 0), HEAD_DIM), jnp.bfloat16)
             for d in range(ctx_count)
         ],
-        in_specs=[SMEM, SMEM, SMEM, VMEM, ANY],
+        in_specs=[SMEM, SMEM, SMEM, VMEM, HBM],
         out_specs=[VMEM] * ctx_count,
         scratch_shapes=[pltpu.SemaphoreType.DMA((2 * kv_used,))],
         compiler_params=PARAMS,
         name="pack_queries",
-    )(where, pair_tiles, tile_slot, q_cross, kv_self)
-
-
-def attend_head(q, meta, keys, values, key_count, scores_sc):
+    )(where, in_hbm(pair_tiles), in_hbm(tile_slot), in_hbm(q_cross), in_hbm(kv_self))
+
+
+def attend_head(q, meta, keys, values, key_count, scores_sc, wait_values):
     rows = q.shape[0]
     padded = keys.shape[0]
     lanes = HEAD_DIM
@@ -127,6 +132,7 @@
     if tail_width:
         tail = jnp.max(tail * EXP2_SCALE + bias[:, :tail_width], axis=1, keepdims=True)
         best = jnp.maximum(best, tail)
+    wait_values()
     shift = jnp.where(best > 0.5 * NEG_FILL, bias - best, NEG_FILL)
     totals = jnp.zeros((rows, lanes), jnp.float32)
     total = jnp.zeros((rows, 1), jnp.float32)
@@ -156,66 +162,74 @@
 
 
 def attend_block(q_ref, keys_ref, values_ref, out_ref, lse_ref, scores_sc, key_count, wait):
-    kv_used, padded_len, tiles_dev, _ = keys_ref.shape
-    padded = padded_len * tiles_dev
-    q_rows = scores_sc.shape[0] * kv_used
+    kv_used = keys_ref.shape[0]
     rows = scores_sc.shape[0]
-    meta = q_ref[q_rows : q_rows + META_ROWS, :]
+    meta = q_ref[q_ref.shape[0] - META_ROWS :, :]
     for k in range(kv_used):
-        wait(k)
+        wait_values = wait(k)
         own = slice(k * rows, (k + 1) * rows)
-        keys = keys_ref.at[k].reshape(padded, HEAD_DIM)
-        values = values_ref.at[k].reshape(padded, HEAD_DIM)
-        out, lse = attend_head(q_ref[own, :], meta, keys, values, key_count, scores_sc)
+        keys, values = keys_ref.at[k], values_ref.at[k]
+        out, lse = attend_head(q_ref[own, :], meta, keys, values, key_count, scores_sc, wait_values)
         out_ref[own, :] = out
         if lse_ref is not None:
             lse_ref[own, :] = lse
+
+
+def no_wait(k):
+    return lambda: None
 
 
 def own_body(where_ref, q_ref, image_hbm, *refs, with_lse):
     out_ref = refs[0]
     lse_ref = refs[1] if with_lse else None
     keys_ref, values_ref, scores_sc, sem = refs[-4:]
-    tile_len, tiles_dev = image_hbm.shape[1:3]
-    kv_used, padded_len = keys_ref.shape[:2]
+    _, tile_len, tiles_dev, width = image_hbm.shape
+    key_count = tile_len * tiles_dev
+    kv_used, padded = keys_ref.shape[:2]
+    image = image_hbm.reshape(2, key_count, width)
 
     def copies(k):
         cols = pl.ds(pl.multiple_of((where_ref[1] + k) * HEAD_DIM, HEAD_DIM), HEAD_DIM)
-        held = pl.ds(0, tile_len)
+        held = pl.ds(0, key_count)
         return [
-            pltpu.make_async_copy(image_hbm.at[w, :, :, cols], ref.at[k, held], sem.at[w, k])
+            pltpu.make_async_copy(image.at[w, :, cols], ref.at[k, held], sem.at[w, k])
             for w, ref in enumerate((keys_ref, values_ref))
         ]
 
-    for k in range(kv_used):
-        for copy in copies(k):
-            copy.start()
-    pad = jnp.zeros((padded_len - tile_len, tiles_dev, HEAD_DIM), jnp.bfloat16)
-    for k in range(kv_used):
-        keys_ref[k, tile_len:] = pad
-        values_ref[k, tile_len:] = pad
+    for copy in copies(0):
+        copy.start()
+    if padded > key_count:
+        pad = jnp.zeros((padded - key_count, HEAD_DIM), jnp.bfloat16)
+        for k in range(kv_used):
+            keys_ref[k, key_count:, :] = pad
+            values_ref[k, key_count:, :] = pad
 
     def wait(k):
-        for copy in copies(k):
-            copy.wait()
+        keys, values = copies(k)
+        keys.wait()
+        if k == 0:
+            for later in range(1, kv_used):
+                for copy in copies(later):
+                    copy.start()
+        return values.wait
 
     attend_block(
-        q_ref, keys_ref, values_ref, out_ref, lse_ref, scores_sc, tile_len * tiles_dev, wait
+        q_ref, keys_ref, values_ref, out_ref, lse_ref, scores_sc, key_count, wait
     )
 
 
 def attend_own(where, packed, image_kv, kv_used, q_rows, with_lse):
     _, tile_len, tiles_dev, _ = image_kv.shape
-    held = pltpu.VMEM((kv_used, -(-tile_len // 8) * 8, tiles_dev, HEAD_DIM), jnp.bfloat16)
+    padded = -(-tile_len * tiles_dev // 16) * 16
+    held = pltpu.VMEM((kv_used, padded, HEAD_DIM), jnp.bfloat16)
     out_shape = [pltpu.VMEM((q_rows, HEAD_DIM), jnp.bfloat16)]
     if with_lse:
         out_shape.append(pltpu.VMEM((q_rows, HEAD_DIM), jnp.float32))
     out_shape += [held, held]
-    padded = held.shape[1] * tiles_dev
     results = pl.pallas_call(
         functools.partial(own_body, with_lse=with_lse),
         out_shape=out_shape,
-        in_specs=[SMEM, VMEM, ANY],
+        in_specs=[SMEM, VMEM, HBM],
         out_specs=[VMEM] * len(out_shape),
         scratch_shapes=[
             pltpu.VMEM((q_rows // kv_used, padded), jnp.float32),
@@ -223,26 +237,25 @@
         ],
         compiler_params=PARAMS,
         name="attend_own",
-    )(where, in_vmem(packed), image_kv)
+    )(where, in_vmem(packed), in_hbm(image_kv))
     return results[:-2], [in_vmem(part) for part in results[-2:]]
 
 
 def arrived_body(q_ref, keys_ref, values_ref, *refs, with_lse, riders, key_count, q_rows):
-    rider_refs, refs = refs[: len(riders)], refs[len(riders) :]
+    rider_refs, refs = refs[:riders], refs[riders:]
     out_ref, scores_sc = refs[0], refs[-1]
     lse_ref = refs[1] if with_lse else None
-    for ref, at in zip(rider_refs, riders):
-        out_ref[q_rows:, :] = ref[at:, :]
+    for ref in rider_refs:
+        out_ref[q_rows:, :] = ref[q_rows : out_ref.shape[0], :]
     attend_block(
-        q_ref, keys_ref, values_ref, out_ref, lse_ref, scores_sc, key_count, lambda k: None
+        q_ref, keys_ref, values_ref, out_ref, lse_ref, scores_sc, key_count, no_wait
     )
 
 
 def attend_arrived(packed, held, key_count, q_rows, with_lse, rider=None):
-    kv_used, padded_len, tiles_dev, _ = held[0].shape
-    at = q_rows + META_ROWS
+    kv_used, padded, _ = held[0].shape
     riders = [] if rider is None else [rider]
-    extra = 0 if rider is None else rider.shape[0] - at
+    extra = 0 if rider is None else rider.shape[0] - q_rows - META_ROWS
     out_shape = [pltpu.VMEM((q_rows + extra, HEAD_DIM), jnp.bfloat16)]
     if with_lse:
         out_shape.append(pltpu.VMEM((q_rows, HEAD_DIM), jnp.float32))
@@ -250,14 +263,14 @@
         functools.partial(
             arrived_body,
             with_lse=with_lse,
-            riders=[at] * len(riders),
+            riders=len(riders),
             key_count=key_count,
             q_rows=q_rows,
         ),
         out_shape=out_shape,
         in_specs=[VMEM] * (3 + len(riders)),
         out_specs=[VMEM] * len(out_shape),
-        scratch_shapes=[pltpu.VMEM((q_rows // kv_used, padded_len * tiles_dev), jnp.float32)],
+        scratch_shapes=[pltpu.VMEM((q_rows // kv_used, padded), jnp.float32)],
         compiler_params=PARAMS,
         name="attend_arrived",
     )(in_vmem(packed), *held, *riders)
@@ -365,7 +378,11 @@
     return (self_out + gate_cols * cross.reshape(tok_rows, q_width)).astype(jnp.bfloat16)
 
 
-def local(q_self, q_cross, kv_self, image_kv, cross_gate, doc_lengths, pair_tiles, tile_slot):
+def partner_order(ctx_count):
+    return list(range(ctx_count - 1, 0, -1))
+
+
+def attend(q_self, q_cross, kv_self, image_kv, cross_gate, doc_lengths, pair_tiles, tile_slot):
     tok_rows, q_width = q_self.shape
     local_heads = q_width // HEAD_DIM
     q_rows = local_heads * BLOCK
@@ -393,8 +410,8 @@
         where, pair_tiles, tile_slot, q_cross, kv_self, ctx_count, tiles_dev, kv_used
     )
     last = ctx_count - 1
-    order = [last] + list(range(last - 1, 0, -1))
-    arrived = {d: send(packed[d], d) for d in [1] + order[:-1]}
+    order = partner_order(ctx_count)
+    arrived = {d: send(packed[d], d) for d in order[-1:] + order[:-1]}
     results = {}
     results[0], held = attend_own(where, packed[0], image_kv, kv_used, q_rows, with_lse)
     for d in order:
@@ -404,11 +421,12 @@
         )
         results[d] = [send(part, ctx_count - d) for part in answer]
 
-    at = q_rows + META_ROWS
-    pieces = [(packed[1], at), (arrived[1], at), (results[last][0], q_rows)][: reach + 1]
+    pieces = [packed[1], arrived[1], results[last][0]][: reach + 1]
+    pieces = [(piece, q_rows) for piece in pieces]
     for _ in range(len(pieces), reach + 1):
         array, first = pieces[-1]
-        pieces.append((send(array[first:], 1), 0))
+        rows = 2 * kv_used * tok_rows
+        pieces.append((send(array[first : first + rows], 1), 0))
     self_out = attend_self(where, doc_lengths, q_self, pieces[::-1], kv_used)
     gate_cols = jnp.repeat(jnp.tanh(cross_gate), HEAD_DIM)[None, :]
     partials = [results[d][0] for d in range(ctx_count)]
@@ -431,4 +449,4 @@
         P("groups"),
     )
     out_specs = P(("groups", "ctx"), ("head", "rep"))
-    return jax.shard_map(local, mesh=mesh, in_specs=in_specs, out_specs=out_specs, check_vma=False)
+    return jax.shard_map(attend, mesh=mesh, in_specs=in_specs, out_specs=out_specs, check_vma=False)

time: 42.8 us -> 37.2 us (0.87)
  local copies, waits for them, and re-layouts: 6.29 us -> 0.1 us
  Pallas kernels: 22.7 us -> 18.4 us
  waiting for transfers between devices: 0.72 us -> 3.64 us
  starting transfers between devices: 12.6 us -> 14.7 us
    unnamed x20 -> x10, local copies, waits for them, and re-layouts: 6.22 us -> 0.03 us
    pallas_call x3, Pallas kernels: 11.5 us -> 8.48 us  [attend_arrived(): pl.pallas_call(functools.partial(arrived_body, with_lse=with_lse, riders=...]
    ppermute x6, waiting for transfers between devices: 0.72 us -> 3.64 us  [send(): return lax.ppermute(array, 'ctx', pairs)]
    pallas_call x1, Pallas kernels: 6.91 us -> 4.7 us  [attend_own(): pl.pallas_call(functools.partial(own_body, with_lse=with_lse), out_shape=...]
    ppermute x6, starting transfers between devices: 12.6 us -> 14.7 us  [send(): return lax.ppermute(array, 'ctx', pairs)]
    pallas_call x1, Pallas kernels: 0.98 us -> 1.9 us  [pack_queries(): pl.pallas_call(functools.partial(pack_body, tiles_dev=tiles_dev, kv_used=...]
  transfers between devices with their start and end apart: 6 -> 6, of which waited for: 1 -> 2; matrix products, arithmetic and copies ran while one was open for 0% -> 0% of each run, Pallas kernels for 47% -> 40%
where the time goes in v3:
time: 37.2 us; the launch traced here: 37 us
  Pallas kernels  18.4 us (49%)
  starting transfers between devices  14.7 us (40%)
  waiting for transfers between devices  3.64 us (10%)
    ppermute x6, starting transfers between devices, send(): return lax.ppermute(array, 'ctx', pairs)  14.7 us
    pallas_call x3, Pallas kernels, attend_arrived(): pl.pallas_call(functools.partial(arrived_body, with_lse=with_lse, riders=...  8.48 us
    pallas_call x1, Pallas kernels, attend_own(): pl.pallas_call(functools.partial(own_body, with_lse=with_lse), out_shape=...  4.7 us
    ppermute x6, waiting for transfers between devices, send(): return lax.ppermute(array, 'ctx', pairs)  3.64 us
    pallas_call x1, Pallas kernels, pack_queries(): pl.pallas_call(functools.partial(pack_body, tiles_dev=tiles_dev, kv_used=...  1.9 us
    pallas_call x1, Pallas kernels, attend_self(): pl.pallas_call(functools.partial(self_body, starts=[at for _, at in piece...  1.76 us
    pallas_call x1, Pallas kernels, mix(): pl.pallas_call(functools.partial(mix_body, tiles_dev=tiles_dev), out_shap...  1.54 us
  transfers between devices with their start and end apart: 6, of which 2 were waited for; matrix products, arithmetic and copies ran while one was open for 0% of the time, Pallas kernels for 40%

profile of v3, /device:TPU:0, one launch (start us, length us, event | category | flops | bytes accessed | tf_op | source)
XLA Modules:
  0.0 37.0 jit_solution(9673901772888823331)
XLA Ops:
  0.0 0.1 pad_add_fusion.where_ref
  0.1 1.9 %pack_queries.1 = (bf16[520,128]{1,0:T(8,128)(2,1)S(1)}, bf16[1032,128]{1,0:T(8,128)(2,1)S(1)}, bf16[520,128]{1,0:T(8,128)(2,1)S(1)}, bf16[520,128]{1,0:T(8,128)(2,1)S(1)}) custom-call(s32[2]{0:T(128)S(1)} %pad_add_fusion.where_ref, s32[4,4]{1,0:T(4,128)} %pairs_ref.3, s32[8]{0:T(128)} %slots_ref.3, bf16[128,2048]{1,0:T(8,128)(2,1)} %q_ref.2, ...), custom_call_target="tpu_custom_call" | custom-call | tf_op jit(solution)/shard_map/pack_queries/pallas_call | solution.py:93
  2.0 3.1 %collective-permute-start.1 = (bf16[1032,128]{1,0:T(8,128)(2,1)S(1)}, bf16[1032,128]{1,0:T(8,128)(2,1)S(1)}, u32[]{:S(2)}, u32[]{:S(2)}) collective-permute-start(bf16[1032,128]{1,0:T(8,128)(2,1)S(1)} %get-tuple-element.16.refs_2_), channel_id=1, source_target_pairs={{0,4},{4,8},{8,12},{12,0},{1,5},{5,9},{9,13},{13,1},{2,6},{6,10},{... | collective-permute-start | bytes 792584 | tf_op jit(solution)/shard_map/ppermute | solution.py:407
  5.1 2.1 %collective-permute-start = (bf16[520,128]{1,0:T(8,128)(2,1)S(1)}, bf16[520,128]{1,0:T(8,128)(2,1)S(1)}, u32[]{:S(2)}, u32[]{:S(2)}) collective-permute-start(bf16[520,128]{1,0:T(8,128)(2,1)S(1)} %get-tuple-element.12), channel_id=1, source_target_pairs={{0,12},{4,0},{8,4},{12,8},{1,13},{5,1},{9,5},{13,9},{2,14},{6,2},{... | collective-permute-start | bytes 399368 | tf_op jit(solution)/shard_map/ppermute | solution.py:407
  7.2 0.9 %collective-permute-start.4 = (bf16[520,128]{1,0:T(8,128)(2,1)S(1)}, bf16[520,128]{1,0:T(8,128)(2,1)S(1)}, u32[]{:S(2)}, u32[]{:S(2)}) collective-permute-start(bf16[520,128]{1,0:T(8,128)(2,1)S(1)} %get-tuple-element.18), channel_id=1, source_target_pairs={{0,8},{4,12},{8,0},{12,4},{1,9},{5,13},{9,1},{13,5},{2,10},{6,14},... | collective-permute-start | bytes 399368 | tf_op jit(solution)/shard_map/ppermute | solution.py:407
  8.1 4.7 %attend_own.1 = (bf16[512,128]{1,0:T(8,128)(2,1)S(1)}, bf16[2,3216,128]{2,1,0:T(8,128)(2,1)S(1)}, bf16[2,3216,128]{2,1,0:T(8,128)(2,1)S(1)}) custom-call(s32[2]{0:T(128)S(1)} %pad_add_fusion.where_ref, bf16[520,128]{1,0:T(8,128)(2,1)S(1)} %get-tuple-element.13.q_ref, bf16[2,1601,2,512]{3,2,1,0:T(2,128)(2,1)} %bitcast.5), custom_call_target="tpu_custom_call" | custom-call | tf_op jit(solution)/shard_map/attend_own/pallas_call | solution.py:229
  12.8 2.9 %collective-permute-done.q_ref = bf16[520,128]{1,0:T(8,128)(2,1)S(1)} collective-permute-done((bf16[520,128]{1,0:T(8,128)(2,1)S(1)}, bf16[520,128]{1,0:T(8,128)(2,1)S(1)}, u32[]{:S(2)}, u32[]{:S(2)}) %collective-permute-start) | collective-permute-done | bytes 133152 | tf_op jit(solution)/shard_map/ppermute | solution.py:407
  15.8 0.0 collective-permute-done.1.refs_0_.refs_1_.q_ref
  15.8 2.8 %attend_arrived.3 = bf16[1024,128]{1,0:T(8,128)(2,1)S(1)} custom-call(bf16[520,128]{1,0:T(8,128)(2,1)S(1)} %collective-permute-done.q_ref, bf16[2,3216,128]{2,1,0:T(8,128)(2,1)S(1)} %get-tuple-element.14.keys_ref, bf16[2,3216,128]{2,1,0:T(8,128)(2,1)S(1)} %get-tuple-element.15.values_ref, bf16[1032,128]{1,0:T(8,128)(2,1)S(1)} %collective-permute-done.1.refs_0_.refs_1_.q_ref), custom_call_target="tpu_custom_call" | custom-call | tf_op jit(solution)/shard_map/attend_arrived/pallas_call | solution.py:262
  18.6 3.6 %collective-permute-start.2 = (bf16[1024,128]{1,0:T(8,128)(2,1)S(1)}, bf16[1024,128]{1,0:T(8,128)(2,1)S(1)}, u32[]{:S(2)}, u32[]{:S(2)}) collective-permute-start(bf16[1024,128]{1,0:T(8,128)(2,1)S(1)} %attend_arrived.3), channel_id=1, source_target_pairs={{0,4},{4,8},{8,12},{12,0},{1,5},{5,9},{9,13},{13,1},{2,6},{6,10},{... | collective-permute-start | bytes 786440 | tf_op jit(solution)/shard_map/ppermute | solution.py:407
  22.2 0.0 collective-permute-done.4.q_ref
  22.2 2.8 %attend_arrived.5 = bf16[512,128]{1,0:T(8,128)(2,1)S(1)} custom-call(bf16[520,128]{1,0:T(8,128)(2,1)S(1)} %collective-permute-done.4.q_ref, bf16[2,3216,128]{2,1,0:T(8,128)(2,1)S(1)} %get-tuple-element.14.keys_ref, bf16[2,3216,128]{2,1,0:T(8,128)(2,1)S(1)} %get-tuple-element.15.values_ref), custom_call_target="tpu_custom_call" | custom-call | tf_op jit(solution)/shard_map/attend_arrived/pallas_call | solution.py:262
  25.0 0.0 copy-start.4
  25.0 0.0 copy-start
  25.0 0.0 copy-start.3
  25.1 2.0 %collective-permute-start.5 = (bf16[512,128]{1,0:T(8,128)(2,1)S(1)}, bf16[512,128]{1,0:T(8,128)(2,1)S(1)}, u32[]{:S(2)}, u32[]{:S(2)}) collective-permute-start(bf16[512,128]{1,0:T(8,128)(2,1)S(1)} %attend_arrived.5), channel_id=1, source_target_pairs={{0,8},{4,12},{8,0},{12,4},{1,9},{5,13},{9,1},{13,5},{2,10},{6,14},... | collective-permute-start | bytes 393224 | tf_op jit(solution)/shard_map/ppermute | solution.py:407
  27.1 2.8 %attend_arrived.4 = bf16[512,128]{1,0:T(8,128)(2,1)S(1)} custom-call(bf16[1032,128]{1,0:T(8,128)(2,1)S(1)} %collective-permute-done.1.refs_0_.refs_1_.q_ref, bf16[2,3216,128]{2,1,0:T(8,128)(2,1)S(1)} %get-tuple-element.14.keys_ref, bf16[2,3216,128]{2,1,0:T(8,128)(2,1)S(1)} %get-tuple-element.15.values_ref), custom_call_target="tpu_custom_call" | custom-call | tf_op jit(solution)/shard_map/attend_arrived/pallas_call | solution.py:262
  29.9 0.0 copy-start.1
  29.9 0.0 copy-start.2
  29.9 3.0 %collective-permute-start.3 = (bf16[512,128]{1,0:T(8,128)(2,1)S(1)}, bf16[512,128]{1,0:T(8,128)(2,1)S(1)}, u32[]{:S(2)}, u32[]{:S(2)}) collective-permute-start(bf16[512,128]{1,0:T(8,128)(2,1)S(1)} %attend_arrived.4), channel_id=1, source_target_pairs={{0,12},{4,0},{8,4},{12,8},{1,13},{5,1},{9,5},{13,9},{2,14},{6,2},{... | collective-permute-start | bytes 393224 | tf_op jit(solution)/shard_map/ppermute | solution.py:407
  32.9 0.0 copy-done.4
  32.9 0.0 collective-permute-done.2.refs_0_.refs_3_
  32.9 0.0 copy-done
  32.9 0.0 copy-done.3
  32.9 1.8 %attend_self.1.self_ref = f32[128,2048]{1,0:T(8,128)S(1)} custom-call(s32[2]{0:T(128)S(1)} %pad_add_fusion.where_ref, s32[4]{0:T(128)S(1)} %copy-done.3, bf16[128,2048]{1,0:T(8,128)(2,1)S(1)} %copy-done, bf16[1024,128]{1,0:T(8,128)(2,1)S(1)} %collective-permute-done.2.refs_0_.refs_3_, bf16[1032,128]{1,0:T(8,128)(2,1)S(1)} %collective-permute-done.1.refs_0_.refs_1_.q_ref, ...), custom_call_target="tpu_custom_call" | custom-call | tf_op jit(solution)/shard_map/attend_self/pallas_call | solution.py:321
  34.7 0.0 collective-permute-done.5.refs_2_
  34.7 0.7 %collective-permute-done.3.refs_1_ = bf16[512,128]{1,0:T(8,128)(2,1)S(1)} collective-permute-done((bf16[512,128]{1,0:T(8,128)(2,1)S(1)}, bf16[512,128]{1,0:T(8,128)(2,1)S(1)}, u32[]{:S(2)}, u32[]{:S(2)}) %collective-permute-start.3) | collective-permute-done | bytes 131104 | tf_op jit(solution)/shard_map/ppermute | solution.py:407
  35.4 0.1 broadcast_in_dim.3
  35.5 0.0 copy-done.1
  35.5 0.0 copy-done.2
  35.5 1.5 %mix.1 = bf16[128,2048]{1,0:T(8,128)(2,1)} custom-call(s32[2]{0:T(128)S(1)} %pad_add_fusion.where_ref, s32[4,4]{1,0:T(4,128)S(1)} %copy-done.1, s32[8]{0:T(128)S(1)} %copy-done.2, f32[1,2048]{1,0:T(1,128)S(1)} %bitcast.4, f32[128,2048]{1,0:T(8,128)S(1)} %attend_self.1.self_ref, bf16[512,128]{1,0:T(8,128)(2,1)S(1)} %get-tuple-element.17.refs_0_, ...), custom_call_target="tpu_custom_call" | custom-call | tf_op jit(solution)/shard_map/mix/pallas_call | solution.py:347
  (1 shorter events, 0.0 us)
Async XLA Ops:
  2.0 13.8 %collective-permute-start.1 = (bf16[1032,128]{1,0:T(8,128)(2,1)S(1)}, bf16[1032,128]{1,0:T(8,128)(2,1)S(1)}, u32[]{:S(2)}, u32[]{:S(2)}) collective-permute-start(bf16[1032,128]{1,0:T(8,128)(2,1)S(1)} %get-tuple-element.16.refs_2_), channel_id=1, source_target_pairs={{0,4},{4,8},{8,12},{12,0},{1,5},{5,9},{9,13},{13,1},{2,6},{6,10},{... | collective-permute-start | bytes 792584 | tf_op jit(solution)/shard_map/ppermute | solution.py:407
  5.1 10.7 %collective-permute-start = (bf16[520,128]{1,0:T(8,128)(2,1)S(1)}, bf16[520,128]{1,0:T(8,128)(2,1)S(1)}, u32[]{:S(2)}, u32[]{:S(2)}) collective-permute-start(bf16[520,128]{1,0:T(8,128)(2,1)S(1)} %get-tuple-element.12), channel_id=1, source_target_pairs={{0,12},{4,0},{8,4},{12,8},{1,13},{5,1},{9,5},{13,9},{2,14},{6,2},{... | collective-permute-start | bytes 399368 | tf_op jit(solution)/shard_map/ppermute | solution.py:407
  7.2 15.0 %collective-permute-start.4 = (bf16[520,128]{1,0:T(8,128)(2,1)S(1)}, bf16[520,128]{1,0:T(8,128)(2,1)S(1)}, u32[]{:S(2)}, u32[]{:S(2)}) collective-permute-start(bf16[520,128]{1,0:T(8,128)(2,1)S(1)} %get-tuple-element.18), channel_id=1, source_target_pairs={{0,8},{4,12},{8,0},{12,4},{1,9},{5,13},{9,1},{13,5},{2,10},{6,14},... | collective-permute-start | bytes 399368 | tf_op jit(solution)/shard_map/ppermute | solution.py:407
  18.6 14.3 %collective-permute-start.2 = (bf16[1024,128]{1,0:T(8,128)(2,1)S(1)}, bf16[1024,128]{1,0:T(8,128)(2,1)S(1)}, u32[]{:S(2)}, u32[]{:S(2)}) collective-permute-start(bf16[1024,128]{1,0:T(8,128)(2,1)S(1)} %attend_arrived.3), channel_id=1, source_target_pairs={{0,4},{4,8},{8,12},{12,0},{1,5},{5,9},{9,13},{13,1},{2,6},{6,10},{... | collective-permute-start | bytes 786440 | tf_op jit(solution)/shard_map/ppermute | solution.py:407
  25.0 7.8 %copy-start.4 = (f32[16]{0:T(128)S(1)}, f32[16]{0:T(128)}, u32[]{:S(2)}) copy-start(f32[16]{0:T(128)} %param.12) | copy-start | bytes 196
  25.0 7.8 %copy-start = (bf16[128,2048]{1,0:T(8,128)(2,1)S(1)}, bf16[128,2048]{1,0:T(8,128)(2,1)}, u32[]{:S(2)}) copy-start(bf16[128,2048]{1,0:T(8,128)(2,1)} %q_ref.3) | copy-start | bytes 1572868
  25.0 7.8 %copy-start.3 = (s32[4]{0:T(128)S(1)}, s32[4]{0:T(128)}, u32[]{:S(2)}) copy-start(s32[4]{0:T(128)} %docs_ref.1) | copy-start | bytes 52
  25.1 9.6 %collective-permute-start.5 = (bf16[512,128]{1,0:T(8,128)(2,1)S(1)}, bf16[512,128]{1,0:T(8,128)(2,1)S(1)}, u32[]{:S(2)}, u32[]{:S(2)}) collective-permute-start(bf16[512,128]{1,0:T(8,128)(2,1)S(1)} %attend_arrived.5), channel_id=1, source_target_pairs={{0,8},{4,12},{8,0},{12,4},{1,9},{5,13},{9,1},{13,5},{2,10},{6,14},... | collective-permute-start | bytes 393224 | tf_op jit(solution)/shard_map/ppermute | solution.py:407
  29.9 5.6 %copy-start.1 = (s32[4,4]{1,0:T(4,128)S(1)}, s32[4,4]{1,0:T(4,128)}, u32[]{:S(2)}) copy-start(s32[4,4]{1,0:T(4,128)} %pairs_ref.3) | copy-start | bytes 196
  29.9 5.6 %copy-start.2 = (s32[8]{0:T(128)S(1)}, s32[8]{0:T(128)}, u32[]{:S(2)}) copy-start(s32[8]{0:T(128)} %slots_ref.3) | copy-start | bytes 100
  29.9 5.5 %collective-permute-start.3 = (bf16[512,128]{1,0:T(8,128)(2,1)S(1)}, bf16[512,128]{1,0:T(8,128)(2,1)S(1)}, u32[]{:S(2)}, u32[]{:S(2)}) collective-permute-start(bf16[512,128]{1,0:T(8,128)(2,1)S(1)} %attend_arrived.4), channel_id=1, source_target_pairs={{0,12},{4,0},{8,4},{12,8},{1,13},{5,1},{9,5},{13,9},{2,14},{6,2},{... | collective-permute-start | bytes 393224 | tf_op jit(solution)/shard_map/ppermute | solution.py:407

commit v4 on v3

--- a/solution.py
+++ b/solution.py
@@ -18,6 +18,8 @@
 NEG_FILL = -1e30
 META_ROWS = 8
 KEY_CHUNK = 256
+LAG = 2
+MOST_TOTAL = 2.0**100
 LOG2E = math.log2(math.e)
 EXP2_SCALE = HEAD_DIM ** (-0.5) * LOG2E
 
@@ -51,65 +53,147 @@
     return block, counts
 
 
-def owner_at(where_ref, distance, ctx_count):
-    return lax.rem(where_ref[0] + distance, ctx_count)
-
-
-def pack_body(where_ref, pairs_ref, slots_ref, q_ref, kv_hbm, *refs, tiles_dev, kv_used):
-    out_refs, sem = refs[:-1], refs[-1]
+def pack_body(
+    pairs_hbm, slots_hbm, q_hbm, kv_hbm, *refs, tiles_dev, kv_used, kv_first
+):
+    out_refs = refs[:-5]
+    q_ref, pairs_ref, slots_ref, kv_sem, sem = refs[-5:]
     ctx_count = len(out_refs)
     heads = q_ref.shape[1] // HEAD_DIM
     tok_rows = kv_hbm.shape[1]
     kv_at = heads * BLOCK
+    tables = [
+        pltpu.make_async_copy(pairs_hbm, pairs_ref, sem.at[0]),
+        pltpu.make_async_copy(slots_hbm, slots_ref, sem.at[1]),
+    ]
+    queries = pltpu.make_async_copy(q_hbm, q_ref, sem.at[2])
     copies = []
     for w in range(2):
         for k in range(kv_used):
-            cols = pl.ds(pl.multiple_of((where_ref[1] + k) * HEAD_DIM, HEAD_DIM), HEAD_DIM)
+            cols = pl.ds(pl.multiple_of((kv_first() + k) * HEAD_DIM, HEAD_DIM), HEAD_DIM)
             part = w * kv_used + k
             rows = pl.ds(kv_at + part * tok_rows, tok_rows)
             copies.append(
-                pltpu.make_async_copy(kv_hbm.at[w, :, cols], out_refs[1].at[rows, :], sem.at[part])
+                pltpu.make_async_copy(kv_hbm.at[w, :, cols], out_refs[1].at[rows, :], kv_sem.at[part])
             )
-    for copy in copies:
+    for copy in tables + [queries] + copies:
         copy.start()
+    for copy in tables:
+        copy.wait()
     stored = owner_slots(pairs_ref, slots_ref)
+    here = lax.axis_index("ctx")
     lanes = lax.broadcasted_iota(jnp.int32, (META_ROWS, HEAD_DIM), 1)
+    blocks = []
     for distance, out_ref in enumerate(out_refs):
-        block, counts = block_for(stored, owner_at(where_ref, distance, ctx_count), tiles_dev)
-        rows = pl.ds(pl.multiple_of(block * BLOCK, BLOCK), BLOCK)
-        for h in range(heads):
-            out_ref[h * BLOCK : (h + 1) * BLOCK, :] = q_ref[rows, h * HEAD_DIM : (h + 1) * HEAD_DIM]
+        owner = lax.rem(here + distance, ctx_count)
+        block, counts = block_for(stored, owner, tiles_dev)
+        blocks.append(block)
         meta = jnp.zeros((META_ROWS, HEAD_DIM), jnp.float32)
         for i, n in enumerate(counts):
             meta = jnp.where(lanes % tiles_dev == i, n.astype(jnp.float32), meta)
         out_ref[out_ref.shape[0] - META_ROWS :, :] = meta.astype(jnp.bfloat16)
+    queries.wait()
+    for block, out_ref in zip(blocks, out_refs):
+        rows = pl.ds(pl.multiple_of(block * BLOCK, BLOCK), BLOCK)
+        for h in range(heads):
+            out_ref[h * BLOCK : (h + 1) * BLOCK, :] = q_ref[rows, h * HEAD_DIM : (h + 1) * HEAD_DIM]
     for copy in copies:
         copy.wait()
 
 
-def pack_queries(where, pair_tiles, tile_slot, q_cross, kv_self, ctx_count, tiles_dev, kv_used):
+def pack_queries(pair_tiles, tile_slot, q_cross, kv_self, ctx_count, tiles_dev, kv_used, kv_first):
     rows = q_cross.shape[1] // HEAD_DIM * BLOCK + META_ROWS
     kv_rows = 2 * kv_used * kv_self.shape[1]
     return pl.pallas_call(
-        functools.partial(pack_body, tiles_dev=tiles_dev, kv_used=kv_used),
+        functools.partial(pack_body, tiles_dev=tiles_dev, kv_used=kv_used, kv_first=kv_first),
         out_shape=[
             pltpu.VMEM((rows + (kv_rows if d == 1 else 0), HEAD_DIM), jnp.bfloat16)
             for d in range(ctx_count)
         ],
-        in_specs=[SMEM, SMEM, SMEM, VMEM, HBM],
+        in_specs=[HBM] * 4,
         out_specs=[VMEM] * ctx_count,
-        scratch_shapes=[pltpu.SemaphoreType.DMA((2 * kv_used,))],
+        scratch_shapes=[
+            pltpu.VMEM(q_cross.shape, q_cross.dtype),
+            pltpu.SMEM(pair_tiles.shape, jnp.int32),
+            pltpu.SMEM(tile_slot.shape, jnp.int32),
+            pltpu.SemaphoreType.DMA((2 * kv_used,)),
+            pltpu.SemaphoreType.DMA((3,)),
+        ],
         compiler_params=PARAMS,
         name="pack_queries",
-    )(where, in_hbm(pair_tiles), in_hbm(tile_slot), in_hbm(q_cross), in_hbm(kv_self))
-
-
-def attend_head(q, meta, keys, values, key_count, scores_sc, wait_values):
+    )(in_hbm(pair_tiles), in_hbm(tile_slot), in_hbm(q_cross), in_hbm(kv_self))
+
+
+def count_bias(meta):
+    count = meta[0:1, :].astype(jnp.float32)
+    return jnp.where(count > 0, jnp.log(jnp.maximum(count, 1.0)) * LOG2E, NEG_FILL)
+
+
+def finish_head(blended, total, best):
+    live = total > 0
+    total = jnp.where(live, total, 1.0)
+    out = (blended / total).astype(jnp.bfloat16)
+    lse = jnp.where(live, best * (1.0 / LOG2E) + jnp.log(total), NEG_FILL)
+    return out, jnp.broadcast_to(lse, (lse.shape[0], HEAD_DIM))
+
+
+def attend_head(q, meta, keys, values, key_count, wait_values):
     rows = q.shape[0]
     padded = keys.shape[0]
     lanes = HEAD_DIM
-    count = meta[0:1, :].astype(jnp.float32)
-    bias = jnp.where(count > 0, jnp.log(jnp.maximum(count, 1.0)) * LOG2E, NEG_FILL)
+    bias = count_bias(meta)
+
+    def score(at, size):
+        return lax.dot_general(
+            q, keys[at : at + size, :], (((1,), (1,)), ((), ())), preferred_element_type=jnp.float32
+        )
+
+    first = score(0, KEY_CHUNK)
+    best = first[:, :lanes]
+    for col in range(lanes, KEY_CHUNK, lanes):
+        best = jnp.maximum(best, first[:, col : col + lanes])
+    best = jnp.max(best * EXP2_SCALE + bias, axis=1, keepdims=True)
+    shift = jnp.where(best > 0.5 * NEG_FILL, bias - best, NEG_FILL)
+    totals = jnp.zeros((rows, lanes), jnp.float32)
+    total = jnp.zeros((rows, 1), jnp.float32)
+    blended = jnp.zeros((rows, HEAD_DIM), jnp.float32)
+    waiting = []
+    wait_values()
+    for at in list(range(0, padded, KEY_CHUNK)) + [None] * LAG:
+        if at is not None:
+            size = min(KEY_CHUNK, padded - at)
+            scores = score(at, size)
+            pieces = []
+            for col in range(0, size, lanes):
+                width = min(lanes, size - col)
+                weights = jnp.exp2(scores[:, col : col + width] * EXP2_SCALE + shift[:, :width])
+                valid = key_count - at - col
+                if width > valid:
+                    held = lax.broadcasted_iota(jnp.int32, weights.shape, 1) < valid
+                    weights = jnp.where(held, weights, 0.0)
+                if width == lanes:
+                    totals = totals + weights
+                else:
+                    total = total + jnp.sum(weights, axis=1, keepdims=True)
+                pieces.append(weights.astype(jnp.bfloat16))
+            weights = jnp.concatenate(pieces, axis=1) if len(pieces) > 1 else pieces[0]
+            waiting.append((weights, at))
+        if len(waiting) > LAG or at is None:
+            weights, start = waiting.pop(0)
+            blended = blended + jnp.dot(
+                weights,
+                values[start : start + weights.shape[1], :],
+                preferred_element_type=jnp.float32,
+            )
+    total = total + jnp.sum(totals, axis=1, keepdims=True)
+    return *finish_head(blended, total, best), total
+
+
+def attend_head_exact(q, meta, keys, values, key_count, scores_sc):
+    rows = q.shape[0]
+    padded = keys.shape[0]
+    lanes = HEAD_DIM
+    bias = count_bias(meta)
     best = None
     for at in range(0, padded, KEY_CHUNK):
         size = min(KEY_CHUNK, padded - at)
@@ -132,7 +216,6 @@
     if tail_width:
         tail = jnp.max(tail * EXP2_SCALE + bias[:, :tail_width], axis=1, keepdims=True)
         best = jnp.maximum(best, tail)
-    wait_values()
     shift = jnp.where(best > 0.5 * NEG_FILL, bias - best, NEG_FILL)
     totals = jnp.zeros((rows, lanes), jnp.float32)
     total = jnp.zeros((rows, 1), jnp.float32)
@@ -154,25 +237,38 @@
             weights, values[at : at + size, :], preferred_element_type=jnp.float32
         )
     total = total + jnp.sum(totals, axis=1, keepdims=True)
-    live = total > 0
-    total = jnp.where(live, total, 1.0)
-    out = (blended / total).astype(jnp.bfloat16)
-    lse = jnp.where(live, best * (1.0 / LOG2E) + jnp.log(total), NEG_FILL)
-    return out, jnp.broadcast_to(lse, (rows, lanes))
+    return finish_head(blended, total, best)
 
 
 def attend_block(q_ref, keys_ref, values_ref, out_ref, lse_ref, scores_sc, key_count, wait):
     kv_used = keys_ref.shape[0]
     rows = scores_sc.shape[0]
     meta = q_ref[q_ref.shape[0] - META_ROWS :, :]
+
+    def place(k):
+        return slice(k * rows, (k + 1) * rows)
+
+    def store(k, out, lse):
+        out_ref[place(k), :] = out
+        if lse_ref is not None:
+            lse_ref[place(k), :] = lse
+
+    highest = jnp.zeros((rows, 1), jnp.float32)
     for k in range(kv_used):
         wait_values = wait(k)
-        own = slice(k * rows, (k + 1) * rows)
         keys, values = keys_ref.at[k], values_ref.at[k]
-        out, lse = attend_head(q_ref[own, :], meta, keys, values, key_count, scores_sc, wait_values)
-        out_ref[own, :] = out
-        if lse_ref is not None:
-            lse_ref[own, :] = lse
+        out, lse, total = attend_head(q_ref[place(k), :], meta, keys, values, key_count, wait_values)
+        store(k, out, lse)
+        highest = jnp.maximum(highest, total)
+
+    @pl.when(jnp.logical_not(jnp.max(highest) <= MOST_TOTAL))
+    def _():
+        for k in range(kv_used):
+            keys, values = keys_ref.at[k], values_ref.at[k]
+            store(
+                k,
+                *attend_head_exact(q_ref[place(k), :], meta, keys, values, key_count, scores_sc),
+            )
 
 
 def no_wait(k):
@@ -241,39 +337,44 @@
     return results[:-2], [in_vmem(part) for part in results[-2:]]
 
 
-def arrived_body(q_ref, keys_ref, values_ref, *refs, with_lse, riders, key_count, q_rows):
-    rider_refs, refs = refs[:riders], refs[riders:]
-    out_ref, scores_sc = refs[0], refs[-1]
-    lse_ref = refs[1] if with_lse else None
-    for ref in rider_refs:
-        out_ref[q_rows:, :] = ref[q_rows : out_ref.shape[0], :]
+def arrived_body(q_ref, keys_ref, values_ref, out_ref, *refs, with_lse, key_count):
+    lse_ref = refs[0] if with_lse else None
     attend_block(
-        q_ref, keys_ref, values_ref, out_ref, lse_ref, scores_sc, key_count, no_wait
+        q_ref, keys_ref, values_ref, out_ref, lse_ref, refs[-1], key_count, no_wait
     )
 
 
-def attend_arrived(packed, held, key_count, q_rows, with_lse, rider=None):
+def attend_arrived(packed, held, key_count, q_rows, with_lse):
     kv_used, padded, _ = held[0].shape
-    riders = [] if rider is None else [rider]
-    extra = 0 if rider is None else rider.shape[0] - q_rows - META_ROWS
-    out_shape = [pltpu.VMEM((q_rows + extra, HEAD_DIM), jnp.bfloat16)]
+    out_shape = [pltpu.VMEM((q_rows, HEAD_DIM), jnp.bfloat16)]
     if with_lse:
         out_shape.append(pltpu.VMEM((q_rows, HEAD_DIM), jnp.float32))
     return pl.pallas_call(
-        functools.partial(
-            arrived_body,
-            with_lse=with_lse,
-            riders=len(riders),
-            key_count=key_count,
-            q_rows=q_rows,
-        ),
+        functools.partial(arrived_body, with_lse=with_lse, key_count=key_count),
         out_shape=out_shape,
-        in_specs=[VMEM] * (3 + len(riders)),
+        in_specs=[VMEM] * 3,
         out_specs=[VMEM] * len(out_shape),
         scratch_shapes=[pltpu.VMEM((q_rows // kv_used, padded), jnp.float32)],
         compiler_params=PARAMS,
         name="attend_arrived",
-    )(in_vmem(packed), *held, *riders)
+    )(in_vmem(packed), *held)
+
+
+def join_body(partial_ref, message_ref, out_ref):
+    q_rows = partial_ref.shape[0]
+    out_ref[:q_rows, :] = partial_ref[...]
+    out_ref[q_rows:, :] = message_ref[q_rows : out_ref.shape[0], :]
+
+
+def join_keys(partial, message):
+    return pl.pallas_call(
+        join_body,
+        out_shape=pltpu.VMEM((message.shape[0] - META_ROWS, HEAD_DIM), jnp.bfloat16),
+        in_specs=[VMEM] * 2,
+        out_specs=VMEM,
+        compiler_params=PARAMS,
+        name="join_keys",
+    )(in_vmem(partial), in_vmem(message))
 
 
 def self_body(where_ref, docs_ref, q_ref, *refs, starts, kv_used):
@@ -329,11 +430,13 @@
     )(where, doc_lengths, in_vmem(q_self), *[in_vmem(array) for array, _ in pieces])
 
 
-def mix_body(where_ref, pairs_ref, slots_ref, gate_ref, self_ref, *refs, tiles_dev):
-    partial_refs, out_ref = refs[:-1], refs[-1]
+def mix_body(pairs_ref, slots_ref, gate_ref, self_ref, *refs, tiles_dev):
+    partial_refs, (out_hbm, out_ref, sem) = refs[:-3], refs[-3:]
     stored = owner_slots(pairs_ref, slots_ref)
+    here = lax.axis_index("ctx")
+    copies = []
     for distance, partial_ref in enumerate(partial_refs):
-        owner = owner_at(where_ref, distance, len(partial_refs))
+        owner = lax.rem(here + distance, len(partial_refs))
         block, _ = block_for(stored, owner, tiles_dev)
         rows = pl.ds(pl.multiple_of(block * BLOCK, BLOCK), BLOCK)
         for h in range(self_ref.shape[1] // HEAD_DIM):
@@ -341,21 +444,30 @@
             cross = partial_ref[h * BLOCK : (h + 1) * BLOCK, :].astype(jnp.float32)
             mixed = self_ref[rows, cols] + gate_ref[:, cols] * cross
             out_ref[rows, cols] = mixed.astype(jnp.bfloat16)
-
-
-def mix(where, pair_tiles, tile_slot, gate_cols, self_out, partials, tiles_dev):
+        copy = pltpu.make_async_copy(out_ref.at[rows, :], out_hbm.at[rows, :], sem.at[distance])
+        copy.start()
+        copies.append(copy)
+    for copy in copies:
+        copy.wait()
+
+
+def mix(pair_tiles, tile_slot, gate_cols, self_out, partials, tiles_dev):
+    out = jax.ShapeDtypeStruct(self_out.shape, jnp.bfloat16)
     return pl.pallas_call(
         functools.partial(mix_body, tiles_dev=tiles_dev),
-        out_shape=jax.ShapeDtypeStruct(self_out.shape, jnp.bfloat16),
-        in_specs=[SMEM] * 3 + [VMEM] * (2 + len(partials)),
-        out_specs=VMEM,
+        out_shape=out,
+        in_specs=[SMEM] * 2 + [VMEM] * (2 + len(partials)),
+        out_specs=HBM,
+        scratch_shapes=[
+            pltpu.VMEM(out.shape, out.dtype),
+            pltpu.SemaphoreType.DMA((len(partials),)),
+        ],
         compiler_params=PARAMS,
         name="mix",
     )(
-        where,
         pair_tiles,
         tile_slot,
-        gate_cols,
+        in_vmem(gate_cols),
         in_vmem(self_out),
         *[in_vmem(partial) for partial in partials],
     )
@@ -398,8 +510,11 @@
     reach = min(ctx_count - 1, -(-(ctx_count * tok_rows // 2 - 1) // tok_rows))
 
     here = lax.axis_index("ctx").astype(jnp.int32)
-    kv_first = (lax.axis_index("rep") * local_heads // grouping).astype(jnp.int32)
-    where = jnp.stack([here, kv_first])
+
+    def kv_first():
+        return lax.axis_index("rep") * local_heads // grouping
+
+    where = jnp.stack([here, kv_first().astype(jnp.int32)])
     image_kv = jnp.transpose(image_kv, (0, 2, 1, 3))
 
     def send(array, distance):
@@ -407,7 +522,7 @@
         return lax.ppermute(array, "ctx", pairs)
 
     packed = pack_queries(
-        where, pair_tiles, tile_slot, q_cross, kv_self, ctx_count, tiles_dev, kv_used
+        pair_tiles, tile_slot, q_cross, kv_self, ctx_count, tiles_dev, kv_used, kv_first
     )
     last = ctx_count - 1
     order = partner_order(ctx_count)
@@ -415,10 +530,9 @@
     results = {}
     results[0], held = attend_own(where, packed[0], image_kv, kv_used, q_rows, with_lse)
     for d in order:
-        rider = in_vmem(arrived[1]) if d == last else None
-        answer = attend_arrived(
-            arrived[d], held, tile_len * tiles_dev, q_rows, with_lse, rider
-        )
+        answer = attend_arrived(arrived[d], held, tile_len * tiles_dev, q_rows, with_lse)
+        if d == last:
+            answer = [join_keys(answer[0], arrived[1]), *answer[1:]]
         results[d] = [send(part, ctx_count - d) for part in answer]
 
     pieces = [packed[1], arrived[1], results[last][0]][: reach + 1]
@@ -431,7 +545,7 @@
     gate_cols = jnp.repeat(jnp.tanh(cross_gate), HEAD_DIM)[None, :]
     partials = [results[d][0] for d in range(ctx_count)]
     if one_owner:
-        return mix(where, pair_tiles, tile_slot, gate_cols, self_out, partials, tiles_dev)
+        return mix(pair_tiles, tile_slot, gate_cols, self_out, partials, tiles_dev)
     partials = [partial[:q_rows] for partial in partials]
     sums = [results[d][1] for d in range(ctx_count)]
     return mix_owners(where, pair_tiles, tile_slot, gate_cols, self_out, partials, sums, tiles_dev)

time: 37.2 us -> 41.8 us (1.12)
  Pallas kernels: 18.4 us -> 27.6 us
  starting transfers between devices: 14.7 us -> 11.4 us
  waiting for transfers between devices: 3.64 us -> 2.18 us
    pallas_call x3 -> x4, Pallas kernels: 8.48 us -> 15.7 us  [the longest x3 15.7 us: attend_arrived(): pl.pallas_call(functools.partial(arrived_body, with_lse=with_lse, key_cou...]
    ppermute x6, starting transfers between devices: 14.7 us -> 11.4 us  [send(): return lax.ppermute(array, 'ctx', pairs)]
    pallas_call x1, Pallas kernels: 4.7 us -> 7.46 us  [attend_own(): pl.pallas_call(functools.partial(own_body, with_lse=with_lse), out_shape=...]
    ppermute x6, waiting for transfers between devices: 3.64 us -> 2.18 us  [send(): return lax.ppermute(array, 'ctx', pairs)]
    pallas_call x1, Pallas kernels: 1.9 us -> 1.2 us  [pack_queries(): pl.pallas_call(functools.partial(pack_body, tiles_dev=tiles_dev, kv_used=...]
  transfers between devices with their start and end apart: 6 -> 6, of which waited for: 2 -> 2; matrix products, arithmetic and copies ran while one was open for 0% -> 0% of each run, Pallas kernels for 40% -> 60%
where the time goes in v4:
time: 41.8 us; the launch traced here: 41.6 us
  Pallas kernels  27.6 us (66%)
  starting transfers between devices  11.4 us (27%)
  waiting for transfers between devices  2.18 us (5%)
    pallas_call x3, Pallas kernels, attend_arrived(): pl.pallas_call(functools.partial(arrived_body, with_lse=with_lse, key_cou...  15.7 us
    ppermute x6, starting transfers between devices, send(): return lax.ppermute(array, 'ctx', pairs)  11.4 us
    pallas_call x1, Pallas kernels, attend_own(): pl.pallas_call(functools.partial(own_body, with_lse=with_lse), out_shape=...  7.46 us
    ppermute x6, waiting for transfers between devices, send(): return lax.ppermute(array, 'ctx', pairs)  2.18 us
    pallas_call x1, Pallas kernels, attend_self(): pl.pallas_call(functools.partial(self_body, starts=[at for _, at in piece...  1.75 us
    pallas_call x1, Pallas kernels, mix(): pl.pallas_call(functools.partial(mix_body, tiles_dev=tiles_dev), out_shap...  1.46 us
    pallas_call x1, Pallas kernels, pack_queries(): pl.pallas_call(functools.partial(pack_body, tiles_dev=tiles_dev, kv_used=...  1.2 us
  transfers between devices with their start and end apart: 6, of which 2 were waited for; matrix products, arithmetic and copies ran while one was open for 0% of the time, Pallas kernels for 60%

profile of v4, /device:TPU:0, one launch (start us, length us, event | category | flops | bytes accessed | tf_op | source)
XLA Modules:
  0.0 41.6 jit_solution(1734586447144877510)
XLA Ops:
  0.0 1.2 %pack_queries.1 = (bf16[520,128]{1,0:T(8,128)(2,1)S(1)}, bf16[1032,128]{1,0:T(8,128)(2,1)S(1)}, bf16[520,128]{1,0:T(8,128)(2,1)S(1)}, bf16[520,128]{1,0:T(8,128)(2,1)S(1)}) custom-call(s32[4,4]{1,0:T(4,128)} %pairs_ref.1, s32[8]{0:T(128)} %slots_ref.1, bf16[128,2048]{1,0:T(8,128)(2,1)} %q_hbm.1, bf16[2,128,512]{2,1,0:T(8,128)(2,1)} %kv_hbm.1), custom_call_target="tpu_custom_call" | custom-call | tf_op jit(solution)/shard_map/pack_queries/pallas_call | solution.py:107
  1.2 3.1 %collective-permute-start.1 = (bf16[1032,128]{1,0:T(8,128)(2,1)S(1)}, bf16[1032,128]{1,0:T(8,128)(2,1)S(1)}, u32[]{:S(2)}, u32[]{:S(2)}) collective-permute-start(bf16[1032,128]{1,0:T(8,128)(2,1)S(1)} %get-tuple-element.16.refs_2_), channel_id=1, source_target_pairs={{0,4},{4,8},{8,12},{12,0},{1,5},{5,9},{9,13},{13,1},{2,6},{6,10},{... | collective-permute-start | bytes 792584 | tf_op jit(solution)/shard_map/ppermute | solution.py:522
  4.3 2.1 %collective-permute-start = (bf16[520,128]{1,0:T(8,128)(2,1)S(1)}, bf16[520,128]{1,0:T(8,128)(2,1)S(1)}, u32[]{:S(2)}, u32[]{:S(2)}) collective-permute-start(bf16[520,128]{1,0:T(8,128)(2,1)S(1)} %get-tuple-element.12), channel_id=1, source_target_pairs={{0,12},{4,0},{8,4},{12,8},{1,13},{5,1},{9,5},{13,9},{2,14},{6,2},{... | collective-permute-start | bytes 399368 | tf_op jit(solution)/shard_map/ppermute | solution.py:522
  6.4 0.9 %collective-permute-start.4 = (bf16[520,128]{1,0:T(8,128)(2,1)S(1)}, bf16[520,128]{1,0:T(8,128)(2,1)S(1)}, u32[]{:S(2)}, u32[]{:S(2)}) collective-permute-start(bf16[520,128]{1,0:T(8,128)(2,1)S(1)} %get-tuple-element.18), channel_id=1, source_target_pairs={{0,8},{4,12},{8,0},{12,4},{1,9},{5,13},{9,1},{13,5},{2,10},{6,14},... | collective-permute-start | bytes 399368 | tf_op jit(solution)/shard_map/ppermute | solution.py:522
  7.4 0.1 pad_add_fusion.where_ref
  7.4 7.5 %attend_own.1 = (bf16[512,128]{1,0:T(8,128)(2,1)S(1)}, bf16[2,3216,128]{2,1,0:T(8,128)(2,1)S(1)}, bf16[2,3216,128]{2,1,0:T(8,128)(2,1)S(1)}) custom-call(s32[2]{0:T(128)S(1)} %pad_add_fusion.where_ref, bf16[520,128]{1,0:T(8,128)(2,1)S(1)} %get-tuple-element.13.q_ref, bf16[2,1601,2,512]{3,2,1,0:T(2,128)(2,1)} %bitcast.5), custom_call_target="tpu_custom_call" | custom-call | tf_op jit(solution)/shard_map/attend_own/pallas_call | solution.py:325
  14.9 0.1 collective-permute-done.q_ref
  15.0 5.2 %attend_arrived.3.partial_ref = bf16[512,128]{1,0:T(8,128)(2,1)S(1)} custom-call(bf16[520,128]{1,0:T(8,128)(2,1)S(1)} %collective-permute-done.q_ref, bf16[2,3216,128]{2,1,0:T(8,128)(2,1)S(1)} %get-tuple-element.14.keys_ref, bf16[2,3216,128]{2,1,0:T(8,128)(2,1)S(1)} %get-tuple-element.15.values_ref), custom_call_target="tpu_custom_call" | custom-call | tf_op jit(solution)/shard_map/attend_arrived/pallas_call | solution.py:352
  20.2 0.0 collective-permute-done.1.message_ref.refs_1_.q_ref
  20.2 2.3 %collective-permute-start.2 = (bf16[1024,128]{1,0:T(8,128)(2,1)S(1)}, bf16[1024,128]{1,0:T(8,128)(2,1)S(1)}, u32[]{:S(2)}, u32[]{:S(2)}) collective-permute-start(bf16[1024,128]{1,0:T(8,128)(2,1)S(1)} %join_keys.1), channel_id=1, source_target_pairs={{0,4},{4,8},{8,12},{12,0},{1,5},{5,9},{9,13},{13,1},{2,6},{6,10},{... | collective-permute-start | bytes 786440 | tf_op jit(solution)/shard_map/ppermute | solution.py:522
  22.6 0.0 collective-permute-done.4.q_ref
  22.6 5.2 %attend_arrived.5 = bf16[512,128]{1,0:T(8,128)(2,1)S(1)} custom-call(bf16[520,128]{1,0:T(8,128)(2,1)S(1)} %collective-permute-done.4.q_ref, bf16[2,3216,128]{2,1,0:T(8,128)(2,1)S(1)} %get-tuple-element.14.keys_ref, bf16[2,3216,128]{2,1,0:T(8,128)(2,1)S(1)} %get-tuple-element.15.values_ref), custom_call_target="tpu_custom_call" | custom-call | tf_op jit(solution)/shard_map/attend_arrived/pallas_call | solution.py:352
  27.8 0.0 copy-start.4
  27.8 0.0 copy-start
  27.8 0.0 copy-start.3
  27.8 1.9 %collective-permute-start.5 = (bf16[512,128]{1,0:T(8,128)(2,1)S(1)}, bf16[512,128]{1,0:T(8,128)(2,1)S(1)}, u32[]{:S(2)}, u32[]{:S(2)}) collective-permute-start(bf16[512,128]{1,0:T(8,128)(2,1)S(1)} %attend_arrived.5), channel_id=1, source_target_pairs={{0,8},{4,12},{8,0},{12,4},{1,9},{5,13},{9,1},{13,5},{2,10},{6,14},... | collective-permute-start | bytes 393224 | tf_op jit(solution)/shard_map/ppermute | solution.py:522
  29.7 5.2 %attend_arrived.4 = bf16[512,128]{1,0:T(8,128)(2,1)S(1)} custom-call(bf16[1032,128]{1,0:T(8,128)(2,1)S(1)} %collective-permute-done.1.message_ref.refs_1_.q_ref, bf16[2,3216,128]{2,1,0:T(8,128)(2,1)S(1)} %get-tuple-element.14.keys_ref, bf16[2,3216,128]{2,1,0:T(8,128)(2,1)S(1)} %get-tuple-element.15.values_ref), custom_call_target="tpu_custom_call" | custom-call | tf_op jit(solution)/shard_map/attend_arrived/pallas_call | solution.py:352
  34.9 0.0 copy-start.1
  34.9 0.0 copy-start.2
  34.9 1.1 %collective-permute-start.3 = (bf16[512,128]{1,0:T(8,128)(2,1)S(1)}, bf16[512,128]{1,0:T(8,128)(2,1)S(1)}, u32[]{:S(2)}, u32[]{:S(2)}) collective-permute-start(bf16[512,128]{1,0:T(8,128)(2,1)S(1)} %attend_arrived.4), channel_id=1, source_target_pairs={{0,12},{4,0},{8,4},{12,8},{1,13},{5,1},{9,5},{13,9},{2,14},{6,2},{... | collective-permute-start | bytes 393224 | tf_op jit(solution)/shard_map/ppermute | solution.py:522
  36.1 0.0 copy-done.4
  36.1 0.0 collective-permute-done.2.refs_0_.refs_3_
  36.1 0.0 copy-done
  36.1 0.0 copy-done.3
  36.1 1.8 %attend_self.1.self_ref = f32[128,2048]{1,0:T(8,128)S(1)} custom-call(s32[2]{0:T(128)S(1)} %pad_add_fusion.where_ref, s32[4]{0:T(128)S(1)} %copy-done.3, bf16[128,2048]{1,0:T(8,128)(2,1)S(1)} %copy-done, bf16[1024,128]{1,0:T(8,128)(2,1)S(1)} %collective-permute-done.2.refs_0_.refs_3_, bf16[1032,128]{1,0:T(8,128)(2,1)S(1)} %collective-permute-done.1.message_ref.refs_1_.q_ref, ...), custom_call_target="tpu_custom_call" | custom-call | tf_op jit(solution)/shard_map/attend_self/pallas_call | solution.py:422
  37.8 0.0 collective-permute-done.5.refs_2_
  37.9 2.1 %collective-permute-done.3.refs_1_ = bf16[512,128]{1,0:T(8,128)(2,1)S(1)} collective-permute-done((bf16[512,128]{1,0:T(8,128)(2,1)S(1)}, bf16[512,128]{1,0:T(8,128)(2,1)S(1)}, u32[]{:S(2)}, u32[]{:S(2)}) %collective-permute-start.3) | collective-permute-done | bytes 131104 | tf_op jit(solution)/shard_map/ppermute | solution.py:522
  39.9 0.1 broadcast_in_dim.3
  40.0 0.0 copy-done.1
  40.0 0.0 copy-done.2
  40.0 1.5 %mix.1 = bf16[128,2048]{1,0:T(8,128)(2,1)} custom-call(s32[4,4]{1,0:T(4,128)S(1)} %copy-done.1, s32[8]{0:T(128)S(1)} %copy-done.2, f32[1,2048]{1,0:T(1,128)S(1)} %bitcast.4, f32[128,2048]{1,0:T(8,128)S(1)} %attend_self.1.self_ref, bf16[512,128]{1,0:T(8,128)(2,1)S(1)} %get-tuple-element.17.refs_0_, bf16[512,128]{1,0:T(8,128)(2,1)S(1)} %collective-permute-done.3.refs_1_, ...), custom_call_target="tpu_custom_call" | custom-call | tf_op jit(solution)/shard_map/mix/pallas_call | solution.py:456
  (2 shorter events, 0.0 us)
Async XLA Ops:
  1.2 19.0 %collective-permute-start.1 = (bf16[1032,128]{1,0:T(8,128)(2,1)S(1)}, bf16[1032,128]{1,0:T(8,128)(2,1)S(1)}, u32[]{:S(2)}, u32[]{:S(2)}) collective-permute-start(bf16[1032,128]{1,0:T(8,128)(2,1)S(1)} %get-tuple-element.16.refs_2_), channel_id=1, source_target_pairs={{0,4},{4,8},{8,12},{12,0},{1,5},{5,9},{9,13},{13,1},{2,6},{6,10},{... | collective-permute-start | bytes 792584 | tf_op jit(solution)/shard_map/ppermute | solution.py:522
  4.3 10.7 %collective-permute-start = (bf16[520,128]{1,0:T(8,128)(2,1)S(1)}, bf16[520,128]{1,0:T(8,128)(2,1)S(1)}, u32[]{:S(2)}, u32[]{:S(2)}) collective-permute-start(bf16[520,128]{1,0:T(8,128)(2,1)S(1)} %get-tuple-element.12), channel_id=1, source_target_pairs={{0,12},{4,0},{8,4},{12,8},{1,13},{5,1},{9,5},{13,9},{2,14},{6,2},{... | collective-permute-start | bytes 399368 | tf_op jit(solution)/shard_map/ppermute | solution.py:522
  6.4 16.2 %collective-permute-start.4 = (bf16[520,128]{1,0:T(8,128)(2,1)S(1)}, bf16[520,128]{1,0:T(8,128)(2,1)S(1)}, u32[]{:S(2)}, u32[]{:S(2)}) collective-permute-start(bf16[520,128]{1,0:T(8,128)(2,1)S(1)} %get-tuple-element.18), channel_id=1, source_target_pairs={{0,8},{4,12},{8,0},{12,4},{1,9},{5,13},{9,1},{13,5},{2,10},{6,14},... | collective-permute-start | bytes 399368 | tf_op jit(solution)/shard_map/ppermute | solution.py:522
  20.2 15.8 %collective-permute-start.2 = (bf16[1024,128]{1,0:T(8,128)(2,1)S(1)}, bf16[1024,128]{1,0:T(8,128)(2,1)S(1)}, u32[]{:S(2)}, u32[]{:S(2)}) collective-permute-start(bf16[1024,128]{1,0:T(8,128)(2,1)S(1)} %join_keys.1), channel_id=1, source_target_pairs={{0,4},{4,8},{8,12},{12,0},{1,5},{5,9},{9,13},{13,1},{2,6},{6,10},{... | collective-permute-start | bytes 786440 | tf_op jit(solution)/shard_map/ppermute | solution.py:522
  27.8 8.3 %copy-start.4 = (f32[16]{0:T(128)S(1)}, f32[16]{0:T(128)}, u32[]{:S(2)}) copy-start(f32[16]{0:T(128)} %param.12) | copy-start | bytes 196
  27.8 8.3 %copy-start = (bf16[128,2048]{1,0:T(8,128)(2,1)S(1)}, bf16[128,2048]{1,0:T(8,128)(2,1)}, u32[]{:S(2)}) copy-start(bf16[128,2048]{1,0:T(8,128)(2,1)} %q_ref.1) | copy-start | bytes 1572868
  27.8 8.3 %copy-start.3 = (s32[4]{0:T(128)S(1)}, s32[4]{0:T(128)}, u32[]{:S(2)}) copy-start(s32[4]{0:T(128)} %docs_ref.1) | copy-start | bytes 52
  27.8 10.0 %collective-permute-start.5 = (bf16[512,128]{1,0:T(8,128)(2,1)S(1)}, bf16[512,128]{1,0:T(8,128)(2,1)S(1)}, u32[]{:S(2)}, u32[]{:S(2)}) collective-permute-start(bf16[512,128]{1,0:T(8,128)(2,1)S(1)} %attend_arrived.5), channel_id=1, source_target_pairs={{0,8},{4,12},{8,0},{12,4},{1,9},{5,13},{9,1},{13,5},{2,10},{6,14},... | collective-permute-start | bytes 393224 | tf_op jit(solution)/shard_map/ppermute | solution.py:522
  34.9 5.1 %copy-start.1 = (s32[4,4]{1,0:T(4,128)S(1)}, s32[4,4]{1,0:T(4,128)}, u32[]{:S(2)}) copy-start(s32[4,4]{1,0:T(4,128)} %pairs_ref.1) | copy-start | bytes 196
  34.9 5.1 %copy-start.2 = (s32[8]{0:T(128)S(1)}, s32[8]{0:T(128)}, u32[]{:S(2)}) copy-start(s32[8]{0:T(128)} %slots_ref.1) | copy-start | bytes 100
  34.9 5.0 %collective-permute-start.3 = (bf16[512,128]{1,0:T(8,128)(2,1)S(1)}, bf16[512,128]{1,0:T(8,128)(2,1)S(1)}, u32[]{:S(2)}, u32[]{:S(2)}) collective-permute-start(bf16[512,128]{1,0:T(8,128)(2,1)S(1)} %attend_arrived.4), channel_id=1, source_target_pairs={{0,12},{4,0},{8,4},{12,8},{1,13},{5,1},{9,5},{13,9},{2,14},{6,2},{... | collective-permute-start | bytes 393224 | tf_op jit(solution)/shard_map/ppermute | solution.py:522

commit v5 on v4

--- a/solution.py
+++ b/solution.py
@@ -430,46 +430,73 @@
     )(where, doc_lengths, in_vmem(q_self), *[in_vmem(array) for array, _ in pieces])
 
 
-def mix_body(pairs_ref, slots_ref, gate_ref, self_ref, *refs, tiles_dev):
-    partial_refs, (out_hbm, out_ref, sem) = refs[:-3], refs[-3:]
-    stored = owner_slots(pairs_ref, slots_ref)
-    here = lax.axis_index("ctx")
+def mix_blocks(blocks_ref, gate_ref, self_ref, partial_refs, distances, out_hbm, out_ref, sem):
     copies = []
-    for distance, partial_ref in enumerate(partial_refs):
-        owner = lax.rem(here + distance, len(partial_refs))
-        block, _ = block_for(stored, owner, tiles_dev)
-        rows = pl.ds(pl.multiple_of(block * BLOCK, BLOCK), BLOCK)
+    for i, (distance, partial_ref) in enumerate(zip(distances, partial_refs)):
+        rows = pl.ds(pl.multiple_of(blocks_ref[distance] * BLOCK, BLOCK), BLOCK)
         for h in range(self_ref.shape[1] // HEAD_DIM):
             cols = slice(h * HEAD_DIM, (h + 1) * HEAD_DIM)
             cross = partial_ref[h * BLOCK : (h + 1) * BLOCK, :].astype(jnp.float32)
             mixed = self_ref[rows, cols] + gate_ref[:, cols] * cross
-            out_ref[rows, cols] = mixed.astype(jnp.bfloat16)
-        copy = pltpu.make_async_copy(out_ref.at[rows, :], out_hbm.at[rows, :], sem.at[distance])
+            out_ref[i, :, cols] = mixed.astype(jnp.bfloat16)
+        copy = pltpu.make_async_copy(out_ref.at[i], out_hbm.at[rows, :], sem.at[i])
         copy.start()
         copies.append(copy)
     for copy in copies:
         copy.wait()
 
 
+def early_body(pairs_ref, slots_ref, gate_ref, self_ref, *refs, distances, tiles_dev):
+    partial_refs, (out_hbm, blocks_ref, out_ref, sem) = refs[:-4], refs[-4:]
+    stored = owner_slots(pairs_ref, slots_ref)
+    here = lax.axis_index("ctx")
+    ctx_count = blocks_ref.shape[0]
+    for distance in range(ctx_count):
+        owner = lax.rem(here + distance, ctx_count)
+        blocks_ref[distance] = block_for(stored, owner, tiles_dev)[0]
+    mix_blocks(blocks_ref, gate_ref, self_ref, partial_refs, distances, out_hbm, out_ref, sem)
+
+
+def late_body(blocks_ref, gate_ref, self_ref, *refs, distances):
+    partial_refs, (_, out_hbm, out_ref, sem) = refs[:-4], refs[-4:]
+    mix_blocks(blocks_ref, gate_ref, self_ref, partial_refs, distances, out_hbm, out_ref, sem)
+
+
 def mix(pair_tiles, tile_slot, gate_cols, self_out, partials, tiles_dev):
-    out = jax.ShapeDtypeStruct(self_out.shape, jnp.bfloat16)
+    ctx_count = len(partials)
+    early, late = [0, ctx_count - 1], list(range(1, ctx_count - 1))
+    out_shape = jax.ShapeDtypeStruct(self_out.shape, jnp.bfloat16)
+
+    def scratch(distances):
+        return [
+            pltpu.VMEM((len(distances), BLOCK, self_out.shape[1]), jnp.bfloat16),
+            pltpu.SemaphoreType.DMA((len(distances),)),
+        ]
+
+    shared = (in_vmem(gate_cols), in_vmem(self_out))
+    out, blocks = pl.pallas_call(
+        functools.partial(early_body, distances=early, tiles_dev=tiles_dev),
+        out_shape=[out_shape, pltpu.SMEM((ctx_count,), jnp.int32)],
+        in_specs=[SMEM] * 2 + [VMEM] * (2 + len(early)),
+        out_specs=[HBM, SMEM],
+        scratch_shapes=scratch(early),
+        compiler_params=PARAMS,
+        name="mix_early",
+    )(pair_tiles, tile_slot, *shared, *[in_vmem(partials[d]) for d in early])
     return pl.pallas_call(
-        functools.partial(mix_body, tiles_dev=tiles_dev),
-        out_shape=out,
-        in_specs=[SMEM] * 2 + [VMEM] * (2 + len(partials)),
+        functools.partial(late_body, distances=late),
+        out_shape=out_shape,
+        in_specs=[SMEM] + [VMEM] * (2 + len(late)) + [HBM],
         out_specs=HBM,
-        scratch_shapes=[
-            pltpu.VMEM(out.shape, out.dtype),
-            pltpu.SemaphoreType.DMA((len(partials),)),
-        ],
-        compiler_params=PARAMS,
-        name="mix",
+        scratch_shapes=scratch(late),
+        input_output_aliases={3 + len(late): 0},
+        compiler_params=PARAMS,
+        name="mix_late",
     )(
-        pair_tiles,
-        tile_slot,
-        in_vmem(gate_cols),
-        in_vmem(self_out),
-        *[in_vmem(partial) for partial in partials],
+        pltpu.with_memory_space_constraint(blocks, pltpu.SMEM),
+        *shared,
+        *[in_vmem(partials[d]) for d in late],
+        in_hbm(out),
     )
 
 

time: 41.8 us -> 41 us (0.981)
  waiting for transfers between devices: 2.18 us -> 0.73 us
  Pallas kernels: 27.6 us -> 28.2 us
    ppermute x6, waiting for transfers between devices: 2.18 us -> 0.73 us  [send(): return lax.ppermute(array, 'ctx', pairs)]
    pallas_call x1 -> x2, Pallas kernels: 1.46 us -> 2.13 us  [the longest x1 1.37 us: mix(): pl.pallas_call(functools.partial(early_body, distances=early, tiles_dev=t...]
  transfers between devices with their start and end apart: 6 -> 6, of which waited for: 2 -> 2; matrix products, arithmetic and copies ran while one was open for 0% -> 0% of each run, Pallas kernels for 60% -> 64%
where the time goes in v5:
time: 41 us; the launch traced here: 40.9 us
  Pallas kernels  28.2 us (69%)
  starting transfers between devices  11.4 us (28%)
  waiting for transfers between devices  0.73 us (2%)
    pallas_call x3, Pallas kernels, attend_arrived(): pl.pallas_call(functools.partial(arrived_body, with_lse=with_lse, key_cou...  15.7 us
    ppermute x6, starting transfers between devices, send(): return lax.ppermute(array, 'ctx', pairs)  11.4 us
    pallas_call x1, Pallas kernels, attend_own(): pl.pallas_call(functools.partial(own_body, with_lse=with_lse), out_shape=...  7.46 us
    pallas_call x1, Pallas kernels, attend_self(): pl.pallas_call(functools.partial(self_body, starts=[at for _, at in piece...  1.75 us
    pallas_call x1, Pallas kernels, mix(): pl.pallas_call(functools.partial(early_body, distances=early, tiles_dev=t...  1.37 us
    pallas_call x1, Pallas kernels, pack_queries(): pl.pallas_call(functools.partial(pack_body, tiles_dev=tiles_dev, kv_used=...  1.2 us
  transfers between devices with their start and end apart: 6, of which 2 were waited for; matrix products, arithmetic and copies ran while one was open for 0% of the time, Pallas kernels for 64%

profile of v5, /device:TPU:0, one launch (start us, length us, event | category | flops | bytes accessed | tf_op | source)
XLA Modules:
  0.0 40.9 jit_solution(3190284933191647769)
XLA Ops:
  0.0 1.2 %pack_queries.1 = (bf16[520,128]{1,0:T(8,128)(2,1)S(1)}, bf16[1032,128]{1,0:T(8,128)(2,1)S(1)}, bf16[520,128]{1,0:T(8,128)(2,1)S(1)}, bf16[520,128]{1,0:T(8,128)(2,1)S(1)}) custom-call(s32[4,4]{1,0:T(4,128)} %pairs_ref.1, s32[8]{0:T(128)} %slots_ref.1, bf16[128,2048]{1,0:T(8,128)(2,1)} %q_hbm.1, bf16[2,128,512]{2,1,0:T(8,128)(2,1)} %kv_hbm.1), custom_call_target="tpu_custom_call" | custom-call | tf_op jit(solution)/shard_map/pack_queries/pallas_call | solution.py:107
  1.2 3.1 %collective-permute-start.1 = (bf16[1032,128]{1,0:T(8,128)(2,1)S(1)}, bf16[1032,128]{1,0:T(8,128)(2,1)S(1)}, u32[]{:S(2)}, u32[]{:S(2)}) collective-permute-start(bf16[1032,128]{1,0:T(8,128)(2,1)S(1)} %get-tuple-element.18.refs_2_), channel_id=1, source_target_pairs={{0,4},{4,8},{8,12},{12,0},{1,5},{5,9},{9,13},{13,1},{2,6},{6,10},{... | collective-permute-start | bytes 792584 | tf_op jit(solution)/shard_map/ppermute | solution.py:549
  4.3 2.1 %collective-permute-start = (bf16[520,128]{1,0:T(8,128)(2,1)S(1)}, bf16[520,128]{1,0:T(8,128)(2,1)S(1)}, u32[]{:S(2)}, u32[]{:S(2)}) collective-permute-start(bf16[520,128]{1,0:T(8,128)(2,1)S(1)} %get-tuple-element.14), channel_id=1, source_target_pairs={{0,12},{4,0},{8,4},{12,8},{1,13},{5,1},{9,5},{13,9},{2,14},{6,2},{... | collective-permute-start | bytes 399368 | tf_op jit(solution)/shard_map/ppermute | solution.py:549
  6.4 0.9 %collective-permute-start.4 = (bf16[520,128]{1,0:T(8,128)(2,1)S(1)}, bf16[520,128]{1,0:T(8,128)(2,1)S(1)}, u32[]{:S(2)}, u32[]{:S(2)}) collective-permute-start(bf16[520,128]{1,0:T(8,128)(2,1)S(1)} %get-tuple-element.21), channel_id=1, source_target_pairs={{0,8},{4,12},{8,0},{12,4},{1,9},{5,13},{9,1},{13,5},{2,10},{6,14},... | collective-permute-start | bytes 399368 | tf_op jit(solution)/shard_map/ppermute | solution.py:549
  7.4 0.1 pad_add_fusion.where_ref
  7.4 7.5 %attend_own.1 = (bf16[512,128]{1,0:T(8,128)(2,1)S(1)}, bf16[2,3216,128]{2,1,0:T(8,128)(2,1)S(1)}, bf16[2,3216,128]{2,1,0:T(8,128)(2,1)S(1)}) custom-call(s32[2]{0:T(128)S(1)} %pad_add_fusion.where_ref, bf16[520,128]{1,0:T(8,128)(2,1)S(1)} %get-tuple-element.15.q_ref, bf16[2,1601,2,512]{3,2,1,0:T(2,128)(2,1)} %bitcast.6), custom_call_target="tpu_custom_call" | custom-call | tf_op jit(solution)/shard_map/attend_own/pallas_call | solution.py:325
  14.9 0.1 collective-permute-done.q_ref
  15.0 5.2 %attend_arrived.3.partial_ref = bf16[512,128]{1,0:T(8,128)(2,1)S(1)} custom-call(bf16[520,128]{1,0:T(8,128)(2,1)S(1)} %collective-permute-done.q_ref, bf16[2,3216,128]{2,1,0:T(8,128)(2,1)S(1)} %get-tuple-element.16.keys_ref, bf16[2,3216,128]{2,1,0:T(8,128)(2,1)S(1)} %get-tuple-element.17.values_ref), custom_call_target="tpu_custom_call" | custom-call | tf_op jit(solution)/shard_map/attend_arrived/pallas_call | solution.py:352
  20.2 0.0 collective-permute-done.1.message_ref.refs_1_.q_ref
  20.2 2.3 %collective-permute-start.2 = (bf16[1024,128]{1,0:T(8,128)(2,1)S(1)}, bf16[1024,128]{1,0:T(8,128)(2,1)S(1)}, u32[]{:S(2)}, u32[]{:S(2)}) collective-permute-start(bf16[1024,128]{1,0:T(8,128)(2,1)S(1)} %join_keys.1), channel_id=1, source_target_pairs={{0,4},{4,8},{8,12},{12,0},{1,5},{5,9},{9,13},{13,1},{2,6},{6,10},{... | collective-permute-start | bytes 786440 | tf_op jit(solution)/shard_map/ppermute | solution.py:549
  22.6 0.0 collective-permute-done.4.q_ref
  22.6 5.2 %attend_arrived.5 = bf16[512,128]{1,0:T(8,128)(2,1)S(1)} custom-call(bf16[520,128]{1,0:T(8,128)(2,1)S(1)} %collective-permute-done.4.q_ref, bf16[2,3216,128]{2,1,0:T(8,128)(2,1)S(1)} %get-tuple-element.16.keys_ref, bf16[2,3216,128]{2,1,0:T(8,128)(2,1)S(1)} %get-tuple-element.17.values_ref), custom_call_target="tpu_custom_call" | custom-call | tf_op jit(solution)/shard_map/attend_arrived/pallas_call | solution.py:352
  27.8 0.0 copy-start.4
  27.8 0.0 copy-start
  27.8 0.0 copy-start.3
  27.8 1.9 %collective-permute-start.5 = (bf16[512,128]{1,0:T(8,128)(2,1)S(1)}, bf16[512,128]{1,0:T(8,128)(2,1)S(1)}, u32[]{:S(2)}, u32[]{:S(2)}) collective-permute-start(bf16[512,128]{1,0:T(8,128)(2,1)S(1)} %attend_arrived.5), channel_id=1, source_target_pairs={{0,8},{4,12},{8,0},{12,4},{1,9},{5,13},{9,1},{13,5},{2,10},{6,14},... | collective-permute-start | bytes 393224 | tf_op jit(solution)/shard_map/ppermute | solution.py:549
  29.7 5.2 %attend_arrived.4 = bf16[512,128]{1,0:T(8,128)(2,1)S(1)} custom-call(bf16[1032,128]{1,0:T(8,128)(2,1)S(1)} %collective-permute-done.1.message_ref.refs_1_.q_ref, bf16[2,3216,128]{2,1,0:T(8,128)(2,1)S(1)} %get-tuple-element.16.keys_ref, bf16[2,3216,128]{2,1,0:T(8,128)(2,1)S(1)} %get-tuple-element.17.values_ref), custom_call_target="tpu_custom_call" | custom-call | tf_op jit(solution)/shard_map/attend_arrived/pallas_call | solution.py:352
  34.9 0.0 copy-start.1
  34.9 0.0 copy-start.2
  34.9 1.1 %collective-permute-start.3 = (bf16[512,128]{1,0:T(8,128)(2,1)S(1)}, bf16[512,128]{1,0:T(8,128)(2,1)S(1)}, u32[]{:S(2)}, u32[]{:S(2)}) collective-permute-start(bf16[512,128]{1,0:T(8,128)(2,1)S(1)} %attend_arrived.4), channel_id=1, source_target_pairs={{0,12},{4,0},{8,4},{12,8},{1,13},{5,1},{9,5},{13,9},{2,14},{6,2},{... | collective-permute-start | bytes 393224 | tf_op jit(solution)/shard_map/ppermute | solution.py:549
  36.1 0.0 copy-done.4
  36.1 0.0 collective-permute-done.2.refs_0_.refs_1_
  36.1 0.0 copy-done
  36.1 0.0 copy-done.3
  36.1 1.8 %attend_self.1.self_ref = f32[128,2048]{1,0:T(8,128)S(1)} custom-call(s32[2]{0:T(128)S(1)} %pad_add_fusion.where_ref, s32[4]{0:T(128)S(1)} %copy-done.3, bf16[128,2048]{1,0:T(8,128)(2,1)S(1)} %copy-done, bf16[1024,128]{1,0:T(8,128)(2,1)S(1)} %collective-permute-done.2.refs_0_.refs_1_, bf16[1032,128]{1,0:T(8,128)(2,1)S(1)} %collective-permute-done.1.message_ref.refs_1_.q_ref, ...), custom_call_target="tpu_custom_call" | custom-call | tf_op jit(solution)/shard_map/attend_self/pallas_call | solution.py:422
  37.8 0.1 broadcast_in_dim.3
  37.9 0.0 copy-done.1
  37.9 0.0 copy-done.2
  37.9 1.4 %mix_early.1 = (bf16[128,2048]{1,0:T(8,128)(2,1)}, s32[4]{0:T(128)S(4)}) custom-call(s32[4,4]{1,0:T(4,128)S(1)} %copy-done.1, s32[8]{0:T(128)S(1)} %copy-done.2, f32[1,2048]{1,0:T(1,128)S(1)} %bitcast.4, f32[128,2048]{1,0:T(8,128)S(1)} %attend_self.1.self_ref, bf16[512,128]{1,0:T(8,128)(2,1)S(1)} %get-tuple-element.19.refs_0_, ...), custom_call_target="tpu_custom_call" | custom-call | tf_op jit(solution)/shard_map/mix_early/pallas_call | solution.py:477
  39.3 0.0 collective-permute-done.5.refs_1_
  39.3 0.6 %collective-permute-done.3.refs_0_ = bf16[512,128]{1,0:T(8,128)(2,1)S(1)} collective-permute-done((bf16[512,128]{1,0:T(8,128)(2,1)S(1)}, bf16[512,128]{1,0:T(8,128)(2,1)S(1)}, u32[]{:S(2)}, u32[]{:S(2)}) %collective-permute-start.3) | collective-permute-done | bytes 131104 | tf_op jit(solution)/shard_map/ppermute | solution.py:549
  39.9 0.8 %mix_late.1 = bf16[128,2048]{1,0:T(8,128)(2,1)} custom-call(s32[4]{0:T(128)S(4)} %get-tuple-element.20.blocks_ref, f32[1,2048]{1,0:T(1,128)S(1)} %bitcast.5, f32[128,2048]{1,0:T(8,128)S(1)} %attend_self.1.self_ref, bf16[512,128]{1,0:T(8,128)(2,1)S(1)} %collective-permute-done.3.refs_0_, ...), custom_call_target="tpu_custom_call", output_to_operand_aliasing={{}: (5, {})} | custom-call | tf_op jit(solution)/shard_map/mix_late/pallas_call | solution.py:486
  (2 shorter events, 0.0 us)
Async XLA Ops:
  1.2 19.0 %collective-permute-start.1 = (bf16[1032,128]{1,0:T(8,128)(2,1)S(1)}, bf16[1032,128]{1,0:T(8,128)(2,1)S(1)}, u32[]{:S(2)}, u32[]{:S(2)}) collective-permute-start(bf16[1032,128]{1,0:T(8,128)(2,1)S(1)} %get-tuple-element.18.refs_2_), channel_id=1, source_target_pairs={{0,4},{4,8},{8,12},{12,0},{1,5},{5,9},{9,13},{13,1},{2,6},{6,10},{... | collective-permute-start | bytes 792584 | tf_op jit(solution)/shard_map/ppermute | solution.py:549
  4.3 10.7 %collective-permute-start = (bf16[520,128]{1,0:T(8,128)(2,1)S(1)}, bf16[520,128]{1,0:T(8,128)(2,1)S(1)}, u32[]{:S(2)}, u32[]{:S(2)}) collective-permute-start(bf16[520,128]{1,0:T(8,128)(2,1)S(1)} %get-tuple-element.14), channel_id=1, source_target_pairs={{0,12},{4,0},{8,4},{12,8},{1,13},{5,1},{9,5},{13,9},{2,14},{6,2},{... | collective-permute-start | bytes 399368 | tf_op jit(solution)/shard_map/ppermute | solution.py:549
  6.4 16.2 %collective-permute-start.4 = (bf16[520,128]{1,0:T(8,128)(2,1)S(1)}, bf16[520,128]{1,0:T(8,128)(2,1)S(1)}, u32[]{:S(2)}, u32[]{:S(2)}) collective-permute-start(bf16[520,128]{1,0:T(8,128)(2,1)S(1)} %get-tuple-element.21), channel_id=1, source_target_pairs={{0,8},{4,12},{8,0},{12,4},{1,9},{5,13},{9,1},{13,5},{2,10},{6,14},... | collective-permute-start | bytes 399368 | tf_op jit(solution)/shard_map/ppermute | solution.py:549
  20.2 15.8 %collective-permute-start.2 = (bf16[1024,128]{1,0:T(8,128)(2,1)S(1)}, bf16[1024,128]{1,0:T(8,128)(2,1)S(1)}, u32[]{:S(2)}, u32[]{:S(2)}) collective-permute-start(bf16[1024,128]{1,0:T(8,128)(2,1)S(1)} %join_keys.1), channel_id=1, source_target_pairs={{0,4},{4,8},{8,12},{12,0},{1,5},{5,9},{9,13},{13,1},{2,6},{6,10},{... | collective-permute-start | bytes 786440 | tf_op jit(solution)/shard_map/ppermute | solution.py:549
  27.8 8.3 %copy-start.4 = (f32[16]{0:T(128)S(1)}, f32[16]{0:T(128)}, u32[]{:S(2)}) copy-start(f32[16]{0:T(128)} %param.12) | copy-start | bytes 196
  27.8 8.3 %copy-start = (bf16[128,2048]{1,0:T(8,128)(2,1)S(1)}, bf16[128,2048]{1,0:T(8,128)(2,1)}, u32[]{:S(2)}) copy-start(bf16[128,2048]{1,0:T(8,128)(2,1)} %q_ref.1) | copy-start | bytes 1572868
  27.8 8.3 %copy-start.3 = (s32[4]{0:T(128)S(1)}, s32[4]{0:T(128)}, u32[]{:S(2)}) copy-start(s32[4]{0:T(128)} %docs_ref.1) | copy-start | bytes 52
  27.8 11.5 %collective-permute-start.5 = (bf16[512,128]{1,0:T(8,128)(2,1)S(1)}, bf16[512,128]{1,0:T(8,128)(2,1)S(1)}, u32[]{:S(2)}, u32[]{:S(2)}) collective-permute-start(bf16[512,128]{1,0:T(8,128)(2,1)S(1)} %attend_arrived.5), channel_id=1, source_target_pairs={{0,8},{4,12},{8,0},{12,4},{1,9},{5,13},{9,1},{13,5},{2,10},{6,14},... | collective-permute-start | bytes 393224 | tf_op jit(solution)/shard_map/ppermute | solution.py:549
  34.9 3.0 %copy-start.1 = (s32[4,4]{1,0:T(4,128)S(1)}, s32[4,4]{1,0:T(4,128)}, u32[]{:S(2)}) copy-start(s32[4,4]{1,0:T(4,128)} %pairs_ref.1) | copy-start | bytes 196
  34.9 3.0 %copy-start.2 = (s32[8]{0:T(128)S(1)}, s32[8]{0:T(128)}, u32[]{:S(2)}) copy-start(s32[8]{0:T(128)} %slots_ref.1) | copy-start | bytes 100
  34.9 5.0 %collective-permute-start.3 = (bf16[512,128]{1,0:T(8,128)(2,1)S(1)}, bf16[512,128]{1,0:T(8,128)(2,1)S(1)}, u32[]{:S(2)}, u32[]{:S(2)}) collective-permute-start(bf16[512,128]{1,0:T(8,128)(2,1)S(1)} %attend_arrived.4), channel_id=1, source_target_pairs={{0,12},{4,0},{8,4},{12,8},{1,13},{5,1},{9,5},{13,9},{2,14},{6,2},{... | collective-permute-start | bytes 393224 | tf_op jit(solution)/shard_map/ppermute | solution.py:549

commit v6 on v5

--- a/solution.py
+++ b/solution.py
@@ -275,7 +275,7 @@
     return lambda: None
 
 
-def own_body(where_ref, q_ref, image_hbm, *refs, with_lse):
+def own_body(q_ref, image_hbm, *refs, with_lse, kv_first):
     out_ref = refs[0]
     lse_ref = refs[1] if with_lse else None
     keys_ref, values_ref, scores_sc, sem = refs[-4:]
@@ -285,20 +285,20 @@
     image = image_hbm.reshape(2, key_count, width)
 
     def copies(k):
-        cols = pl.ds(pl.multiple_of((where_ref[1] + k) * HEAD_DIM, HEAD_DIM), HEAD_DIM)
+        cols = pl.ds(pl.multiple_of((kv_first() + k) * HEAD_DIM, HEAD_DIM), HEAD_DIM)
         held = pl.ds(0, key_count)
         return [
             pltpu.make_async_copy(image.at[w, :, cols], ref.at[k, held], sem.at[w, k])
             for w, ref in enumerate((keys_ref, values_ref))
         ]
 
-    for copy in copies(0):
-        copy.start()
     if padded > key_count:
         pad = jnp.zeros((padded - key_count, HEAD_DIM), jnp.bfloat16)
         for k in range(kv_used):
             keys_ref[k, key_count:, :] = pad
             values_ref[k, key_count:, :] = pad
+    for copy in copies(0):
+        copy.start()
 
     def wait(k):
         keys, values = copies(k)
@@ -314,7 +314,7 @@
     )
 
 
-def attend_own(where, packed, image_kv, kv_used, q_rows, with_lse):
+def attend_own(packed, image_kv, kv_used, q_rows, with_lse, kv_first):
     _, tile_len, tiles_dev, _ = image_kv.shape
     padded = -(-tile_len * tiles_dev // 16) * 16
     held = pltpu.VMEM((kv_used, padded, HEAD_DIM), jnp.bfloat16)
@@ -323,9 +323,9 @@
         out_shape.append(pltpu.VMEM((q_rows, HEAD_DIM), jnp.float32))
     out_shape += [held, held]
     results = pl.pallas_call(
-        functools.partial(own_body, with_lse=with_lse),
+        functools.partial(own_body, with_lse=with_lse, kv_first=kv_first),
         out_shape=out_shape,
-        in_specs=[SMEM, VMEM, HBM],
+        in_specs=[VMEM, HBM],
         out_specs=[VMEM] * len(out_shape),
         scratch_shapes=[
             pltpu.VMEM((q_rows // kv_used, padded), jnp.float32),
@@ -333,7 +333,7 @@
         ],
         compiler_params=PARAMS,
         name="attend_own",
-    )(where, in_vmem(packed), in_hbm(image_kv))
+    )(in_vmem(packed), in_hbm(image_kv))
     return results[:-2], [in_vmem(part) for part in results[-2:]]
 
 
@@ -377,12 +377,12 @@
     )(in_vmem(partial), in_vmem(message))
 
 
-def self_body(where_ref, docs_ref, q_ref, *refs, starts, kv_used):
+def self_body(docs_ref, q_ref, *refs, starts, kv_used):
     kv_refs, out_ref, bias_sc = refs[:-2], refs[-2], refs[-1]
     tok_rows, q_width = q_ref.shape
     per_kv = q_width // HEAD_DIM // kv_used
     shape = bias_sc.shape
-    row_start = where_ref[0] * tok_rows
+    row_start = lax.axis_index("ctx") * tok_rows
     query_pos = row_start + lax.broadcasted_iota(jnp.int32, (tok_rows, 1), 0)
     key_pos = row_start + tok_rows - shape[1] + lax.broadcasted_iota(jnp.int32, shape, 1)
     doc_start = jnp.zeros((tok_rows, 1), jnp.int32)
@@ -417,17 +417,17 @@
             out_ref[:, h * HEAD_DIM : (h + 1) * HEAD_DIM] = blended[i * tok_rows : (i + 1) * tok_rows]
 
 
-def attend_self(where, doc_lengths, q_self, pieces, kv_used):
+def attend_self(doc_lengths, q_self, pieces, kv_used):
     tok_rows, q_width = q_self.shape
     return pl.pallas_call(
         functools.partial(self_body, starts=[at for _, at in pieces], kv_used=kv_used),
         out_shape=pltpu.VMEM((tok_rows, q_width), jnp.float32),
-        in_specs=[SMEM, SMEM] + [VMEM] * (1 + len(pieces)),
+        in_specs=[SMEM] + [VMEM] * (1 + len(pieces)),
         out_specs=VMEM,
         scratch_shapes=[pltpu.VMEM((tok_rows, len(pieces) * tok_rows), jnp.float32)],
         compiler_params=PARAMS,
         name="attend_self",
-    )(where, doc_lengths, in_vmem(q_self), *[in_vmem(array) for array, _ in pieces])
+    )(doc_lengths, in_vmem(q_self), *[in_vmem(array) for array, _ in pieces])
 
 
 def mix_blocks(blocks_ref, gate_ref, self_ref, partial_refs, distances, out_hbm, out_ref, sem):
@@ -500,13 +500,13 @@
     )
 
 
-def mix_owners(where, pair_tiles, tile_slot, gate_cols, self_out, partials, sums, tiles_dev):
+def mix_owners(pair_tiles, tile_slot, gate_cols, self_out, partials, sums, tiles_dev):
     block_count = pair_tiles.shape[0]
     tok_rows, q_width = self_out.shape
     heads = q_width // HEAD_DIM
     ctx_count = len(partials)
     owners = jnp.take(tile_slot, pair_tiles.reshape(-1), axis=0).reshape(block_count, -1) // tiles_dev
-    partners = (where[0] + jnp.arange(ctx_count, dtype=jnp.int32)) % ctx_count
+    partners = (lax.axis_index("ctx") + jnp.arange(ctx_count, dtype=jnp.int32)) % ctx_count
     live = jnp.any(owners[:, :, None] == partners[None, None, :], axis=1)[:, :, None, None]
     lse = jnp.stack(sums)[None]
     top = jnp.max(jnp.where(live, lse, NEG_FILL), axis=1, keepdims=True)
@@ -536,12 +536,10 @@
     with_lse = not one_owner
     reach = min(ctx_count - 1, -(-(ctx_count * tok_rows // 2 - 1) // tok_rows))
 
-    here = lax.axis_index("ctx").astype(jnp.int32)
 
     def kv_first():
         return lax.axis_index("rep") * local_heads // grouping
 
-    where = jnp.stack([here, kv_first().astype(jnp.int32)])
     image_kv = jnp.transpose(image_kv, (0, 2, 1, 3))
 
     def send(array, distance):
@@ -555,7 +553,7 @@
     order = partner_order(ctx_count)
     arrived = {d: send(packed[d], d) for d in order[-1:] + order[:-1]}
     results = {}
-    results[0], held = attend_own(where, packed[0], image_kv, kv_used, q_rows, with_lse)
+    results[0], held = attend_own(packed[0], image_kv, kv_used, q_rows, with_lse, kv_first)
     for d in order:
         answer = attend_arrived(arrived[d], held, tile_len * tiles_dev, q_rows, with_lse)
         if d == last:
@@ -568,14 +566,14 @@
         array, first = pieces[-1]
         rows = 2 * kv_used * tok_rows
         pieces.append((send(array[first : first + rows], 1), 0))
-    self_out = attend_self(where, doc_lengths, q_self, pieces[::-1], kv_used)
+    self_out = attend_self(doc_lengths, q_self, pieces[::-1], kv_used)
     gate_cols = jnp.repeat(jnp.tanh(cross_gate), HEAD_DIM)[None, :]
     partials = [results[d][0] for d in range(ctx_count)]
     if one_owner:
         return mix(pair_tiles, tile_slot, gate_cols, self_out, partials, tiles_dev)
     partials = [partial[:q_rows] for partial in partials]
     sums = [results[d][1] for d in range(ctx_count)]
-    return mix_owners(where, pair_tiles, tile_slot, gate_cols, self_out, partials, sums, tiles_dev)
+    return mix_owners(pair_tiles, tile_slot, gate_cols, self_out, partials, sums, tiles_dev)
 
 
 def solution(mesh):

time: 41 us -> 41 us (level)
  waiting for transfers between devices: 0.73 us -> 1.35 us
  Pallas kernels: 28.2 us -> 27.7 us
    ppermute x6, waiting for transfers between devices: 0.73 us -> 1.35 us  [send(): return lax.ppermute(array, 'ctx', pairs)]
    pallas_call x1, Pallas kernels: 7.46 us -> 6.91 us  [attend_own(): pl.pallas_call(functools.partial(own_body, with_lse=with_lse, kv_first=kv...]
  transfers between devices with their start and end apart: 6 -> 6, of which waited for: 2 -> 2; matrix products, arithmetic and copies ran while one was open for 0% -> 0% of each run, Pallas kernels for 64% -> 63%
where the time goes in v6:
time: 41 us; the launch traced here: 40.9 us
  Pallas kernels  27.7 us (68%)
  starting transfers between devices  11.4 us (28%)
  waiting for transfers between devices  1.35 us (3%)
    pallas_call x3, Pallas kernels, attend_arrived(): pl.pallas_call(functools.partial(arrived_body, with_lse=with_lse, key_cou...  15.6 us
    ppermute x6, starting transfers between devices, send(): return lax.ppermute(array, 'ctx', pairs)  11.4 us
    pallas_call x1, Pallas kernels, attend_own(): pl.pallas_call(functools.partial(own_body, with_lse=with_lse, kv_first=kv...  6.91 us
    pallas_call x1, Pallas kernels, attend_self(): pl.pallas_call(functools.partial(self_body, starts=[at for _, at in piece...  1.75 us
    pallas_call x1, Pallas kernels, mix(): pl.pallas_call(functools.partial(early_body, distances=early, tiles_dev=t...  1.37 us
    ppermute x6, waiting for transfers between devices, send(): return lax.ppermute(array, 'ctx', pairs)  1.35 us
    pallas_call x1, Pallas kernels, pack_queries(): pl.pallas_call(functools.partial(pack_body, tiles_dev=tiles_dev, kv_used=...  1.2 us
  transfers between devices with their start and end apart: 6, of which 2 were waited for; matrix products, arithmetic and copies ran while one was open for 0% of the time, Pallas kernels for 63%

profile of v6, /device:TPU:0, one launch (start us, length us, event | category | flops | bytes accessed | tf_op | source)
XLA Modules:
  0.0 40.9 jit_solution(11760583508850174974)
XLA Ops:
  0.0 1.2 %pack_queries.1 = (bf16[520,128]{1,0:T(8,128)(2,1)S(1)}, bf16[1032,128]{1,0:T(8,128)(2,1)S(1)}, bf16[520,128]{1,0:T(8,128)(2,1)S(1)}, bf16[520,128]{1,0:T(8,128)(2,1)S(1)}) custom-call(s32[4,4]{1,0:T(4,128)} %pairs_ref.1, s32[8]{0:T(128)} %slots_ref.1, bf16[128,2048]{1,0:T(8,128)(2,1)} %q_hbm.1, bf16[2,128,512]{2,1,0:T(8,128)(2,1)} %kv_hbm.1), custom_call_target="tpu_custom_call" | custom-call | tf_op jit(solution)/shard_map/pack_queries/pallas_call | solution.py:107
  1.2 3.1 %collective-permute-start.1 = (bf16[1032,128]{1,0:T(8,128)(2,1)S(1)}, bf16[1032,128]{1,0:T(8,128)(2,1)S(1)}, u32[]{:S(2)}, u32[]{:S(2)}) collective-permute-start(bf16[1032,128]{1,0:T(8,128)(2,1)S(1)} %get-tuple-element.18.refs_2_), channel_id=1, source_target_pairs={{0,4},{4,8},{8,12},{12,0},{1,5},{5,9},{9,13},{13,1},{2,6},{6,10},{... | collective-permute-start | bytes 792584 | tf_op jit(solution)/shard_map/ppermute | solution.py:547
  4.3 2.1 %collective-permute-start = (bf16[520,128]{1,0:T(8,128)(2,1)S(1)}, bf16[520,128]{1,0:T(8,128)(2,1)S(1)}, u32[]{:S(2)}, u32[]{:S(2)}) collective-permute-start(bf16[520,128]{1,0:T(8,128)(2,1)S(1)} %get-tuple-element.14), channel_id=1, source_target_pairs={{0,12},{4,0},{8,4},{12,8},{1,13},{5,1},{9,5},{13,9},{2,14},{6,2},{... | collective-permute-start | bytes 399368 | tf_op jit(solution)/shard_map/ppermute | solution.py:547
  6.4 0.9 %collective-permute-start.4 = (bf16[520,128]{1,0:T(8,128)(2,1)S(1)}, bf16[520,128]{1,0:T(8,128)(2,1)S(1)}, u32[]{:S(2)}, u32[]{:S(2)}) collective-permute-start(bf16[520,128]{1,0:T(8,128)(2,1)S(1)} %get-tuple-element.21), channel_id=1, source_target_pairs={{0,8},{4,12},{8,0},{12,4},{1,9},{5,13},{9,1},{13,5},{2,10},{6,14},... | collective-permute-start | bytes 399368 | tf_op jit(solution)/shard_map/ppermute | solution.py:547
  7.4 6.9 %attend_own.1 = (bf16[512,128]{1,0:T(8,128)(2,1)S(1)}, bf16[2,3216,128]{2,1,0:T(8,128)(2,1)S(1)}, bf16[2,3216,128]{2,1,0:T(8,128)(2,1)S(1)}) custom-call(bf16[520,128]{1,0:T(8,128)(2,1)S(1)} %get-tuple-element.15.q_ref, bf16[2,1601,2,512]{3,2,1,0:T(2,128)(2,1)} %bitcast.4), custom_call_target="tpu_custom_call" | custom-call | tf_op jit(solution)/shard_map/attend_own/pallas_call | solution.py:325
  14.3 0.7 %collective-permute-done.q_ref = bf16[520,128]{1,0:T(8,128)(2,1)S(1)} collective-permute-done((bf16[520,128]{1,0:T(8,128)(2,1)S(1)}, bf16[520,128]{1,0:T(8,128)(2,1)S(1)}, u32[]{:S(2)}, u32[]{:S(2)}) %collective-permute-start) | collective-permute-done | bytes 133152 | tf_op jit(solution)/shard_map/ppermute | solution.py:547
  15.0 5.2 %attend_arrived.3.partial_ref = bf16[512,128]{1,0:T(8,128)(2,1)S(1)} custom-call(bf16[520,128]{1,0:T(8,128)(2,1)S(1)} %collective-permute-done.q_ref, bf16[2,3216,128]{2,1,0:T(8,128)(2,1)S(1)} %get-tuple-element.16.keys_ref, bf16[2,3216,128]{2,1,0:T(8,128)(2,1)S(1)} %get-tuple-element.17.values_ref), custom_call_target="tpu_custom_call" | custom-call | tf_op jit(solution)/shard_map/attend_arrived/pallas_call | solution.py:352
  20.2 0.0 collective-permute-done.1.message_ref.refs_1_.q_ref
  20.2 2.3 %collective-permute-start.2 = (bf16[1024,128]{1,0:T(8,128)(2,1)S(1)}, bf16[1024,128]{1,0:T(8,128)(2,1)S(1)}, u32[]{:S(2)}, u32[]{:S(2)}) collective-permute-start(bf16[1024,128]{1,0:T(8,128)(2,1)S(1)} %join_keys.1), channel_id=1, source_target_pairs={{0,4},{4,8},{8,12},{12,0},{1,5},{5,9},{9,13},{13,1},{2,6},{6,10},{... | collective-permute-start | bytes 786440 | tf_op jit(solution)/shard_map/ppermute | solution.py:547
  22.6 0.0 collective-permute-done.4.q_ref
  22.6 5.2 %attend_arrived.5 = bf16[512,128]{1,0:T(8,128)(2,1)S(1)} custom-call(bf16[520,128]{1,0:T(8,128)(2,1)S(1)} %collective-permute-done.4.q_ref, bf16[2,3216,128]{2,1,0:T(8,128)(2,1)S(1)} %get-tuple-element.16.keys_ref, bf16[2,3216,128]{2,1,0:T(8,128)(2,1)S(1)} %get-tuple-element.17.values_ref), custom_call_target="tpu_custom_call" | custom-call | tf_op jit(solution)/shard_map/attend_arrived/pallas_call | solution.py:352
  27.8 0.0 copy-start.4
  27.8 0.0 copy-start
  27.8 0.0 copy-start.3
  27.8 1.9 %collective-permute-start.5 = (bf16[512,128]{1,0:T(8,128)(2,1)S(1)}, bf16[512,128]{1,0:T(8,128)(2,1)S(1)}, u32[]{:S(2)}, u32[]{:S(2)}) collective-permute-start(bf16[512,128]{1,0:T(8,128)(2,1)S(1)} %attend_arrived.5), channel_id=1, source_target_pairs={{0,8},{4,12},{8,0},{12,4},{1,9},{5,13},{9,1},{13,5},{2,10},{6,14},... | collective-permute-start | bytes 393224 | tf_op jit(solution)/shard_map/ppermute | solution.py:547
  29.7 5.2 %attend_arrived.4 = bf16[512,128]{1,0:T(8,128)(2,1)S(1)} custom-call(bf16[1032,128]{1,0:T(8,128)(2,1)S(1)} %collective-permute-done.1.message_ref.refs_1_.q_ref, bf16[2,3216,128]{2,1,0:T(8,128)(2,1)S(1)} %get-tuple-element.16.keys_ref, bf16[2,3216,128]{2,1,0:T(8,128)(2,1)S(1)} %get-tuple-element.17.values_ref), custom_call_target="tpu_custom_call" | custom-call | tf_op jit(solution)/shard_map/attend_arrived/pallas_call | solution.py:352
  34.9 0.0 copy-start.1
  34.9 0.0 copy-start.2
  34.9 1.1 %collective-permute-start.3 = (bf16[512,128]{1,0:T(8,128)(2,1)S(1)}, bf16[512,128]{1,0:T(8,128)(2,1)S(1)}, u32[]{:S(2)}, u32[]{:S(2)}) collective-permute-start(bf16[512,128]{1,0:T(8,128)(2,1)S(1)} %attend_arrived.4), channel_id=1, source_target_pairs={{0,12},{4,0},{8,4},{12,8},{1,13},{5,1},{9,5},{13,9},{2,14},{6,2},{... | collective-permute-start | bytes 393224 | tf_op jit(solution)/shard_map/ppermute | solution.py:547
  36.0 0.0 copy-done.4
  36.0 0.0 collective-permute-done.2.refs_0_.refs_1_
  36.0 0.0 copy-done
  36.1 0.0 copy-done.3
  36.1 1.8 %attend_self.1.self_ref = f32[128,2048]{1,0:T(8,128)S(1)} custom-call(s32[4]{0:T(128)S(1)} %copy-done.3, bf16[128,2048]{1,0:T(8,128)(2,1)S(1)} %copy-done, bf16[1024,128]{1,0:T(8,128)(2,1)S(1)} %collective-permute-done.2.refs_0_.refs_1_, bf16[1032,128]{1,0:T(8,128)(2,1)S(1)} %collective-permute-done.1.message_ref.refs_1_.q_ref, ...), custom_call_target="tpu_custom_call" | custom-call | tf_op jit(solution)/shard_map/attend_self/pallas_call | solution.py:422
  37.8 0.1 broadcast_in_dim.3
  37.9 0.0 copy-done.1
  37.9 0.0 copy-done.2
  37.9 1.4 %mix_early.1 = (bf16[128,2048]{1,0:T(8,128)(2,1)}, s32[4]{0:T(128)S(4)}) custom-call(s32[4,4]{1,0:T(4,128)S(1)} %copy-done.1, s32[8]{0:T(128)S(1)} %copy-done.2, f32[1,2048]{1,0:T(1,128)S(1)} %bitcast.2, f32[128,2048]{1,0:T(8,128)S(1)} %attend_self.1.self_ref, bf16[512,128]{1,0:T(8,128)(2,1)S(1)} %get-tuple-element.19.refs_0_, ...), custom_call_target="tpu_custom_call" | custom-call | tf_op jit(solution)/shard_map/mix_early/pallas_call | solution.py:477
  39.3 0.0 collective-permute-done.5.refs_1_
  39.3 0.6 %collective-permute-done.3.refs_0_ = bf16[512,128]{1,0:T(8,128)(2,1)S(1)} collective-permute-done((bf16[512,128]{1,0:T(8,128)(2,1)S(1)}, bf16[512,128]{1,0:T(8,128)(2,1)S(1)}, u32[]{:S(2)}, u32[]{:S(2)}) %collective-permute-start.3) | collective-permute-done | bytes 131104 | tf_op jit(solution)/shard_map/ppermute | solution.py:547
  39.9 0.8 %mix_late.1 = bf16[128,2048]{1,0:T(8,128)(2,1)} custom-call(s32[4]{0:T(128)S(4)} %get-tuple-element.20.blocks_ref, f32[1,2048]{1,0:T(1,128)S(1)} %bitcast.3, f32[128,2048]{1,0:T(8,128)S(1)} %attend_self.1.self_ref, bf16[512,128]{1,0:T(8,128)(2,1)S(1)} %collective-permute-done.3.refs_0_, ...), custom_call_target="tpu_custom_call", output_to_operand_aliasing={{}: (5, {})} | custom-call | tf_op jit(solution)/shard_map/mix_late/pallas_call | solution.py:486
  (2 shorter events, 0.0 us)
Async XLA Ops:
  1.2 19.0 %collective-permute-start.1 = (bf16[1032,128]{1,0:T(8,128)(2,1)S(1)}, bf16[1032,128]{1,0:T(8,128)(2,1)S(1)}, u32[]{:S(2)}, u32[]{:S(2)}) collective-permute-start(bf16[1032,128]{1,0:T(8,128)(2,1)S(1)} %get-tuple-element.18.refs_2_), channel_id=1, source_target_pairs={{0,4},{4,8},{8,12},{12,0},{1,5},{5,9},{9,13},{13,1},{2,6},{6,10},{... | collective-permute-start | bytes 792584 | tf_op jit(solution)/shard_map/ppermute | solution.py:547
  4.3 10.7 %collective-permute-start = (bf16[520,128]{1,0:T(8,128)(2,1)S(1)}, bf16[520,128]{1,0:T(8,128)(2,1)S(1)}, u32[]{:S(2)}, u32[]{:S(2)}) collective-permute-start(bf16[520,128]{1,0:T(8,128)(2,1)S(1)} %get-tuple-element.14), channel_id=1, source_target_pairs={{0,12},{4,0},{8,4},{12,8},{1,13},{5,1},{9,5},{13,9},{2,14},{6,2},{... | collective-permute-start | bytes 399368 | tf_op jit(solution)/shard_map/ppermute | solution.py:547
  6.4 16.1 %collective-permute-start.4 = (bf16[520,128]{1,0:T(8,128)(2,1)S(1)}, bf16[520,128]{1,0:T(8,128)(2,1)S(1)}, u32[]{:S(2)}, u32[]{:S(2)}) collective-permute-start(bf16[520,128]{1,0:T(8,128)(2,1)S(1)} %get-tuple-element.21), channel_id=1, source_target_pairs={{0,8},{4,12},{8,0},{12,4},{1,9},{5,13},{9,1},{13,5},{2,10},{6,14},... | collective-permute-start | bytes 399368 | tf_op jit(solution)/shard_map/ppermute | solution.py:547
  20.2 15.8 %collective-permute-start.2 = (bf16[1024,128]{1,0:T(8,128)(2,1)S(1)}, bf16[1024,128]{1,0:T(8,128)(2,1)S(1)}, u32[]{:S(2)}, u32[]{:S(2)}) collective-permute-start(bf16[1024,128]{1,0:T(8,128)(2,1)S(1)} %join_keys.1), channel_id=1, source_target_pairs={{0,4},{4,8},{8,12},{12,0},{1,5},{5,9},{9,13},{13,1},{2,6},{6,10},{... | collective-permute-start | bytes 786440 | tf_op jit(solution)/shard_map/ppermute | solution.py:547
  27.8 8.3 %copy-start.4 = (f32[16]{0:T(128)S(1)}, f32[16]{0:T(128)}, u32[]{:S(2)}) copy-start(f32[16]{0:T(128)} %param.12) | copy-start | bytes 196
  27.8 8.3 %copy-start = (bf16[128,2048]{1,0:T(8,128)(2,1)S(1)}, bf16[128,2048]{1,0:T(8,128)(2,1)}, u32[]{:S(2)}) copy-start(bf16[128,2048]{1,0:T(8,128)(2,1)} %q_ref.1) | copy-start | bytes 1572868
  27.8 8.3 %copy-start.3 = (s32[4]{0:T(128)S(1)}, s32[4]{0:T(128)}, u32[]{:S(2)}) copy-start(s32[4]{0:T(128)} %docs_ref.1) | copy-start | bytes 52
  27.8 11.5 %collective-permute-start.5 = (bf16[512,128]{1,0:T(8,128)(2,1)S(1)}, bf16[512,128]{1,0:T(8,128)(2,1)S(1)}, u32[]{:S(2)}, u32[]{:S(2)}) collective-permute-start(bf16[512,128]{1,0:T(8,128)(2,1)S(1)} %attend_arrived.5), channel_id=1, source_target_pairs={{0,8},{4,12},{8,0},{12,4},{1,9},{5,13},{9,1},{13,5},{2,10},{6,14},... | collective-permute-start | bytes 393224 | tf_op jit(solution)/shard_map/ppermute | solution.py:547
  34.9 3.0 %copy-start.1 = (s32[4,4]{1,0:T(4,128)S(1)}, s32[4,4]{1,0:T(4,128)}, u32[]{:S(2)}) copy-start(s32[4,4]{1,0:T(4,128)} %pairs_ref.1) | copy-start | bytes 196
  34.9 3.0 %copy-start.2 = (s32[8]{0:T(128)S(1)}, s32[8]{0:T(128)}, u32[]{:S(2)}) copy-start(s32[8]{0:T(128)} %slots_ref.1) | copy-start | bytes 100
  34.9 5.0 %collective-permute-start.3 = (bf16[512,128]{1,0:T(8,128)(2,1)S(1)}, bf16[512,128]{1,0:T(8,128)(2,1)S(1)}, u32[]{:S(2)}, u32[]{:S(2)}) collective-permute-start(bf16[512,128]{1,0:T(8,128)(2,1)S(1)} %attend_arrived.4), channel_id=1, source_target_pairs={{0,12},{4,0},{8,4},{12,8},{1,13},{5,1},{9,5},{13,9},{2,14},{6,2},{... | collective-permute-start | bytes 393224 | tf_op jit(solution)/shard_map/ppermute | solution.py:547

commit v7 on v6

--- a/solution.py
+++ b/solution.py
@@ -432,6 +432,8 @@
 
 def mix_blocks(blocks_ref, gate_ref, self_ref, partial_refs, distances, out_hbm, out_ref, sem):
     copies = []
+    width = self_ref.shape[1]
+    ends = [width // HEAD_DIM // 2, width // HEAD_DIM]
     for i, (distance, partial_ref) in enumerate(zip(distances, partial_refs)):
         rows = pl.ds(pl.multiple_of(blocks_ref[distance] * BLOCK, BLOCK), BLOCK)
         for h in range(self_ref.shape[1] // HEAD_DIM):
@@ -439,9 +441,14 @@
             cross = partial_ref[h * BLOCK : (h + 1) * BLOCK, :].astype(jnp.float32)
             mixed = self_ref[rows, cols] + gate_ref[:, cols] * cross
             out_ref[i, :, cols] = mixed.astype(jnp.bfloat16)
-        copy = pltpu.make_async_copy(out_ref.at[i], out_hbm.at[rows, :], sem.at[i])
-        copy.start()
-        copies.append(copy)
+            if h + 1 in ends:
+                part = ends.index(h + 1)
+                cols = pl.ds(part * width // 2, (h + 1) * HEAD_DIM - part * width // 2)
+                copy = pltpu.make_async_copy(
+                    out_ref.at[i, :, cols], out_hbm.at[rows, cols], sem.at[2 * i + part]
+                )
+                copy.start()
+                copies.append(copy)
     for copy in copies:
         copy.wait()
 
@@ -470,7 +477,7 @@
     def scratch(distances):
         return [
             pltpu.VMEM((len(distances), BLOCK, self_out.shape[1]), jnp.bfloat16),
-            pltpu.SemaphoreType.DMA((len(distances),)),
+            pltpu.SemaphoreType.DMA((2 * len(distances),)),
         ]
 
     shared = (in_vmem(gate_cols), in_vmem(self_out))

time: 41 us -> 41 us (level)
  no operation moved by 1% of the time
where the time goes in v7:
time: 41 us; the launch traced here: 40.8 us
  Pallas kernels  27.7 us (68%)
  starting transfers between devices  11.4 us (28%)
  waiting for transfers between devices  1.34 us (3%)
    pallas_call x3, Pallas kernels, attend_arrived(): pl.pallas_call(functools.partial(arrived_body, with_lse=with_lse, key_cou...  15.6 us
    ppermute x6, starting transfers between devices, send(): return lax.ppermute(array, 'ctx', pairs)  11.4 us
    pallas_call x1, Pallas kernels, attend_own(): pl.pallas_call(functools.partial(own_body, with_lse=with_lse, kv_first=kv...  6.91 us
    pallas_call x1, Pallas kernels, attend_self(): pl.pallas_call(functools.partial(self_body, starts=[at for _, at in piece...  1.75 us
    pallas_call x1, Pallas kernels, mix(): pl.pallas_call(functools.partial(early_body, distances=early, tiles_dev=t...  1.38 us
    ppermute x6, waiting for transfers between devices, send(): return lax.ppermute(array, 'ctx', pairs)  1.34 us
    pallas_call x1, Pallas kernels, pack_queries(): pl.pallas_call(functools.partial(pack_body, tiles_dev=tiles_dev, kv_used=...  1.2 us
  transfers between devices with their start and end apart: 6, of which 2 were waited for; matrix products, arithmetic and copies ran while one was open for 0% of the time, Pallas kernels for 63%

profile of v7, /device:TPU:0, one launch (start us, length us, event | category | flops | bytes accessed | tf_op | source)
XLA Modules:
  0.0 40.8 jit_solution(3566540538357693861)
XLA Ops:
  0.0 1.2 %pack_queries.1 = (bf16[520,128]{1,0:T(8,128)(2,1)S(1)}, bf16[1032,128]{1,0:T(8,128)(2,1)S(1)}, bf16[520,128]{1,0:T(8,128)(2,1)S(1)}, bf16[520,128]{1,0:T(8,128)(2,1)S(1)}) custom-call(s32[4,4]{1,0:T(4,128)} %pairs_ref.1, s32[8]{0:T(128)} %slots_ref.1, bf16[128,2048]{1,0:T(8,128)(2,1)} %q_hbm.1, bf16[2,128,512]{2,1,0:T(8,128)(2,1)} %kv_hbm.1), custom_call_target="tpu_custom_call" | custom-call | tf_op jit(solution)/shard_map/pack_queries/pallas_call | solution.py:107
  1.2 3.1 %collective-permute-start.1 = (bf16[1032,128]{1,0:T(8,128)(2,1)S(1)}, bf16[1032,128]{1,0:T(8,128)(2,1)S(1)}, u32[]{:S(2)}, u32[]{:S(2)}) collective-permute-start(bf16[1032,128]{1,0:T(8,128)(2,1)S(1)} %get-tuple-element.18.refs_2_), channel_id=1, source_target_pairs={{0,4},{4,8},{8,12},{12,0},{1,5},{5,9},{9,13},{13,1},{2,6},{6,10},{... | collective-permute-start | bytes 792584 | tf_op jit(solution)/shard_map/ppermute | solution.py:554
  4.3 2.1 %collective-permute-start = (bf16[520,128]{1,0:T(8,128)(2,1)S(1)}, bf16[520,128]{1,0:T(8,128)(2,1)S(1)}, u32[]{:S(2)}, u32[]{:S(2)}) collective-permute-start(bf16[520,128]{1,0:T(8,128)(2,1)S(1)} %get-tuple-element.14), channel_id=1, source_target_pairs={{0,12},{4,0},{8,4},{12,8},{1,13},{5,1},{9,5},{13,9},{2,14},{6,2},{... | collective-permute-start | bytes 399368 | tf_op jit(solution)/shard_map/ppermute | solution.py:554
  6.4 0.9 %collective-permute-start.4 = (bf16[520,128]{1,0:T(8,128)(2,1)S(1)}, bf16[520,128]{1,0:T(8,128)(2,1)S(1)}, u32[]{:S(2)}, u32[]{:S(2)}) collective-permute-start(bf16[520,128]{1,0:T(8,128)(2,1)S(1)} %get-tuple-element.21), channel_id=1, source_target_pairs={{0,8},{4,12},{8,0},{12,4},{1,9},{5,13},{9,1},{13,5},{2,10},{6,14},... | collective-permute-start | bytes 399368 | tf_op jit(solution)/shard_map/ppermute | solution.py:554
  7.4 6.9 %attend_own.1 = (bf16[512,128]{1,0:T(8,128)(2,1)S(1)}, bf16[2,3216,128]{2,1,0:T(8,128)(2,1)S(1)}, bf16[2,3216,128]{2,1,0:T(8,128)(2,1)S(1)}) custom-call(bf16[520,128]{1,0:T(8,128)(2,1)S(1)} %get-tuple-element.15.q_ref, bf16[2,1601,2,512]{3,2,1,0:T(2,128)(2,1)} %bitcast.4), custom_call_target="tpu_custom_call" | custom-call | tf_op jit(solution)/shard_map/attend_own/pallas_call | solution.py:325
  14.3 0.7 %collective-permute-done.q_ref = bf16[520,128]{1,0:T(8,128)(2,1)S(1)} collective-permute-done((bf16[520,128]{1,0:T(8,128)(2,1)S(1)}, bf16[520,128]{1,0:T(8,128)(2,1)S(1)}, u32[]{:S(2)}, u32[]{:S(2)}) %collective-permute-start) | collective-permute-done | bytes 133152 | tf_op jit(solution)/shard_map/ppermute | solution.py:554
  15.0 5.2 %attend_arrived.3.partial_ref = bf16[512,128]{1,0:T(8,128)(2,1)S(1)} custom-call(bf16[520,128]{1,0:T(8,128)(2,1)S(1)} %collective-permute-done.q_ref, bf16[2,3216,128]{2,1,0:T(8,128)(2,1)S(1)} %get-tuple-element.16.keys_ref, bf16[2,3216,128]{2,1,0:T(8,128)(2,1)S(1)} %get-tuple-element.17.values_ref), custom_call_target="tpu_custom_call" | custom-call | tf_op jit(solution)/shard_map/attend_arrived/pallas_call | solution.py:352
  20.2 0.0 collective-permute-done.1.message_ref.refs_1_.q_ref
  20.2 2.3 %collective-permute-start.2 = (bf16[1024,128]{1,0:T(8,128)(2,1)S(1)}, bf16[1024,128]{1,0:T(8,128)(2,1)S(1)}, u32[]{:S(2)}, u32[]{:S(2)}) collective-permute-start(bf16[1024,128]{1,0:T(8,128)(2,1)S(1)} %join_keys.1), channel_id=1, source_target_pairs={{0,4},{4,8},{8,12},{12,0},{1,5},{5,9},{9,13},{13,1},{2,6},{6,10},{... | collective-permute-start | bytes 786440 | tf_op jit(solution)/shard_map/ppermute | solution.py:554
  22.6 0.0 collective-permute-done.4.q_ref
  22.6 5.2 %attend_arrived.5 = bf16[512,128]{1,0:T(8,128)(2,1)S(1)} custom-call(bf16[520,128]{1,0:T(8,128)(2,1)S(1)} %collective-permute-done.4.q_ref, bf16[2,3216,128]{2,1,0:T(8,128)(2,1)S(1)} %get-tuple-element.16.keys_ref, bf16[2,3216,128]{2,1,0:T(8,128)(2,1)S(1)} %get-tuple-element.17.values_ref), custom_call_target="tpu_custom_call" | custom-call | tf_op jit(solution)/shard_map/attend_arrived/pallas_call | solution.py:352
  27.8 0.0 copy-start.4
  27.8 0.0 copy-start
  27.8 0.0 copy-start.3
  27.8 1.9 %collective-permute-start.5 = (bf16[512,128]{1,0:T(8,128)(2,1)S(1)}, bf16[512,128]{1,0:T(8,128)(2,1)S(1)}, u32[]{:S(2)}, u32[]{:S(2)}) collective-permute-start(bf16[512,128]{1,0:T(8,128)(2,1)S(1)} %attend_arrived.5), channel_id=1, source_target_pairs={{0,8},{4,12},{8,0},{12,4},{1,9},{5,13},{9,1},{13,5},{2,10},{6,14},... | collective-permute-start | bytes 393224 | tf_op jit(solution)/shard_map/ppermute | solution.py:554
  29.7 5.2 %attend_arrived.4 = bf16[512,128]{1,0:T(8,128)(2,1)S(1)} custom-call(bf16[1032,128]{1,0:T(8,128)(2,1)S(1)} %collective-permute-done.1.message_ref.refs_1_.q_ref, bf16[2,3216,128]{2,1,0:T(8,128)(2,1)S(1)} %get-tuple-element.16.keys_ref, bf16[2,3216,128]{2,1,0:T(8,128)(2,1)S(1)} %get-tuple-element.17.values_ref), custom_call_target="tpu_custom_call" | custom-call | tf_op jit(solution)/shard_map/attend_arrived/pallas_call | solution.py:352
  34.9 0.0 copy-start.1
  34.9 0.0 copy-start.2
  34.9 1.1 %collective-permute-start.3 = (bf16[512,128]{1,0:T(8,128)(2,1)S(1)}, bf16[512,128]{1,0:T(8,128)(2,1)S(1)}, u32[]{:S(2)}, u32[]{:S(2)}) collective-permute-start(bf16[512,128]{1,0:T(8,128)(2,1)S(1)} %attend_arrived.4), channel_id=1, source_target_pairs={{0,12},{4,0},{8,4},{12,8},{1,13},{5,1},{9,5},{13,9},{2,14},{6,2},{... | collective-permute-start | bytes 393224 | tf_op jit(solution)/shard_map/ppermute | solution.py:554
  36.0 0.0 copy-done.4
  36.0 0.0 collective-permute-done.2.refs_0_.refs_1_
  36.0 0.0 copy-done
  36.1 0.0 copy-done.3
  36.1 1.8 %attend_self.1.self_ref = f32[128,2048]{1,0:T(8,128)S(1)} custom-call(s32[4]{0:T(128)S(1)} %copy-done.3, bf16[128,2048]{1,0:T(8,128)(2,1)S(1)} %copy-done, bf16[1024,128]{1,0:T(8,128)(2,1)S(1)} %collective-permute-done.2.refs_0_.refs_1_, bf16[1032,128]{1,0:T(8,128)(2,1)S(1)} %collective-permute-done.1.message_ref.refs_1_.q_ref, ...), custom_call_target="tpu_custom_call" | custom-call | tf_op jit(solution)/shard_map/attend_self/pallas_call | solution.py:422
  37.8 0.1 broadcast_in_dim.3
  37.9 0.0 copy-done.1
  37.9 0.0 copy-done.2
  37.9 1.4 %mix_early.1 = (bf16[128,2048]{1,0:T(8,128)(2,1)}, s32[4]{0:T(128)S(4)}) custom-call(s32[4,4]{1,0:T(4,128)S(1)} %copy-done.1, s32[8]{0:T(128)S(1)} %copy-done.2, f32[1,2048]{1,0:T(1,128)S(1)} %bitcast.2, f32[128,2048]{1,0:T(8,128)S(1)} %attend_self.1.self_ref, bf16[512,128]{1,0:T(8,128)(2,1)S(1)} %get-tuple-element.19.refs_0_, ...), custom_call_target="tpu_custom_call" | custom-call | tf_op jit(solution)/shard_map/mix_early/pallas_call | solution.py:484
  39.3 0.0 collective-permute-done.5.refs_1_
  39.3 0.6 %collective-permute-done.3.refs_0_ = bf16[512,128]{1,0:T(8,128)(2,1)S(1)} collective-permute-done((bf16[512,128]{1,0:T(8,128)(2,1)S(1)}, bf16[512,128]{1,0:T(8,128)(2,1)S(1)}, u32[]{:S(2)}, u32[]{:S(2)}) %collective-permute-start.3) | collective-permute-done | bytes 131104 | tf_op jit(solution)/shard_map/ppermute | solution.py:554
  39.9 0.8 %mix_late.1 = bf16[128,2048]{1,0:T(8,128)(2,1)} custom-call(s32[4]{0:T(128)S(4)} %get-tuple-element.20.blocks_ref, f32[1,2048]{1,0:T(1,128)S(1)} %bitcast.3, f32[128,2048]{1,0:T(8,128)S(1)} %attend_self.1.self_ref, bf16[512,128]{1,0:T(8,128)(2,1)S(1)} %collective-permute-done.3.refs_0_, ...), custom_call_target="tpu_custom_call", output_to_operand_aliasing={{}: (5, {})} | custom-call | tf_op jit(solution)/shard_map/mix_late/pallas_call | solution.py:493
  (2 shorter events, 0.0 us)
Async XLA Ops:
  1.2 19.0 %collective-permute-start.1 = (bf16[1032,128]{1,0:T(8,128)(2,1)S(1)}, bf16[1032,128]{1,0:T(8,128)(2,1)S(1)}, u32[]{:S(2)}, u32[]{:S(2)}) collective-permute-start(bf16[1032,128]{1,0:T(8,128)(2,1)S(1)} %get-tuple-element.18.refs_2_), channel_id=1, source_target_pairs={{0,4},{4,8},{8,12},{12,0},{1,5},{5,9},{9,13},{13,1},{2,6},{6,10},{... | collective-permute-start | bytes 792584 | tf_op jit(solution)/shard_map/ppermute | solution.py:554
  4.3 10.7 %collective-permute-start = (bf16[520,128]{1,0:T(8,128)(2,1)S(1)}, bf16[520,128]{1,0:T(8,128)(2,1)S(1)}, u32[]{:S(2)}, u32[]{:S(2)}) collective-permute-start(bf16[520,128]{1,0:T(8,128)(2,1)S(1)} %get-tuple-element.14), channel_id=1, source_target_pairs={{0,12},{4,0},{8,4},{12,8},{1,13},{5,1},{9,5},{13,9},{2,14},{6,2},{... | collective-permute-start | bytes 399368 | tf_op jit(solution)/shard_map/ppermute | solution.py:554
  6.4 16.1 %collective-permute-start.4 = (bf16[520,128]{1,0:T(8,128)(2,1)S(1)}, bf16[520,128]{1,0:T(8,128)(2,1)S(1)}, u32[]{:S(2)}, u32[]{:S(2)}) collective-permute-start(bf16[520,128]{1,0:T(8,128)(2,1)S(1)} %get-tuple-element.21), channel_id=1, source_target_pairs={{0,8},{4,12},{8,0},{12,4},{1,9},{5,13},{9,1},{13,5},{2,10},{6,14},... | collective-permute-start | bytes 399368 | tf_op jit(solution)/shard_map/ppermute | solution.py:554
  20.2 15.8 %collective-permute-start.2 = (bf16[1024,128]{1,0:T(8,128)(2,1)S(1)}, bf16[1024,128]{1,0:T(8,128)(2,1)S(1)}, u32[]{:S(2)}, u32[]{:S(2)}) collective-permute-start(bf16[1024,128]{1,0:T(8,128)(2,1)S(1)} %join_keys.1), channel_id=1, source_target_pairs={{0,4},{4,8},{8,12},{12,0},{1,5},{5,9},{9,13},{13,1},{2,6},{6,10},{... | collective-permute-start | bytes 786440 | tf_op jit(solution)/shard_map/ppermute | solution.py:554
  27.8 8.3 %copy-start.4 = (f32[16]{0:T(128)S(1)}, f32[16]{0:T(128)}, u32[]{:S(2)}) copy-start(f32[16]{0:T(128)} %param.12) | copy-start | bytes 196
  27.8 8.3 %copy-start = (bf16[128,2048]{1,0:T(8,128)(2,1)S(1)}, bf16[128,2048]{1,0:T(8,128)(2,1)}, u32[]{:S(2)}) copy-start(bf16[128,2048]{1,0:T(8,128)(2,1)} %q_ref.1) | copy-start | bytes 1572868
  27.8 8.3 %copy-start.3 = (s32[4]{0:T(128)S(1)}, s32[4]{0:T(128)}, u32[]{:S(2)}) copy-start(s32[4]{0:T(128)} %docs_ref.1) | copy-start | bytes 52
  27.8 11.5 %collective-permute-start.5 = (bf16[512,128]{1,0:T(8,128)(2,1)S(1)}, bf16[512,128]{1,0:T(8,128)(2,1)S(1)}, u32[]{:S(2)}, u32[]{:S(2)}) collective-permute-start(bf16[512,128]{1,0:T(8,128)(2,1)S(1)} %attend_arrived.5), channel_id=1, source_target_pairs={{0,8},{4,12},{8,0},{12,4},{1,9},{5,13},{9,1},{13,5},{2,10},{6,14},... | collective-permute-start | bytes 393224 | tf_op jit(solution)/shard_map/ppermute | solution.py:554
  34.9 3.0 %copy-start.1 = (s32[4,4]{1,0:T(4,128)S(1)}, s32[4,4]{1,0:T(4,128)}, u32[]{:S(2)}) copy-start(s32[4,4]{1,0:T(4,128)} %pairs_ref.1) | copy-start | bytes 196
  34.9 3.0 %copy-start.2 = (s32[8]{0:T(128)S(1)}, s32[8]{0:T(128)}, u32[]{:S(2)}) copy-start(s32[8]{0:T(128)} %slots_ref.1) | copy-start | bytes 100
  34.9 5.0 %collective-permute-start.3 = (bf16[512,128]{1,0:T(8,128)(2,1)S(1)}, bf16[512,128]{1,0:T(8,128)(2,1)S(1)}, u32[]{:S(2)}, u32[]{:S(2)}) collective-permute-start(bf16[512,128]{1,0:T(8,128)(2,1)S(1)} %attend_arrived.4), channel_id=1, source_target_pairs={{0,12},{4,0},{8,4},{12,8},{1,13},{5,1},{9,5},{13,9},{2,14},{6,2},{... | collective-permute-start | bytes 393224 | tf_op jit(solution)/shard_map/ppermute | solution.py:554
